TPU v7x, 256 devices: a whole 4x4x8 slice. The times are simulated.
256 devices in a mesh: tile: 64 (over x, z, core), depth: 4 (over y).
Axes of the slice: x: 4, y: 4, z: 8, core: 2. Of those that a mesh axis runs over, the one named last changes fastest.
Arguments:
- soil_state: float32 [16, 512, 6, 128], P('depth', 'tile')
- tile_count: int32 [16, 512], P('depth', 'tile'), may hold values from 64 to 128, as said below
- tile_neighbors: int32 [16, 512, 6], P('depth', 'tile'), may hold values from 0 to 8, as said below
- marker_pos: float32 [3, 1048576], P(None, ('tile', 'depth')), may hold values from -1 to 1
- marker_vel: float32 [3, 1048576], P(None, ('tile', 'depth')), may hold values from -5 to 5
- marker_tile: int32 [1048576], P(('tile', 'depth')), may hold values from 0 to 31
- marker_owner: int32 [1048576, 1], P(('tile', 'depth')), may hold values from 0 to 63; in each aligned block of 4096 rows (0 to 4095, 4096 to 8191, ...) at most 256 rows name the same one
- marker_slot: int32 [1048576], P(('tile', 'depth')), may hold values from 0 to 127
- body_state: float32 [9, 8192], P(None, 'tile'), may hold values from -4 to 4
- body_inertia: float32 [4, 8192], P(None, 'tile'), may hold values from 0.5 to 2
Outputs:
- soil_accel: float32 [16, 512, 3, 128], P('depth', 'tile')
- body_next: float32 [9, 8192], P(None, 'tile')
- marker_vel_next: float32 [3, 1048576], P(None, ('tile', 'depth'))
Inputs may be any that keep to these rules, and one draw needn't show every extreme that they name: `tile_count`: number of real particles of the tile; slots from it on are padding. `tile_neighbors`: a code c names the tile at layer offset c // 3 - 1 and horizontal offset c % 3 - 1; each tile lists 6 distinct codes, the first being 4 (itself). `marker_tile`: index among the 4 x 8 tiles of the device that holds the marker, layer-major. `marker_owner`: in each aligned block of 4096 markers (those of one device) no owner is named more than 256 times, a bound that some block reaches.
All inputs are finite; a program needn't handle non-finite values.
Results may differ from a plain program's by a relative error of at most 0.0001.
Values sent between devices are 32-bit elements; how exact they have to be, the bound alone decides.
No kernel may reach another device: no remote copies, remote signals or barrier semaphores. Data moves between devices by JAX's collectives and lax.ppermute only.
A program may use at most 64 MiB of HBM per device.

v0:
```python
import math

import jax
import jax.numpy as jnp
from jax import lax
from jax.sharding import PartitionSpec as P

stiffness = 40.0
rest_density = 2.0
viscosity = 20.0
time_step = 0.05
gravity = 1.0


def with_halo(shard, sides, width):
    for axis, dim in sides:
        size, length = (lax.axis_size(axis), shard.shape[dim])
        up = [(i, (i + 1) % size) for i in range(size - 1)]
        down = [(j, i) for i, j in up]
        last = lax.slice_in_dim(shard, length - width, length, axis=dim)
        first = lax.slice_in_dim(shard, 0, width, axis=dim)
        before = lax.ppermute(last, axis, up)
        after = lax.ppermute(first, axis, down)
        shard = jnp.concatenate([before, shard, after], axis=dim)
    return shard


def split_up(shard, dim, length):
    before, after = (shard.shape[:dim], shard.shape[dim + 1 :])
    return jnp.moveaxis(shard.reshape(*before, length, -1, *after), dim, 0)


def summed_on_arrival(shard, axis, dim):
    length = lax.axis_size(axis)
    blocks = lax.all_to_all(split_up(shard, dim, length), axis, 0, 0, tiled=True)
    return jnp.sum(blocks, axis=0)


def from_everyone(shard, axis):
    length = lax.axis_size(axis)
    return lax.all_to_all(
        jnp.broadcast_to(shard[None], (length, *shard.shape)), axis, 0, 0, tiled=True
    )


def of_everyone(shard, axis):
    everything = from_everyone(shard, axis)
    return jnp.sum(everything, axis=0)


def laid_out(blocks, dim):
    shape = list(blocks.shape[1:])
    shape[dim] *= blocks.shape[0]
    return jnp.moveaxis(blocks, 0, dim).reshape(shape)


def gathered_copies(shard, axis, dim):
    blocks = from_everyone(shard, axis)
    return laid_out(blocks, dim)


def cross(first_vec, second_vec):
    return jnp.stack(
        [
            first_vec[1] * second_vec[2] - first_vec[2] * second_vec[1],
            first_vec[2] * second_vec[0] - first_vec[0] * second_vec[2],
            first_vec[0] * second_vec[1] - first_vec[1] * second_vec[0],
        ],
        axis=0,
    )


def pair_weights(left_pos, right_pos, right_live):
    distance = jnp.zeros((left_pos.shape[0], left_pos.shape[2], right_pos.shape[2]), jnp.float32)
    for component in range(3):
        offset = left_pos[:, component, :, None] - right_pos[:, component, None, :]
        distance = distance + offset * offset
    return right_live[:, None, :] * jnp.exp(-distance)


def block_density(own_tiles, nbr_ids, table):
    summed = jnp.zeros((own_tiles.shape[0], own_tiles.shape[2]), jnp.float32)
    for entry_num in range(nbr_ids.shape[1]):
        neighbor = table[nbr_ids[:, entry_num]]
        summed = summed + jnp.sum(
            pair_weights(own_tiles[:, 0:3], neighbor[:, 0:3], neighbor[:, 6]), axis=2
        )
    return 1.0 + summed / own_tiles.shape[2]


def block_accel(own_tiles, own_extra, nbr_ids, table, extra_table):
    accel_parts = [
        jnp.zeros((own_tiles.shape[0], own_tiles.shape[2]), jnp.float32) for component in range(3)
    ]
    for entry_num in range(nbr_ids.shape[1]):
        neighbor = table[nbr_ids[:, entry_num]]
        neighbor_extra = extra_table[nbr_ids[:, entry_num]]
        weight = pair_weights(own_tiles[:, 0:3], neighbor[:, 0:3], neighbor[:, 6])
        press = 2.0 * (own_extra[:, 0, :, None] + neighbor_extra[:, 0, None, :])
        damping = viscosity * neighbor_extra[:, 1, None, :]
        for component in range(3):
            offset = own_tiles[:, component, :, None] - neighbor[:, component, None, :]
            relative = neighbor[:, 3 + component, None, :] - own_tiles[:, 3 + component, :, None]
            accel_parts[component] = accel_parts[component] + jnp.sum(
                weight * (press * offset + damping * relative), axis=2
            )
    accel_out = jnp.stack(accel_parts, axis=1) / own_tiles.shape[2]
    return accel_out * own_tiles[:, 6:7, :]


def marker_force(marker_place, marker_speed, source):
    distance = jnp.zeros((source.shape[0], source.shape[2]), jnp.float32)
    for component in range(3):
        offset = marker_place[:, component, None] - source[:, component, :]
        distance = distance + offset * offset
    weight = source[:, 6, :] * jnp.exp(-distance)
    forces = []
    for component in range(3):
        offset = marker_place[:, component, None] - source[:, component, :]
        relative = source[:, 3 + component, :] - marker_speed[:, component, None]
        forces.append(
            jnp.sum(
                weight * (2.0 * source[:, 7, :] * offset + viscosity * source[:, 8, :] * relative),
                axis=1,
            )
        )
    return jnp.stack(forces, axis=1) / source.shape[2]


def advance(totals, body_state, body_inertia):
    center = body_state[0:3]
    velocity = body_state[3:6]
    spin = body_state[6:9]
    inv_mass = body_inertia[0:1]
    moment = body_inertia[1:4]
    force_sum = totals[0:3]
    moment_sum = totals[3:6]
    torque = moment_sum - cross(center, force_sum)
    down = jnp.array([0.0, 0.0, -gravity], jnp.float32)[:, None]
    new_vel = velocity + time_step * (inv_mass * force_sum + down)
    new_spin = spin + time_step * (torque - cross(spin, moment * spin)) / moment
    new_center = center + time_step * new_vel
    return (
        jnp.concatenate([new_center, new_vel, new_spin], axis=0),
        jnp.concatenate([center, new_vel, new_spin], axis=0),
    )


def local(
    soil_state,
    tile_count,
    tile_neighbors,
    marker_pos,
    marker_vel,
    marker_tile,
    marker_owner,
    marker_slot,
    body_state,
    body_inertia,
):
    layers, columns, fields, tile_size = soil_state.shape
    neigh_count = tile_neighbors.shape[2]
    marker_count = marker_pos.shape[1]
    body_tile = body_state.shape[1]
    tile_devs = lax.axis_size("tile")
    live_mask = (
        lax.broadcasted_iota(jnp.int32, (layers, columns, tile_size), 2) < tile_count[:, :, None]
    ).astype(jnp.float32)
    packed = jnp.concatenate([soil_state, live_mask[:, :, None, :]], axis=2)
    extended = with_halo(packed, (("tile", 1), ("depth", 0)), 1)
    flat_ext = extended.reshape(((layers + 2) * (columns + 2), 7, tile_size))
    layer_ids = lax.broadcasted_iota(jnp.int32, (layers, columns, neigh_count), 0)
    column_ids = lax.broadcasted_iota(jnp.int32, (layers, columns, neigh_count), 1)
    nbr_ids = (layer_ids + tile_neighbors // 3) * (columns + 2) + column_ids + tile_neighbors % 3
    tile_total = layers * columns
    groups = tile_total // 4
    own_tiles = packed.reshape((groups, 4, 7, tile_size))
    grouped_ids = nbr_ids.reshape((groups, 4, neigh_count))
    density = lax.map(
        lambda operands: block_density(operands[0], operands[1], flat_ext), (own_tiles, grouped_ids)
    )
    density = density.reshape((layers, columns, tile_size))
    extra_rows = jnp.stack(
        [stiffness * (density - rest_density) / (density * density), 1.0 / density], axis=2
    )
    extra_ext = with_halo(extra_rows, (("tile", 1), ("depth", 0)), 1)
    flat_extra = extra_ext.reshape(((layers + 2) * (columns + 2), 2, tile_size))
    accel_out = lax.map(
        lambda operands: block_accel(operands[0], operands[1], operands[2], flat_ext, flat_extra),
        (own_tiles, extra_rows.reshape((groups, 4, 2, tile_size)), grouped_ids),
    )
    soil_accel = accel_out.reshape((layers, columns, 3, tile_size))
    source_table = jnp.concatenate([packed, extra_rows], axis=2).reshape((tile_total, 9, tile_size))
    marker_block = math.gcd(marker_count, 128)
    blocks = marker_count // marker_block
    forces = lax.map(
        lambda operands: marker_force(operands[0], operands[1], source_table[operands[2]]),
        (
            marker_pos.T.reshape((blocks, marker_block, 3)),
            marker_vel.T.reshape((blocks, marker_block, 3)),
            marker_tile.reshape((blocks, marker_block)),
        ),
    )
    forces = forces.reshape((marker_count, 3)).T
    moments = cross(marker_pos, forces)
    marker_terms = jnp.concatenate([forces, moments], axis=0)
    owner_ids = marker_owner[:, 0]
    body_ids = owner_ids * body_tile + marker_slot
    partial_sums = jax.ops.segment_sum(
        marker_terms.T, body_ids, num_segments=tile_devs * body_tile
    ).T
    body_share = summed_on_arrival(partial_sums, "tile", 1)
    totals = of_everyone(body_share, "depth")
    body_next, refresh = advance(totals, body_state, body_inertia)
    all_states = gathered_copies(refresh, "tile", 1)
    picked = all_states[:, owner_ids * body_tile + marker_slot]
    lever = marker_pos - picked[0:3]
    marker_vel_next = picked[3:6] + cross(picked[6:9], lever)
    return (soil_accel, body_next, marker_vel_next)


def solution(mesh):
    placed = (
        P("depth", "tile", None, None),
        P("depth", "tile"),
        P("depth", "tile", None),
        P(None, ("tile", "depth")),
        P(None, ("tile", "depth")),
        P(("tile", "depth")),
        P(("tile", "depth"), None),
        P(("tile", "depth")),
        P(None, "tile"),
        P(None, "tile"),
    )
    return jax.shard_map(
        local,
        mesh=mesh,
        in_specs=placed,
        out_specs=(P("depth", "tile", None, None), P(None, "tile"), P(None, ("tile", "depth"))),
        check_vma=False,
    )
```

profile of v0, /device:TPU:1, one launch (start us, length us, event | category | flops | bytes accessed | tf_op | source)
XLA Modules:
  0.0 372.3 jit_solution(11637527460863033843)
XLA Ops:
  2.4 5.1 %collective-permute-start.1 = (f32[4,1,7,128]{3,1,2,0:T(1,128)S(1)}, f32[4,1,7,128]{3,1,2,0:T(1,128)S(1)}, u32[]{:S(2)}, u32[]{:S(2)}) collective-permute-start(f32[4,1,7,128]{3,1,2,0:T(1,128)S(1)} %get-tuple-element.376), channel_id=1, source_target_pairs={{4,0},{8,4},{12,8},{16,12},{20,16},{24,20},{28,24},{32,28},{36,32}... | collective-permute-start | bytes 43016 | tf_op jit(solution)/shard_map/ppermute | solution.py:23
  17.9 4.0 %collective-permute-start.2 = (f32[1,10,7,128]{3,1,2,0:T(8,128)S(1)}, f32[1,10,7,128]{3,1,2,0:T(8,128)S(1)}, u32[]{:S(2)}, u32[]{:S(2)}) collective-permute-start(f32[1,10,7,128]{3,1,2,0:T(8,128)S(1)} %get-tuple-element.370), channel_id=1, source_target_pairs={{0,1},{1,2},{2,3},{4,5},{5,6},{6,7},{8,9},{9,10},{10,11},{12,13},{... | collective-permute-start | bytes 107528 | tf_op jit(solution)/shard_map/ppermute | solution.py:22
  24.2 40.8 %while.30 = (s32[]{:T(128)}, f32[8,4,128]{2,1,0:T(4,128)S(1)}, s32[8,4,6]{2,1,0:T(4,128)S(1)}, f32[60,7,128]{2,1,0:T(8,128)S(1)}, f32[8,4,7,128]{3,1,2,0:T(4,128)S(1)}, /*index=5*/s32[]{:T(128)}) while((s32[]{:T(128)}, f32[8,4,128]{2,1,0:T(4,128)S(1)}, s32[8,4,6]{2,1,0:T(4,128)S(1)}, f32[60,7,128]{2,1,0:T(8,128)S(1)}, ...), condition=%wide.region_7.8_spmd, body=%wide.region_0.7_spmd.sunk | while | flops 4332106 | bytes 424601 | solution.py:179
  65.1 3.5 collective-permute-start.5
  68.6 2.0 collective-permute-start.4
  70.7 92.4 %while.32 = (s32[]{:T(128)}, f32[32,128,3]{1,2,0:T(4,128)S(1)}, s32[32,128]{1,0:T(8,128)}, f32[32,9,128]{2,1,0:T(8,128)S(1)}, f32[32,128,3]{1,2,0:T(4,128)S(1)}, /*index=5*/f32[32,128,3]{1,2,0:T(4,128)}, s32[]{:T(128)}) while((s32[]{:T(128)}, f32[32,128,3]{1,2,0:T(4,128)S(1)}, s32[32,128]{1,0:T(8,128)}, f32[32,9,128]{2,1,0:T(8,128)S(1)}, ...), condition=%wide.region_32.33_spmd, body=%wide.region_28.32_spmd.sunk | while | flops 493698 | bytes 2975841 | solution.py:196
  165.2 24.8 %scatter_custom_fusion = f32[8192,6]{1,0:T(8,128)} fusion(s32[4096]{0:T(1024)S(1)} %get-tuple-element.246, f32[4096,6]{1,0:T(8,128)} %copy.147, f32[]{:T(128)} %constant.77.clone.1), kind=kCustom, calls=%fused_computation.251 | custom fusion | flops 24576 | bytes 197120 | tf_op jit(solution)/shard_map/scatter-add | solution.py:209
  190.1 3.5 copy.148
  193.6 13.8 %all-to-all-start = ((f32[64,6,128]{2,1,0:T(8,128)}), f32[64,6,128]{2,1,0:T(8,128)S(1)}, u32[]{:S(2)}, u32[]{:S(2)}) async-start(f32[64,6,128]{2,1,0:T(8,128)} %bitcast.147), calls=%async_computation | async-start | bytes 524288 | tf_op jit(solution)/shard_map/all_to_all | solution.py:35
  208.8 4.3 %collective-permute-start.6 = (f32[1,10,2,128]{3,2,1,0:T(2,128)S(1)}, f32[1,10,2,128]{3,2,1,0:T(2,128)S(1)}, u32[]{:S(2)}, u32[]{:S(2)}) collective-permute-start(f32[1,10,2,128]{3,2,1,0:T(2,128)S(1)} %get-tuple-element.380), channel_id=1, source_target_pairs={{0,1},{1,2},{2,3},{4,5},{5,6},{6,7},{8,9},{9,10},{10,11},{12,13},{... | collective-permute-start | bytes 30728 | tf_op jit(solution)/shard_map/ppermute | solution.py:22
  213.1 6.3 %all-to-all-done = f32[64,6,128]{2,1,0:T(8,128)S(1)} async-done(((f32[64,6,128]{2,1,0:T(8,128)}), f32[64,6,128]{2,1,0:T(8,128)S(1)}, u32[]{:S(2)}, u32[]{:S(2)}) %all-to-all-start) | async-done | bytes 196640 | tf_op jit(solution)/shard_map/all_to_all | solution.py:35
  220.1 4.8 %all-to-all-start.1 = ((f32[4,6,128]{2,1,0:T(8,128)}), f32[4,6,128]{2,1,0:T(8,128)S(1)}, u32[]{:S(2)}, u32[]{:S(2)}) async-start(f32[4,6,128]{2,1,0:T(8,128)} %broadcast_in_dim.31), calls=%async_computation.1 | async-start | bytes 32768 | tf_op jit(solution)/shard_map/all_to_all | solution.py:41
  224.9 4.1 %all-to-all-done.1 = f32[4,6,128]{2,1,0:T(8,128)S(1)} async-done(((f32[4,6,128]{2,1,0:T(8,128)}), f32[4,6,128]{2,1,0:T(8,128)S(1)}, u32[]{:S(2)}, u32[]{:S(2)}) %all-to-all-start.1) | async-done | bytes 12320 | tf_op jit(solution)/shard_map/all_to_all | solution.py:41
  230.6 7.5 %all-to-all-start.2 = ((f32[64,9,128]{2,1,0:T(8,128)}), f32[64,9,128]{2,1,0:T(8,128)S(1)}, u32[]{:S(2)}, u32[]{:S(2)}) async-start(f32[64,9,128]{2,1,0:T(8,128)} %broadcast_in_dim.32), calls=%async_computation.2 | async-start | bytes 1048576 | tf_op jit(solution)/shard_map/all_to_all | solution.py:41
  238.1 97.9 %while.31 = (s32[]{:T(128)}, f32[8,4,3,128]{3,1,0,2:T(4,128)S(1)}, s32[8,4,6]{2,1,0:T(4,128)S(1)}, f32[60,7,128]{2,1,0:T(8,128)S(1)}, f32[8,4,7,128]{3,1,2,0:T(4...) while((s32[]{:T(128)}, f32[8,4,3,128]{3,1,0,2:T(4,128)S(1)}, ...), condition=%wide.region_27.28_spmd, body=%wide.region_8.27_spmd.sunk | while | flops 11809354 | bytes 828173 | solution.py:188
  336.6 2.6 copy.152
  339.2 13.0 %gather_fusion.19 = f32[4096,9]{1,0:T(8,128)S(1)} fusion(f32[9,8192]{0,1:T(8,128)} %bitcast.463, s32[4096]{0:T(1024)S(1)} %get-tuple-element.245), kind=kCustom, calls=%fused_computation.19 | custom fusion | bytes 311296 | tf_op jit(solution)/shard_map/gather | solution.py:216
  352.2 4.2 %fusion.142 = (f32[1,4096]{0,1:T(8,128)}, f32[1,4096]{0,1:T(8,128)}, f32[1,4096]{0,1:T(8,128)}) fusion(f32[9,4096]{0,1:T(8,128)S(1)} %bitcast.459), kind=kLoop, calls=%fused_computation.333 | loop fusion | bytes 98304 | tf_op jit(solution)/shard_map/slice | solution.py:65
  356.5 2.2 copy.155
  358.7 2.2 copy.154
  361.5 2.2 copy.157
  363.9 2.0 copy.160
  365.9 3.5 slice_add_fusion
  369.4 2.8 copy.162
  (864 shorter events, 248.8 us)
Async XLA Ops:
  2.4 13.4 %collective-permute-start.1 = (f32[4,1,7,128]{3,1,2,0:T(1,128)S(1)}, f32[4,1,7,128]{3,1,2,0:T(1,128)S(1)}, u32[]{:S(2)}, u32[]{:S(2)}) collective-permute-start(f32[4,1,7,128]{3,1,2,0:T(1,128)S(1)} %get-tuple-element.376), channel_id=1, source_target_pairs={{4,0},{8,4},{12,8},{16,12},{20,16},{24,20},{28,24},{32,28},{36,32}... | collective-permute-start | bytes 43016 | tf_op jit(solution)/shard_map/ppermute | solution.py:23
  7.5 8.3 %collective-permute-start = (f32[4,1,7,128]{3,1,2,0:T(1,128)S(1)}, f32[4,1,7,128]{3,1,2,0:T(1,128)S(1)}, u32[]{:S(2)}, u32[]{:S(2)}) collective-permute-start(f32[4,1,7,128]{3,1,2,0:T(1,128)S(1)} %get-tuple-element.375), channel_id=1, source_target_pairs={{0,4},{4,8},{8,12},{12,16},{16,20},{20,24},{24,28},{28,32},{32,36}... | collective-permute-start | bytes 43016 | tf_op jit(solution)/shard_map/ppermute | solution.py:22
  16.6 6.4 %collective-permute-start.3 = (f32[1,10,7,128]{3,1,2,0:T(8,128)S(1)}, f32[1,10,7,128]{3,1,2,0:T(8,128)S(1)}, u32[]{:S(2)}, u32[]{:S(2)}) collective-permute-start(f32[1,10,7,128]{3,1,2,0:T(8,128)S(1)} %get-tuple-element.371), channel_id=1, source_target_pairs={{1,0},{2,1},{3,2},{5,4},{6,5},{7,6},{9,8},{10,9},{11,10},{13,12},{... | collective-permute-start | bytes 107528 | tf_op jit(solution)/shard_map/ppermute | solution.py:23
  17.9 5.2 %collective-permute-start.2 = (f32[1,10,7,128]{3,1,2,0:T(8,128)S(1)}, f32[1,10,7,128]{3,1,2,0:T(8,128)S(1)}, u32[]{:S(2)}, u32[]{:S(2)}) collective-permute-start(f32[1,10,7,128]{3,1,2,0:T(8,128)S(1)} %get-tuple-element.370), channel_id=1, source_target_pairs={{0,1},{1,2},{2,3},{4,5},{5,6},{6,7},{8,9},{9,10},{10,11},{12,13},{... | collective-permute-start | bytes 107528 | tf_op jit(solution)/shard_map/ppermute | solution.py:22
  24.1 46.6 %copy-start = (f32[3,4096]{1,0:T(4,128)S(1)}, f32[3,4096]{1,0:T(4,128)}, u32[]{:S(2)}) copy-start(f32[3,4096]{1,0:T(4,128)} %param.20) | copy-start | bytes 147460
  65.1 142.4 %collective-permute-start.5 = (f32[4,1,2,128]{3,2,1,0:T(2,128)S(1)}, f32[4,1,2,128]{3,2,1,0:T(2,128)S(1)}, u32[]{:S(2)}, u32[]{:S(2)}) collective-permute-start(f32[4,1,2,128]{3,2,1,0:T(2,128)S(1)} %get-tuple-element.383), channel_id=1, source_target_pairs={{4,0},{8,4},{12,8},{16,12},{20,16},{24,20},{28,24},{32,28},{36,32}... | collective-permute-start | bytes 12296 | tf_op jit(solution)/shard_map/ppermute | solution.py:23
  68.6 138.9 %collective-permute-start.4 = (f32[4,1,2,128]{3,2,1,0:T(2,128)S(1)}, f32[4,1,2,128]{3,2,1,0:T(2,128)S(1)}, u32[]{:S(2)}, u32[]{:S(2)}) collective-permute-start(f32[4,1,2,128]{3,2,1,0:T(2,128)S(1)} %get-tuple-element.382), channel_id=1, source_target_pairs={{0,4},{4,8},{8,12},{12,16},{16,20},{20,24},{24,28},{28,32},{32,36}... | collective-permute-start | bytes 12296 | tf_op jit(solution)/shard_map/ppermute | solution.py:22
  190.0 17.4 %copy-start.2 = (f32[4,128]{1,0:T(4,128)S(1)}, f32[4,128]{1,0:T(4,128)}, u32[]{:S(2)}) copy-start(f32[4,128]{1,0:T(4,128)} %param.26) | copy-start | bytes 6148
  190.0 39.0 %copy-start.1 = (f32[9,128]{1,0:T(8,128)S(1)}, f32[9,128]{1,0:T(8,128)}, u32[]{:S(2)}) copy-start(f32[9,128]{1,0:T(8,128)} %param.25) | copy-start | bytes 13828
  190.0 39.0 %copy-start.3 = (f32[3]{0:T(128)S(1)}, f32[3]{0:T(128)}, u32[]{:S(2)}) copy-start(f32[3]{0:T(128)} %constant.113.clone) | copy-start | bytes 40
  193.6 25.8 %all-to-all-start = ((f32[64,6,128]{2,1,0:T(8,128)}), f32[64,6,128]{2,1,0:T(8,128)S(1)}, u32[]{:S(2)}, u32[]{:S(2)}) async-start(f32[64,6,128]{2,1,0:T(8,128)} %bitcast.147), calls=%async_computation | async-start | bytes 524288 | tf_op jit(solution)/shard_map/all_to_all | solution.py:35
  207.5 17.3 %collective-permute-start.7 = (f32[1,10,2,128]{3,2,1,0:T(2,128)S(1)}, f32[1,10,2,128]{3,2,1,0:T(2,128)S(1)}, u32[]{:S(2)}, u32[]{:S(2)}) collective-permute-start(f32[1,10,2,128]{3,2,1,0:T(2,128)S(1)} %get-tuple-element.381), channel_id=1, source_target_pairs={{1,0},{2,1},{3,2},{5,4},{6,5},{7,6},{9,8},{10,9},{11,10},{13,12},{... | collective-permute-start | bytes 30728 | tf_op jit(solution)/shard_map/ppermute | solution.py:23
  208.8 16.0 %collective-permute-start.6 = (f32[1,10,2,128]{3,2,1,0:T(2,128)S(1)}, f32[1,10,2,128]{3,2,1,0:T(2,128)S(1)}, u32[]{:S(2)}, u32[]{:S(2)}) collective-permute-start(f32[1,10,2,128]{3,2,1,0:T(2,128)S(1)} %get-tuple-element.380), channel_id=1, source_target_pairs={{0,1},{1,2},{2,3},{4,5},{5,6},{6,7},{8,9},{9,10},{10,11},{12,13},{... | collective-permute-start | bytes 30728 | tf_op jit(solution)/shard_map/ppermute | solution.py:22
  220.1 9.0 %all-to-all-start.1 = ((f32[4,6,128]{2,1,0:T(8,128)}), f32[4,6,128]{2,1,0:T(8,128)S(1)}, u32[]{:S(2)}, u32[]{:S(2)}) async-start(f32[4,6,128]{2,1,0:T(8,128)} %broadcast_in_dim.31), calls=%async_computation.1 | async-start | bytes 32768 | tf_op jit(solution)/shard_map/all_to_all | solution.py:41
  230.6 106.0 %all-to-all-start.2 = ((f32[64,9,128]{2,1,0:T(8,128)}), f32[64,9,128]{2,1,0:T(8,128)S(1)}, u32[]{:S(2)}, u32[]{:S(2)}) async-start(f32[64,9,128]{2,1,0:T(8,128)} %broadcast_in_dim.32), calls=%async_computation.2 | async-start | bytes 1048576 | tf_op jit(solution)/shard_map/all_to_all | solution.py:41
where the time goes:
time: 375 us; the launch traced here: 372 us
  local copies, waits for them, and re-layouts  184 us (49%)
  other arithmetic  123 us (33%)
  starting transfers between devices  49.5 us (13%)
  waiting for transfers between devices  10.5 us (3%)
  loops' own time  3.9 us (1%)
    reduce_sum x48, other arithmetic, block_accel(): jnp.sum(weight * (press * offset + damping * relative), axis=2)  38.6 us
    gather x48, local copies, waits for them, and re-layouts, block_accel(): neighbor_extra = extra_table[nbr_ids[:, entry_num]]  27.4 us
    gather x48, local copies, waits for them, and re-layouts, block_accel(): neighbor = table[nbr_ids[:, entry_num]]  26.5 us
    gather x48, local copies, waits for them, and re-layouts, block_density(): neighbor = table[nbr_ids[:, entry_num]]  26.4 us
    scatter-add x1, other arithmetic, local(): jax.ops.segment_sum(marker_terms.T, body_ids, num_segments=tile_devs * bo...  24.8 us
    gather x32, local copies, waits for them, and re-layouts, local(): source_table[operands[2]]  24.2 us
    select_n x32, other arithmetic, local(): source_table[operands[2]]  22.3 us
    squeeze x32, local copies, waits for them, and re-layouts, local(): lax.map(lambda operands: marker_force(operands[0], operands[1], source_ta...  22.1 us
  transfers between devices with their start and end apart: 11, of which 3 were waited for; matrix products, arithmetic and copies ran while one was open for 61% of the time, Pallas kernels for 0%

commit v1 on v0

v1 whole, which is shorter than its diff:
```python
import functools

import jax
import jax.numpy as jnp
from jax import lax
from jax.experimental import pallas as pl
from jax.experimental.pallas import tpu as pltpu
from jax.sharding import PartitionSpec as P

stiffness = 40.0
rest_density = 2.0
viscosity = 20.0
time_step = 0.05
gravity = 1.0
VMEM = pltpu.VMEM
SMEM = pltpu.SMEM
TP = 128
ROWS = 16


def vspec():
    return pl.BlockSpec(memory_space=VMEM)


def with_halo(shard, sides):
    for axis, dim in sides:
        size, length = (lax.axis_size(axis), shard.shape[dim])
        up = [(i, (i + 1) % size) for i in range(size - 1)]
        down = [(j, i) for i, j in up]
        last = lax.slice_in_dim(shard, length - 1, length, axis=dim)
        first = lax.slice_in_dim(shard, 0, 1, axis=dim)
        before = lax.ppermute(last, axis, up)
        after = lax.ppermute(first, axis, down)
        shard = jnp.concatenate([before, shard, after], axis=dim)
    return shard


def neighbor_id(codes, layer, column, entry, width):
    code = codes[layer, column, entry]
    down = (code * 11) >> 5
    return (layer + down) * width + column + code - 3 * down


def rows_of(ref, ident, row, count):
    return jnp.broadcast_to(ref[ident, row : row + 1, :], (count, TP))


def to_row(column_sums, eye):
    return jnp.sum(jnp.where(eye, column_sums, 0.0), axis=0, keepdims=True)


def density_kernel(codes, own, ext, out, *, columns):
    eye = lax.broadcasted_iota(jnp.int32, (TP, TP), 0) == lax.broadcasted_iota(
        jnp.int32, (TP, TP), 1
    )

    def tile_step(tile, carry):
        layer, column = tile // columns, tile % columns
        idents = [neighbor_id(codes, layer, column, k, columns + 2) for k in range(6)]
        mine = own[layer, column]
        cols = jnp.transpose(mine)
        sums = []
        for block in range(TP // ROWS):
            here = cols[block * ROWS : (block + 1) * ROWS]
            place = [jnp.broadcast_to(here[:, c : c + 1], (ROWS, TP)) for c in range(3)]
            total = jnp.zeros((ROWS, TP), jnp.float32)
            for ident in idents:
                distance = None
                for c in range(3):
                    offset = place[c] - rows_of(ext, ident, c, ROWS)
                    square = offset * offset
                    distance = square if distance is None else distance + square
                total = total + rows_of(ext, ident, 6, ROWS) * jnp.exp(-distance)
            sums.append(jnp.sum(total, axis=1, keepdims=True))
        summed = to_row(jnp.concatenate(sums, axis=0), eye)
        density = 1.0 + summed / TP
        press = (2.0 * stiffness) * (density - rest_density) / (density * density)
        damp = viscosity / density
        live = mine[6:7]
        out[layer, column] = jnp.concatenate(
            [press, damp, press * live, damp * live, jnp.zeros((4, TP), jnp.float32)], axis=0
        )
        return carry

    lax.fori_loop(0, own.shape[0] * columns, tile_step, 0)


def accel_kernel(codes, own, extra, ext, ext_extra, out, *, columns):
    eye = lax.broadcasted_iota(jnp.int32, (TP, TP), 0) == lax.broadcasted_iota(
        jnp.int32, (TP, TP), 1
    )

    def tile_step(tile, carry):
        layer, column = tile // columns, tile % columns
        idents = [neighbor_id(codes, layer, column, k, columns + 2) for k in range(6)]
        mine = own[layer, column]
        cols = jnp.transpose(mine)
        more = jnp.transpose(extra[layer, column])
        sums = [[], [], []]
        for block in range(TP // ROWS):
            span = slice(block * ROWS, (block + 1) * ROWS)
            here = cols[span]
            place = [jnp.broadcast_to(here[:, c : c + 1], (ROWS, TP)) for c in range(3)]
            speed = [jnp.broadcast_to(here[:, 3 + c : 4 + c], (ROWS, TP)) for c in range(3)]
            press_here = jnp.broadcast_to(more[span, 0:1], (ROWS, TP))
            total = [jnp.zeros((ROWS, TP), jnp.float32) for c in range(3)]
            for ident in idents:
                offsets = [place[c] - rows_of(ext, ident, c, ROWS) for c in range(3)]
                distance = offsets[0] * offsets[0] + offsets[1] * offsets[1]
                distance = distance + offsets[2] * offsets[2]
                weight = rows_of(ext, ident, 6, ROWS) * jnp.exp(-distance)
                press = weight * (press_here + rows_of(ext_extra, ident, 0, ROWS))
                damp = weight * rows_of(ext_extra, ident, 1, ROWS)
                for c in range(3):
                    relative = rows_of(ext, ident, 3 + c, ROWS) - speed[c]
                    total[c] = total[c] + (press * offsets[c] + damp * relative)
            for c in range(3):
                sums[c].append(jnp.sum(total[c], axis=1, keepdims=True))
        scale = mine[6:7] * (1.0 / TP)
        for c in range(3):
            row = to_row(jnp.concatenate(sums[c], axis=0), eye)
            out[layer, column, c : c + 1, :] = row * scale
        return carry

    lax.fori_loop(0, own.shape[0] * columns, tile_step, 0)


def marker_kernel(own, extra, place, speed, tiles, owners, slots, out, table, terms):
    layers, columns = own.shape[0], own.shape[1]
    count = layers * columns
    blocks = place.shape[1] // TP
    owner_count = out.shape[0]
    states = own[...].reshape((count, 8, TP))
    extras = extra[...].reshape((count, 8, TP))
    blank = jnp.zeros((TP - count, TP), jnp.float32)
    for field in range(8):
        part = states[:, field, :] if field < 6 else extras[:, field - 4, :]
        table[field] = jnp.transpose(jnp.concatenate([part, blank], axis=0))

    def block_step(block, carry):
        lanes = pl.ds(pl.multiple_of(block * TP, TP), TP)
        which = jnp.broadcast_to(tiles[pl.ds(block, 1), :], (8, TP))
        y = place[:, lanes]
        u = speed[:, lanes]
        at = [jnp.broadcast_to(y[c : c + 1], (8, TP)) for c in range(3)]
        moving = [jnp.broadcast_to(u[c : c + 1], (8, TP)) for c in range(3)]
        total = [jnp.zeros((8, TP), jnp.float32) for c in range(3)]
        for group in range(TP // 8):
            span = slice(group * 8, group * 8 + 8)
            fields = [
                jnp.take_along_axis(table[field, span, :], which, axis=1) for field in range(8)
            ]
            offsets = [at[c] - fields[c] for c in range(3)]
            distance = offsets[0] * offsets[0] + offsets[1] * offsets[1]
            distance = distance + offsets[2] * offsets[2]
            weight = jnp.exp(-distance)
            press = weight * fields[6]
            damp = weight * fields[7]
            for c in range(3):
                total[c] = total[c] + (press * offsets[c] + damp * (fields[3 + c] - moving[c]))
        force = [jnp.sum(total[c], axis=0, keepdims=True) * (1.0 / TP) for c in range(3)]
        where = [y[c : c + 1] for c in range(3)]
        moment = [
            where[1] * force[2] - where[2] * force[1],
            where[2] * force[0] - where[0] * force[2],
            where[0] * force[1] - where[1] * force[0],
        ]
        terms[:, lanes] = jnp.concatenate(
            force + moment + [jnp.zeros((2, TP), jnp.float32)], axis=0
        )
        return carry

    lax.fori_loop(0, blocks, block_step, 0)
    out[...] = jnp.zeros(out.shape, jnp.float32)
    wide = 2

    def sum_step(step, carry):
        left, right = [], []
        for part in range(wide):
            block = step * wide + part
            lanes = pl.ds(pl.multiple_of(block * TP, TP), TP)
            value = terms[:, lanes]
            high = value.astype(jnp.bfloat16).astype(jnp.float32)
            low = value - high
            owner = jnp.broadcast_to(owners[pl.ds(block, 1), :], (8, TP))
            slot = jnp.broadcast_to(slots[pl.ds(block, 1), :], (TP, TP))
            hot = (slot == lax.broadcasted_iota(jnp.int32, (TP, TP), 0)).astype(jnp.bfloat16)
            masks = [owner == o for o in range(owner_count)]
            for piece in (high, low):
                left.append(
                    jnp.concatenate(
                        [jnp.where(mask, piece, 0.0) for mask in masks], axis=0
                    ).astype(jnp.bfloat16)
                )
                right.append(hot)
        summed = lax.dot_general(
            jnp.concatenate(left, axis=1),
            jnp.concatenate(right, axis=1),
            (((1,), (1,)), ((), ())),
            preferred_element_type=jnp.float32,
        )
        out[...] = out[...] + summed.reshape(out.shape)
        return carry

    lax.fori_loop(0, blocks // wide, sum_step, 0)


def share_kernel(blocks, out):
    out[...] = jnp.sum(blocks[...], axis=0)


def cross(a, b):
    return [
        a[1] * b[2] - a[2] * b[1],
        a[2] * b[0] - a[0] * b[2],
        a[0] * b[1] - a[1] * b[0],
    ]


def advance_kernel(first, second, third, fourth, state, inertia, out, sent):
    totals = (first[...] + second[...]) + (third[...] + fourth[...])
    row = lambda ref, r: ref[r : r + 1, :]
    force = [totals[c : c + 1] for c in range(3)]
    moments = [totals[3 + c : 4 + c] for c in range(3)]
    center = [row(state, c) for c in range(3)]
    velocity = [row(state, 3 + c) for c in range(3)]
    spin = [row(state, 6 + c) for c in range(3)]
    inv_mass = row(inertia, 0)
    moment = [row(inertia, 1 + c) for c in range(3)]
    arm = cross(center, force)
    gyro = cross(spin, [moment[c] * spin[c] for c in range(3)])
    pull = [0.0, 0.0, -gravity]
    new_vel = [velocity[c] + time_step * (inv_mass * force[c] + pull[c]) for c in range(3)]
    new_spin = [
        spin[c] + time_step * ((moments[c] - arm[c]) - gyro[c]) / moment[c] for c in range(3)
    ]
    new_center = [center[c] + time_step * new_vel[c] for c in range(3)]
    out[...] = jnp.concatenate(new_center + new_vel + new_spin, axis=0)
    swing = cross(new_spin, center)
    base = [new_vel[c] - swing[c] for c in range(3)]
    block = jnp.concatenate(base + new_spin + [jnp.zeros((2, TP), jnp.float32)], axis=0)
    sent[...] = jnp.broadcast_to(block[None], sent.shape)


def pick_kernel(states, place, owners, slots, out):
    blocks = place.shape[1] // TP

    def block_step(block, carry):
        lanes = pl.ds(pl.multiple_of(block * TP, TP), TP)
        slot = jnp.broadcast_to(slots[pl.ds(block, 1), :], (8, TP))
        owner = jnp.broadcast_to(owners[pl.ds(block, 1), :], (8, TP))
        picked = jnp.zeros((8, TP), jnp.float32)
        for o in range(states.shape[0]):
            found = jnp.take_along_axis(states[o], slot, axis=1)
            picked = jnp.where(owner == o, found, picked)
        y = place[:, lanes]
        turn = cross([picked[3 + c : 4 + c] for c in range(3)], [y[c : c + 1] for c in range(3)])
        out[:, lanes] = picked[0:3] + jnp.concatenate(turn, axis=0)
        return carry

    lax.fori_loop(0, blocks, block_step, 0)


def cost(flops, moved, heavy=0):
    return pl.CostEstimate(flops=flops, bytes_accessed=moved, transcendentals=heavy)


def local(
    soil_state,
    tile_count,
    tile_neighbors,
    marker_pos,
    marker_vel,
    marker_tile,
    marker_owner,
    marker_slot,
    body_state,
    body_inertia,
):
    layers, columns, fields, tile_size = soil_state.shape
    marker_count = marker_pos.shape[1]
    tile_devs = lax.axis_size("tile")
    depth_devs = lax.axis_size("depth")
    f32 = jnp.float32
    smem = pl.BlockSpec(memory_space=SMEM)
    live = (
        lax.broadcasted_iota(jnp.int32, (layers, columns, 1, tile_size), 3)
        < tile_count[:, :, None, None]
    ).astype(f32)
    packed = jnp.concatenate(
        [soil_state, live, jnp.zeros((layers, columns, 1, tile_size), f32)], axis=2
    )
    sides = (("tile", 1), ("depth", 0))
    ext_count = (layers + 2) * (columns + 2)
    ext = with_halo(packed, sides).reshape((ext_count, 8, tile_size))
    pairs = layers * columns * 6 * tile_size * tile_size
    extra = pl.pallas_call(
        functools.partial(density_kernel, columns=columns),
        out_shape=jax.ShapeDtypeStruct((layers, columns, 8, tile_size), f32),
        in_specs=[smem, vspec(), vspec()],
        out_specs=vspec(),
        cost_estimate=cost(pairs * 12, 1 << 18, pairs),
        name="density",
    )(tile_neighbors, packed, ext)
    owners = marker_owner.reshape((marker_count // TP, TP))
    slots = marker_slot.reshape((marker_count // TP, TP))
    tiles = marker_tile.reshape((marker_count // TP, TP))
    partial_sums = pl.pallas_call(
        marker_kernel,
        out_shape=jax.ShapeDtypeStruct((tile_devs, 8, TP), f32),
        in_specs=[vspec()] * 7,
        out_specs=vspec(),
        scratch_shapes=[VMEM((8, TP, TP), f32), VMEM((8, marker_count), f32)],
        cost_estimate=cost(marker_count * TP * 25, 1 << 19, marker_count * TP),
        name="markers",
    )(packed, extra, marker_pos, marker_vel, tiles, owners, slots)
    arrived = lax.all_to_all(partial_sums, "tile", 0, 0, tiled=True)
    ext_extra = with_halo(extra, sides).reshape((ext_count, 8, tile_size))
    soil_accel = pl.pallas_call(
        functools.partial(accel_kernel, columns=columns),
        out_shape=jax.ShapeDtypeStruct((layers, columns, 3, tile_size), f32),
        in_specs=[smem] + [vspec()] * 4,
        out_specs=vspec(),
        cost_estimate=cost(pairs * 30, 1 << 19, pairs),
        name="accel",
    )(tile_neighbors, packed, extra, ext, ext_extra)
    share = pl.pallas_call(
        share_kernel,
        out_shape=jax.ShapeDtypeStruct((8, TP), f32),
        in_specs=[vspec()],
        out_specs=vspec(),
        name="share",
    )(arrived)
    others = [
        lax.ppermute(share, "depth", [(i, (i + k) % depth_devs) for i in range(depth_devs)])
        for k in range(1, depth_devs)
    ]
    body_next, sent = pl.pallas_call(
        advance_kernel,
        out_shape=(
            jax.ShapeDtypeStruct((9, TP), f32),
            jax.ShapeDtypeStruct((tile_devs, 8, TP), f32),
        ),
        in_specs=[vspec()] * 6,
        out_specs=(vspec(), vspec()),
        name="advance",
    )(share, *others, body_state, body_inertia)
    states = lax.all_to_all(sent, "tile", 0, 0, tiled=True)
    marker_vel_next = pl.pallas_call(
        pick_kernel,
        out_shape=jax.ShapeDtypeStruct((3, marker_count), f32),
        in_specs=[vspec()] * 4,
        out_specs=vspec(),
        name="pick",
    )(states, marker_pos, owners, slots)
    return (soil_accel, body_next, marker_vel_next)


def solution(mesh):
    placed = (
        P("depth", "tile", None, None),
        P("depth", "tile"),
        P("depth", "tile", None),
        P(None, ("tile", "depth")),
        P(None, ("tile", "depth")),
        P(("tile", "depth")),
        P(("tile", "depth"), None),
        P(("tile", "depth")),
        P(None, "tile"),
        P(None, "tile"),
    )
    return jax.shard_map(
        local,
        mesh=mesh,
        in_specs=placed,
        out_specs=(P("depth", "tile", None, None), P(None, "tile"), P(None, ("tile", "depth"))),
        check_vma=False,
    )
```

time: 375 us -> 165 us (0.44)
  local copies, waits for them, and re-layouts: 184 us -> 4.44 us
  other arithmetic: 123 us -> 2.32 us
  Pallas kernels: 0 us -> 85 us
  blocking collectives: 0 us -> 24.7 us
  starting transfers between devices: 49.5 us -> 30.7 us
  waiting for transfers between devices: 10.5 us -> 16.2 us
  loops' own time: 3.9 us -> 0 us
    gather x177 -> x0, local copies, waits for them, and re-layouts: 118 us -> none  [the longest x48 27.4 us: block_accel(): neighbor_extra = extra_table[nbr_ids[:, entry_num]]]
    pallas_call x0 -> x6, Pallas kernels: none -> 85 us  [the longest x1 42.2 us: local(): pl.pallas_call(functools.partial(accel_kernel, columns=columns), out_shap...]
    reduce_sum x98 -> x0, other arithmetic: 57.9 us -> none  [the longest x48 38.6 us: block_accel(): jnp.sum(weight * (press * offset + damping * relative), axis=2)]
    select_n x48 -> x0, other arithmetic: 26.4 us -> none  [the longest x32 22.3 us: local(): source_table[operands[2]]]
    slice x133 -> x2, local copies, waits for them, and re-layouts: 24.9 us -> 0.01 us  [with_halo(): last = lax.slice_in_dim(shard, length - 1, length, axis=dim)]
    scatter-add x1 -> x0, other arithmetic: 24.8 us -> none  [local(): jax.ops.segment_sum(marker_terms.T, body_ids, num_segments=tile_devs * bo...]
    all_to_all x0 -> x1, blocking collectives: none -> 24.7 us  [local(): arrived = lax.all_to_all(partial_sums, 'tile', 0, 0, tiled=True)]
    squeeze x72 -> x0, local copies, waits for them, and re-layouts: 22.4 us -> none  [the longest x32 22.1 us: local(): lax.map(lambda operands: marker_force(operands[0], operands[1], source_ta...]
  transfers between devices with their start and end apart: 11 -> 12, of which waited for: 3 -> 6; matrix products, arithmetic and copies ran while one was open for 61% -> 2% of each run, Pallas kernels for 0% -> 26%
where the time goes in v1:
time: 165 us; the launch traced here: 164 us
  Pallas kernels  85 us (52%)
  starting transfers between devices  30.7 us (19%)
  blocking collectives  24.7 us (15%)
  waiting for transfers between devices  16.2 us (10%)
  local copies, waits for them, and re-layouts  4.44 us (3%)
  other arithmetic  2.32 us (1%)
    pallas_call x1, Pallas kernels, local(): pl.pallas_call(functools.partial(accel_kernel, columns=columns), out_shap...  42.2 us
    all_to_all x1, blocking collectives, local(): arrived = lax.all_to_all(partial_sums, 'tile', 0, 0, tiled=True)  24.7 us
    pallas_call x1, Pallas kernels, local(): pl.pallas_call(functools.partial(density_kernel, columns=columns), out_sh...  19.4 us
    pallas_call x1, Pallas kernels, local(): pl.pallas_call(marker_kernel, out_shape=jax.ShapeDtypeStruct((tile_devs,...  14 us
    ppermute x4, starting transfers between devices, with_halo(): before = lax.ppermute(last, axis, up)  13 us
    ppermute x4, waiting for transfers between devices, with_halo(): after = lax.ppermute(first, axis, down)  12.7 us
    all_to_all x1, starting transfers between devices, local(): states = lax.all_to_all(sent, 'tile', 0, 0, tiled=True)  7.88 us
    ppermute x4, starting transfers between devices, with_halo(): after = lax.ppermute(first, axis, down)  6.43 us
  transfers between devices with their start and end apart: 12, of which 6 were waited for; matrix products, arithmetic and copies ran while one was open for 2% of the time, Pallas kernels for 26%

profile of v1, /device:TPU:1, one launch (start us, length us, event | category | flops | bytes accessed | tf_op | source)
XLA Modules:
  0.0 164.2 jit_solution(9079052374366183853)
XLA Ops:
  2.4 4.9 %collective-permute-start = (f32[4,1,8,128]{3,2,1,0:T(8,128)S(1)}, f32[4,1,8,128]{3,2,1,0:T(8,128)S(1)}, u32[]{:S(2)}, u32[]{:S(2)}) collective-permute-start(f32[4,1,8,128]{3,2,1,0:T(8,128)S(1)} %get-tuple-element.16), channel_id=1, source_target_pairs={{0,4},{4,8},{8,12},{12,16},{16,20},{20,24},{24,28},{28,32},{32,36}... | collective-permute-start | bytes 49160 | tf_op jit(solution)/shard_map/ppermute | solution.py:32
  7.4 1.9 %collective-permute-start.1 = (f32[4,1,8,128]{3,2,1,0:T(8,128)S(1)}, f32[4,1,8,128]{3,2,1,0:T(8,128)S(1)}, u32[]{:S(2)}, u32[]{:S(2)}) collective-permute-start(f32[4,1,8,128]{3,2,1,0:T(8,128)S(1)} %get-tuple-element.17), channel_id=1, source_target_pairs={{4,0},{8,4},{12,8},{16,12},{20,16},{24,20},{28,24},{32,28},{36,32}... | collective-permute-start | bytes 49160 | tf_op jit(solution)/shard_map/ppermute | solution.py:33
  9.3 3.1 %collective-permute-done.1 = f32[4,1,8,128]{3,2,1,0:T(8,128)S(1)} collective-permute-done((f32[4,1,8,128]{3,2,1,0:T(8,128)S(1)}, f32[4,1,8,128]{3,2,1,0:T(8,128)S(1)}, u32[]{:S(2)}, u32[]{:S(2)}) %collective-permute-start.1) | collective-permute-done | bytes 16416 | tf_op jit(solution)/shard_map/ppermute | solution.py:33
  12.5 3.2 %collective-permute-start.2 = (f32[1,10,8,128]{3,2,1,0:T(8,128)S(1)}, f32[1,10,8,128]{3,2,1,0:T(8,128)S(1)}, u32[]{:S(2)}, u32[]{:S(2)}) collective-permute-start(f32[1,10,8,128]{3,2,1,0:T(8,128)S(1)} %get-tuple-element.10), channel_id=1, source_target_pairs={{0,1},{1,2},{2,3},{4,5},{5,6},{6,7},{8,9},{9,10},{10,11},{12,13},{... | collective-permute-start | bytes 122888 | tf_op jit(solution)/shard_map/ppermute | solution.py:32
  15.7 1.3 collective-permute-start.3
  17.7 2.7 %collective-permute-done.3 = f32[1,10,8,128]{3,2,1,0:T(8,128)S(1)} collective-permute-done((f32[1,10,8,128]{3,2,1,0:T(8,128)S(1)}, f32[1,10,8,128]{3,2,1,0:T(8,128)S(1)}, u32[]{:S(2)}, u32[]{:S(2)}) %collective-permute-start.3) | collective-permute-done | bytes 40992 | tf_op jit(solution)/shard_map/ppermute | solution.py:33
  21.2 19.4 %density.1.extra = f32[4,8,8,128]{3,2,1,0:T(8,128)} custom-call(s32[4,8,6]{2,1,0:T(8,128)} %copy.15.codes, f32[4,8,8,128]{3,2,1,0:T(8,128)} %copy-done.2, f32[60,8,128]{2,1,0:T(8,128)} %bitcast.5), custom_call_target="tpu_custom_call" | custom-call | flops 37748736 | bytes 262144 | tf_op jit(solution)/shard_map/density/pallas_call | solution.py:297
  40.6 14.0 %markers.1 = f32[64,8,128]{2,1,0:T(8,128)} custom-call(f32[4,8,8,128]{3,2,1,0:T(8,128)} %copy-done.2, f32[4,8,8,128]{3,2,1,0:T(8,128)} %density.1.extra, f32[3,4096]{1,0:T(4,128)} %place.3, f32[3,4096]{1,0:T(4,128)} %speed.1, s32[32,128]{1,0:T(8,128)} %bitcast.12, s32[32,128]{1,0:T(8,128)} %bitcast.8, s32[32,128]{1,0:T(8,128)} %bitcast.10), custom_call_target="tpu_custom_call" | custom-call | flops 13107200 | bytes 524288 | tf_op jit(solution)/shard_map/markers/pallas_call | solution.py:308
  54.6 24.7 %all_to_all.10.blocks = f32[64,8,128]{2,1,0:T(8,128)} all-to-all(f32[64,8,128]{2,1,0:T(8,128)} %markers.1), channel_id=1, replica_groups=mesh['tile'=64,'depth'=4] {'tile'}, dimensions={0} | all-to-all | bytes 524288 | tf_op jit(solution)/shard_map/all_to_all | solution.py:317
  79.3 1.6 share.1.first
  81.7 2.2 %collective-permute-start.9 = (f32[8,128]{1,0:T(8,128)}, f32[8,128]{1,0:T(8,128)S(1)}, u32[]{:S(2)}, u32[]{:S(2)}) collective-permute-start(f32[8,128]{1,0:T(8,128)} %share.1.first), channel_id=1, source_target_pairs={{0,2},{1,3},{2,0},{3,1},{4,6},{5,7},{6,4},{7,5},{8,10},{9,11},{10,... | collective-permute-start | bytes 12296 | tf_op jit(solution)/shard_map/ppermute | solution.py:335
  84.4 1.5 collective-permute-done.9.third
  85.9 1.9 %collective-permute-done.8.second = f32[8,128]{1,0:T(8,128)S(1)} collective-permute-done((f32[8,128]{1,0:T(8,128)}, f32[8,128]{1,0:T(8,128)S(1)}, u32[]{:S(2)}, u32[]{:S(2)}) %collective-permute-start.8) | collective-permute-done | bytes 4128 | tf_op jit(solution)/shard_map/ppermute | solution.py:335
  88.5 1.5 advance.1
  89.9 7.9 %all-to-all-start.1 = ((f32[64,8,128]{2,1,0:T(8,128)}), f32[64,8,128]{2,1,0:T(8,128)S(1)}, u32[]{:S(2)}, u32[]{:S(2)}) async-start(f32[64,8,128]{2,1,0:T(8,128)} %get-tuple-element.6), calls=%async_computation.1 | async-start | bytes 524288 | tf_op jit(solution)/shard_map/all_to_all | solution.py:348
  97.9 3.5 %collective-permute-start.4 = (f32[4,1,8,128]{3,2,1,0:T(8,128)S(1)}, f32[4,1,8,128]{3,2,1,0:T(8,128)S(1)}, u32[]{:S(2)}, u32[]{:S(2)}) collective-permute-start(f32[4,1,8,128]{3,2,1,0:T(8,128)S(1)} %get-tuple-element.14), channel_id=1, source_target_pairs={{0,4},{4,8},{8,12},{12,16},{16,20},{20,24},{24,28},{28,32},{32,36}... | collective-permute-start | bytes 49160 | tf_op jit(solution)/shard_map/ppermute | solution.py:32
  101.4 1.9 %collective-permute-start.5 = (f32[4,1,8,128]{3,2,1,0:T(8,128)S(1)}, f32[4,1,8,128]{3,2,1,0:T(8,128)S(1)}, u32[]{:S(2)}, u32[]{:S(2)}) collective-permute-start(f32[4,1,8,128]{3,2,1,0:T(8,128)S(1)} %get-tuple-element.15), channel_id=1, source_target_pairs={{4,0},{8,4},{12,8},{16,12},{20,16},{24,20},{28,24},{32,28},{36,32}... | collective-permute-start | bytes 49160 | tf_op jit(solution)/shard_map/ppermute | solution.py:33
  103.3 3.4 %collective-permute-done.5 = f32[4,1,8,128]{3,2,1,0:T(8,128)S(1)} collective-permute-done((f32[4,1,8,128]{3,2,1,0:T(8,128)S(1)}, f32[4,1,8,128]{3,2,1,0:T(8,128)S(1)}, u32[]{:S(2)}, u32[]{:S(2)}) %collective-permute-start.5) | collective-permute-done | bytes 16416 | tf_op jit(solution)/shard_map/ppermute | solution.py:33
  106.8 1.3 collective-permute-start.6
  108.1 1.3 collective-permute-start.7
  109.4 3.4 %collective-permute-done.7 = f32[1,10,8,128]{3,2,1,0:T(8,128)S(1)} collective-permute-done((f32[1,10,8,128]{3,2,1,0:T(8,128)S(1)}, f32[1,10,8,128]{3,2,1,0:T(8,128)S(1)}, u32[]{:S(2)}, u32[]{:S(2)}) %collective-permute-start.7) | collective-permute-done | bytes 40992 | tf_op jit(solution)/shard_map/ppermute | solution.py:33
  113.5 42.2 %accel.1 = f32[4,8,3,128]{3,2,1,0:T(4,128)} custom-call(s32[4,8,6]{2,1,0:T(8,128)} %copy.15.codes, f32[4,8,8,128]{3,2,1,0:T(8,128)} %copy-done.2, f32[4,8,8,128]{3,2,1,0:T(8,128)} %density.1.extra, f32[60,8,128]{2,1,0:T(8,128)} %bitcast.6, f32[60,8,128]{2,1,0:T(8,128)} %bitcast.7), custom_call_target="tpu_custom_call" | custom-call | flops 94371840 | bytes 524288 | tf_op jit(solution)/shard_map/accel/pallas_call | solution.py:319
  155.7 1.5 copy.16
  157.9 6.3 %pick.1 = f32[3,4096]{1,0:T(4,128)} custom-call(f32[64,8,128]{2,1,0:T(8,128)} %copy-done, f32[3,4096]{1,0:T(4,128)} %place.3, s32[32,128]{1,0:T(8,128)} %bitcast.9, s32[32,128]{1,0:T(8,128)} %bitcast.11), custom_call_target="tpu_custom_call" | custom-call | tf_op jit(solution)/shard_map/pick/pallas_call | solution.py:349
  (33 shorter events, 6.6 us)
Async XLA Ops:
  2.4 10.0 %copy-start.2 = (f32[4,8,8,128]{3,2,1,0:T(8,128)}, f32[4,8,8,128]{3,2,1,0:T(8,128)S(1)}, u32[]{:S(2)}) copy-start(f32[4,8,8,128]{3,2,1,0:T(8,128)S(1)} %pad_maximum_fusion.2.own) | copy-start | bytes 393220
  2.4 6.9 %collective-permute-start = (f32[4,1,8,128]{3,2,1,0:T(8,128)S(1)}, f32[4,1,8,128]{3,2,1,0:T(8,128)S(1)}, u32[]{:S(2)}, u32[]{:S(2)}) collective-permute-start(f32[4,1,8,128]{3,2,1,0:T(8,128)S(1)} %get-tuple-element.16), channel_id=1, source_target_pairs={{0,4},{4,8},{8,12},{12,16},{16,20},{20,24},{24,28},{28,32},{32,36}... | collective-permute-start | bytes 49160 | tf_op jit(solution)/shard_map/ppermute | solution.py:32
  7.4 5.1 %collective-permute-start.1 = (f32[4,1,8,128]{3,2,1,0:T(8,128)S(1)}, f32[4,1,8,128]{3,2,1,0:T(8,128)S(1)}, u32[]{:S(2)}, u32[]{:S(2)}) collective-permute-start(f32[4,1,8,128]{3,2,1,0:T(8,128)S(1)} %get-tuple-element.17), channel_id=1, source_target_pairs={{4,0},{8,4},{12,8},{16,12},{20,16},{24,20},{28,24},{32,28},{36,32}... | collective-permute-start | bytes 49160 | tf_op jit(solution)/shard_map/ppermute | solution.py:33
  12.4 4.6 %copy-start.3 = (s32[4,8,6]{1,0,2:T(4,128)S(1)}, s32[4,8,6]{1,0,2:T(4,128)}, u32[]{:S(2)}) copy-start(s32[4,8,6]{1,0,2:T(4,128)} %param.12) | copy-start | bytes 2308
  12.5 5.2 %collective-permute-start.2 = (f32[1,10,8,128]{3,2,1,0:T(8,128)S(1)}, f32[1,10,8,128]{3,2,1,0:T(8,128)S(1)}, u32[]{:S(2)}, u32[]{:S(2)}) collective-permute-start(f32[1,10,8,128]{3,2,1,0:T(8,128)S(1)} %get-tuple-element.10), channel_id=1, source_target_pairs={{0,1},{1,2},{2,3},{4,5},{5,6},{6,7},{8,9},{9,10},{10,11},{12,13},{... | collective-permute-start | bytes 122888 | tf_op jit(solution)/shard_map/ppermute | solution.py:32
  15.7 4.7 %collective-permute-start.3 = (f32[1,10,8,128]{3,2,1,0:T(8,128)S(1)}, f32[1,10,8,128]{3,2,1,0:T(8,128)S(1)}, u32[]{:S(2)}, u32[]{:S(2)}) collective-permute-start(f32[1,10,8,128]{3,2,1,0:T(8,128)S(1)} %get-tuple-element.11), channel_id=1, source_target_pairs={{1,0},{2,1},{3,2},{5,4},{6,5},{7,6},{9,8},{10,9},{11,10},{13,12},{... | collective-permute-start | bytes 122888 | tf_op jit(solution)/shard_map/ppermute | solution.py:33
  80.9 3.5 %collective-permute-start.10 = (f32[8,128]{1,0:T(8,128)}, f32[8,128]{1,0:T(8,128)S(1)}, u32[]{:S(2)}, u32[]{:S(2)}) collective-permute-start(f32[8,128]{1,0:T(8,128)} %share.1.first), channel_id=1, source_target_pairs={{0,3},{1,0},{2,1},{3,2},{4,7},{5,4},{6,5},{7,6},{8,11},{9,8},{10,9... | collective-permute-start | bytes 12296 | tf_op jit(solution)/shard_map/ppermute | solution.py:335
  81.7 4.2 %collective-permute-start.9 = (f32[8,128]{1,0:T(8,128)}, f32[8,128]{1,0:T(8,128)S(1)}, u32[]{:S(2)}, u32[]{:S(2)}) collective-permute-start(f32[8,128]{1,0:T(8,128)} %share.1.first), channel_id=1, source_target_pairs={{0,2},{1,3},{2,0},{3,1},{4,6},{5,7},{6,4},{7,5},{8,10},{9,11},{10,... | collective-permute-start | bytes 12296 | tf_op jit(solution)/shard_map/ppermute | solution.py:335
  84.0 3.9 %collective-permute-start.8 = (f32[8,128]{1,0:T(8,128)}, f32[8,128]{1,0:T(8,128)S(1)}, u32[]{:S(2)}, u32[]{:S(2)}) collective-permute-start(f32[8,128]{1,0:T(8,128)} %share.1.first), channel_id=1, source_target_pairs={{0,1},{1,2},{2,3},{3,0},{4,5},{5,6},{6,7},{7,4},{8,9},{9,10},{10,1... | collective-permute-start | bytes 12296 | tf_op jit(solution)/shard_map/ppermute | solution.py:335
  84.4 3.5 %copy-start.4 = (f32[8,128]{1,0:T(8,128)}, f32[8,128]{1,0:T(8,128)S(1)}, u32[]{:S(2)}) copy-start(f32[8,128]{1,0:T(8,128)S(1)} %collective-permute-done.10.fourth) | copy-start | bytes 12292
  85.9 1.9 %copy-start.5 = (f32[8,128]{1,0:T(8,128)}, f32[8,128]{1,0:T(8,128)S(1)}, u32[]{:S(2)}) copy-start(f32[8,128]{1,0:T(8,128)S(1)} %collective-permute-done.9.third) | copy-start | bytes 12292
  87.9 0.6 copy-start.6
  89.9 7.9 %copy-start.1 = (f32[4,8,8,128]{3,2,1,0:T(8,128)S(1)}, f32[4,8,8,128]{3,2,1,0:T(8,128)}, u32[]{:S(2)}) copy-start(f32[4,8,8,128]{3,2,1,0:T(8,128)} %density.1.extra) | copy-start | bytes 393220
  89.9 67.2 %all-to-all-start.1 = ((f32[64,8,128]{2,1,0:T(8,128)}), f32[64,8,128]{2,1,0:T(8,128)S(1)}, u32[]{:S(2)}, u32[]{:S(2)}) async-start(f32[64,8,128]{2,1,0:T(8,128)} %get-tuple-element.6), calls=%async_computation.1 | async-start | bytes 524288 | tf_op jit(solution)/shard_map/all_to_all | solution.py:348
  97.9 5.5 %collective-permute-start.4 = (f32[4,1,8,128]{3,2,1,0:T(8,128)S(1)}, f32[4,1,8,128]{3,2,1,0:T(8,128)S(1)}, u32[]{:S(2)}, u32[]{:S(2)}) collective-permute-start(f32[4,1,8,128]{3,2,1,0:T(8,128)S(1)} %get-tuple-element.14), channel_id=1, source_target_pairs={{0,4},{4,8},{8,12},{12,16},{16,20},{20,24},{24,28},{28,32},{32,36}... | collective-permute-start | bytes 49160 | tf_op jit(solution)/shard_map/ppermute | solution.py:32
  101.4 5.4 %collective-permute-start.5 = (f32[4,1,8,128]{3,2,1,0:T(8,128)S(1)}, f32[4,1,8,128]{3,2,1,0:T(8,128)S(1)}, u32[]{:S(2)}, u32[]{:S(2)}) collective-permute-start(f32[4,1,8,128]{3,2,1,0:T(8,128)S(1)} %get-tuple-element.15), channel_id=1, source_target_pairs={{4,0},{8,4},{12,8},{16,12},{20,16},{24,20},{28,24},{32,28},{36,32}... | collective-permute-start | bytes 49160 | tf_op jit(solution)/shard_map/ppermute | solution.py:33
  106.8 2.6 %collective-permute-start.6 = (f32[1,10,8,128]{3,2,1,0:T(8,128)S(1)}, f32[1,10,8,128]{3,2,1,0:T(8,128)S(1)}, u32[]{:S(2)}, u32[]{:S(2)}) collective-permute-start(f32[1,10,8,128]{3,2,1,0:T(8,128)S(1)} %get-tuple-element.12), channel_id=1, source_target_pairs={{0,1},{1,2},{2,3},{4,5},{5,6},{6,7},{8,9},{9,10},{10,11},{12,13},{... | collective-permute-start | bytes 122888 | tf_op jit(solution)/shard_map/ppermute | solution.py:32
  108.1 4.7 %collective-permute-start.7 = (f32[1,10,8,128]{3,2,1,0:T(8,128)S(1)}, f32[1,10,8,128]{3,2,1,0:T(8,128)S(1)}, u32[]{:S(2)}, u32[]{:S(2)}) collective-permute-start(f32[1,10,8,128]{3,2,1,0:T(8,128)S(1)} %get-tuple-element.13), channel_id=1, source_target_pairs={{1,0},{2,1},{3,2},{5,4},{6,5},{7,6},{9,8},{10,9},{11,10},{13,12},{... | collective-permute-start | bytes 122888 | tf_op jit(solution)/shard_map/ppermute | solution.py:33
  157.2 0.7 copy-start

commit v2 on v1

v2 whole, which is shorter than its diff:
```python
import functools

import jax
import jax.numpy as jnp
from jax import lax
from jax.experimental import pallas as pl
from jax.experimental.pallas import tpu as pltpu
from jax.sharding import PartitionSpec as P

stiffness = 40.0
rest_density = 2.0
viscosity = 20.0
time_step = 0.05
gravity = 1.0
VMEM = pltpu.VMEM
SMEM = pltpu.SMEM
TP = 128
ROWS = 16
AUG = 48
FACTORS = 80
SCALE = (2.0 * 1.4426950408889634) ** 0.5
FAR = 1e30
PLACE_LIMIT = 4.0
SPEED_LIMIT = 256.0
F32 = jnp.float32
BF16 = jnp.bfloat16
NT = (((1,), (1,)), ((), ()))


def vspec():
    return pl.BlockSpec(memory_space=VMEM)


def sspec():
    return pl.BlockSpec(memory_space=SMEM)


def params(limit=16 << 20):
    return pltpu.CompilerParams(vmem_limit_bytes=limit)


def cost(flops, moved, heavy=0):
    return pl.CostEstimate(flops=flops, bytes_accessed=moved, transcendentals=heavy)


def row_mask():
    return lax.broadcasted_iota(jnp.int32, (8, TP), 0)


def eye_mask():
    return lax.broadcasted_iota(jnp.int32, (TP, TP), 0) == lax.broadcasted_iota(
        jnp.int32, (TP, TP), 1
    )


def split3(value):
    high = value.astype(BF16).astype(F32)
    rest = value - high
    middle = rest.astype(BF16).astype(F32)
    return high, middle, rest - middle


def augmented(raw, source):
    row = row_mask()
    scaled = raw * SCALE
    square = scaled * scaled
    norm = -0.5 * (square[0:1] + square[1:2] + square[2:3])
    if source:
        third, fourth = norm + (raw[6:7] - 1.0) * FAR, jnp.ones((1, TP), F32)
    else:
        third, fourth = jnp.ones((1, TP), F32), norm
    full = jnp.where(
        row < 3, scaled, jnp.where(row == 3, third, jnp.where(row == 4, fourth, 0.0))
    )
    h, m, l = split3(full)
    return jnp.concatenate([h, m, h, m, l, h] if source else [h, h, m, m, h, l], axis=0)


def assemble(own, west, east, up, down, ext):
    layers, columns = own.shape[0], own.shape[1]
    ext[0:2] = up[...]
    ext[layers + 2 : layers + 4] = down[...]
    ext[2 : layers + 2, 0:2] = west[...]
    ext[2 : layers + 2, columns + 2 : columns + 4] = east[...]
    ext[2 : layers + 2, 2 : columns + 2] = own[...]


def moderate(ext):
    span, width = ext.shape[0], ext.shape[1]
    flat = ext[...].reshape((span * width, 8, TP))
    peak = jnp.max(jnp.abs(flat), axis=0)
    row = row_mask()
    ratio = jnp.where(
        row < 3, peak / PLACE_LIMIT, jnp.where(row < 6, peak / SPEED_LIMIT, 0.0)
    )
    return jnp.max(ratio) <= 1.0


def near(codes, layer, column, row, col):
    places = []
    for k in range(6):
        code = codes[k, layer, column]
        down = (code * 11) >> 5
        places.append((row + down - 1, col + code - 3 * down - 1))
    return places


def to_row(total, eye):
    sums = jnp.sum(total, axis=1, keepdims=True)
    return jnp.sum(jnp.where(eye, sums, 0.0), axis=0, keepdims=True)


def fast_weights(left, btab, places):
    weights = []
    for p in range(3):
        right = jnp.concatenate([btab[places[2 * p]], btab[places[2 * p + 1]]], axis=1)
        weights.append(
            jnp.exp2(lax.dot_general(left, right, (((1,), (0,)), ((), ())), preferred_element_type=F32))
        )
    return weights


def fast_sum(left, btab, places, eye):
    total = None
    for weight in fast_weights(left, btab, places):
        part = weight[:, 0:TP] + weight[:, TP : 2 * TP]
        total = part if total is None else total + part
    return to_row(total, eye)


def rows_of(ref, place, row, count):
    return jnp.broadcast_to(ref[place[0], place[1], row : row + 1, :], (count, TP))


def slow_sum(ext, row, col, places, eye):
    cols = jnp.transpose(ext[row, col])
    sums = []
    for block in range(TP // ROWS):
        here = cols[block * ROWS : (block + 1) * ROWS]
        spot = [jnp.broadcast_to(here[:, c : c + 1], (ROWS, TP)) for c in range(3)]
        total = jnp.zeros((ROWS, TP), F32)
        for place in places:
            distance = None
            for c in range(3):
                offset = spot[c] - rows_of(ext, place, c, ROWS)
                square = offset * offset
                distance = square if distance is None else distance + square
            total = total + rows_of(ext, place, 6, ROWS) * jnp.exp(-distance)
        sums.append(jnp.sum(total, axis=1, keepdims=True))
    return jnp.sum(jnp.where(eye, jnp.concatenate(sums, axis=0), 0.0), axis=0, keepdims=True)


def slow_accel(ext, press_ref, damp_ref, row, col, places, eye):
    cols = jnp.transpose(ext[row, col])
    more = jnp.transpose(
        jnp.broadcast_to(press_ref[row - 1, pl.ds(col - 1, 1), :], (8, TP))
    )
    sums = [[], [], []]
    for block in range(TP // ROWS):
        span = slice(block * ROWS, (block + 1) * ROWS)
        here = cols[span]
        spot = [jnp.broadcast_to(here[:, c : c + 1], (ROWS, TP)) for c in range(3)]
        speed = [jnp.broadcast_to(here[:, 3 + c : 4 + c], (ROWS, TP)) for c in range(3)]
        press_here = jnp.broadcast_to(more[span, 0:1], (ROWS, TP))
        total = [jnp.zeros((ROWS, TP), F32) for c in range(3)]
        for place in places:
            offsets = [spot[c] - rows_of(ext, place, c, ROWS) for c in range(3)]
            distance = offsets[0] * offsets[0] + offsets[1] * offsets[1]
            distance = distance + offsets[2] * offsets[2]
            weight = rows_of(ext, place, 6, ROWS) * jnp.exp(-distance)
            there = (place[0] - 1, pl.ds(place[1] - 1, 1), slice(None))
            press = weight * (press_here + jnp.broadcast_to(press_ref[there], (ROWS, TP)))
            damp = weight * jnp.broadcast_to(damp_ref[there], (ROWS, TP))
            for c in range(3):
                relative = rows_of(ext, place, 3 + c, ROWS) - speed[c]
                total[c] = total[c] + (press * offsets[c] + damp * relative)
        for c in range(3):
            sums[c].append(jnp.sum(total[c], axis=1, keepdims=True))
    return [
        jnp.sum(jnp.where(eye, jnp.concatenate(part, axis=0), 0.0), axis=0, keepdims=True)
        for part in sums
    ]


def state_of(summed):
    density = 1.0 + summed * (1.0 / TP)
    press = (2.0 * stiffness) * (density - rest_density) / (density * density)
    return press, viscosity / density


def fill_sources(ext, btab, first, last, left, right):
    def step(index, carry):
        row, col = first + index // (right - left), left + index % (right - left)
        btab[row, col] = augmented(ext[row, col], True).astype(BF16)
        return carry

    lax.fori_loop(0, (last - first) * (right - left), step, 0, unroll=4)


def left_of(ext, row, col):
    return jnp.transpose(augmented(ext[row, col], False)).astype(BF16)


def prep_kernel(counts, codes, soil, out):
    layers, columns = out.shape[0], out.shape[1]
    lane = lax.broadcasted_iota(jnp.int32, (1, TP), 1)
    for layer in range(layers):
        for column in range(columns):
            listed = jnp.zeros((1, TP), jnp.int32)
            for k in range(6):
                listed = jnp.where(lane == k, codes[k, layer, column], listed)
            live = jnp.where(lane < counts[layer, column], 1.0, 0.0)
            rows = [soil[layer, c, column : column + 1, :] for c in range(6)]
            out[layer, column] = jnp.concatenate(rows + [live, listed.astype(F32)], axis=0)


def density_kernel(codes, own, west, east, up, down, out, ext, btab, sums, lives):
    layers, columns = own.shape[0], own.shape[1]
    assemble(own, west, east, up, down, ext)
    eye = eye_mask()
    fast = moderate(ext)

    @pl.when(fast)
    def _():
        fill_sources(ext, btab, 1, layers + 3, 1, columns + 3)

        def step(pair, carry):
            for half in range(2):
                tile = pair * 2 + half
                layer, column = tile // columns, tile % columns
                places = near(codes, layer, column, layer + 2, column + 2)
                left = left_of(ext, layer + 2, column + 2)
                sums[pl.ds(tile, 1), :] = fast_sum(left, btab, places, eye)
            return carry

        lax.fori_loop(0, layers * columns // 2, step, 0)

    @pl.when(jnp.logical_not(fast))
    def _():
        def step(tile, carry):
            layer, column = tile // columns, tile % columns
            places = near(codes, layer, column, layer + 2, column + 2)
            sums[pl.ds(tile, 1), :] = slow_sum(ext, layer + 2, column + 2, places, eye)
            return carry

        lax.fori_loop(0, layers * columns, step, 0)

    for layer in range(layers):
        for column in range(columns):
            tile = layer * columns + column
            lives[tile : tile + 1, :] = own[layer, column, 6:7, :]
    press, damp = state_of(sums[...])
    live = lives[...]
    out[0] = press
    out[1] = damp
    out[2] = press * live
    out[3] = damp * live


def accel_kernel(
    codes, own, west, east, up, down, extra, out, ext, btab, ftab, press_ref, damp_ref
):
    layers, columns = own.shape[0], own.shape[1]
    assemble(own, west, east, up, down, ext)
    eye = eye_mask()
    fast = moderate(ext)
    for layer in range(layers):
        span = slice(layer * columns, (layer + 1) * columns)
        press_ref[layer + 1, 1 : columns + 1, :] = extra[0, span, :]
        damp_ref[layer + 1, 1 : columns + 1, :] = extra[1, span, :]

    def ring(handle):
        def across(index, carry):
            handle(1, index + 1)
            handle(layers + 2, index + 1)
            return carry

        def along(index, carry):
            handle(index + 2, 1)
            handle(index + 2, columns + 2)
            return carry

        lax.fori_loop(0, columns + 2, across, 0)
        lax.fori_loop(0, layers, along, 0)

    def keep(row, col, summed):
        press, damp = state_of(summed)
        press_ref[row - 1, pl.ds(col - 1, 1), :] = press
        damp_ref[row - 1, pl.ds(col - 1, 1), :] = damp

    @pl.when(fast)
    def _():
        fill_sources(ext, btab, 0, layers + 4, 0, columns + 4)

        def ring_sum(row, col):
            places = near(codes, row, col, row, col)
            keep(row, col, fast_sum(left_of(ext, row, col), btab, places, eye))

        ring(ring_sum)

        def factors(index, carry):
            row, col = 1 + index // (columns + 2), 1 + index % (columns + 2)
            raw = ext[row, col]
            press = jnp.broadcast_to(press_ref[row - 1, pl.ds(col - 1, 1), :], (8, TP))
            damp = jnp.broadcast_to(damp_ref[row - 1, pl.ds(col - 1, 1), :], (8, TP))
            value = jnp.concatenate([raw, press * raw, damp * raw], axis=0)
            parts = split3(value)
            ftab[row, col] = jnp.concatenate(
                list(parts) + [jnp.zeros((FACTORS - 72, TP), F32)], axis=0
            ).astype(BF16)
            return carry

        lax.fori_loop(0, (layers + 2) * (columns + 2), factors, 0, unroll=2)

        def step(pair, carry):
            for half in range(2):
                tile = pair * 2 + half
                layer, column = tile // columns, tile % columns
                row, col = layer + 2, column + 2
                places = near(codes, row, col, row, col)
                weights = fast_weights(left_of(ext, row, col), btab, places)
                highs = [w.astype(BF16) for w in weights]
                lows = [(w - h.astype(F32)).astype(BF16) for w, h in zip(weights, highs)]
                sources = [ftab[place] for place in places]
                summed = lax.dot_general(
                    jnp.concatenate(sources + sources, axis=1),
                    jnp.concatenate(highs + lows, axis=1),
                    NT,
                    preferred_element_type=F32,
                )
                summed = summed[0:24] + summed[24:48] + summed[48:72]
                plain, pressed, damped = summed[0:8], summed[8:16], summed[16:24]
                raw = ext[row, col]
                press = press_ref[row - 1, pl.ds(col - 1, 1), :]
                push = raw * (press * plain[6:7] + pressed[6:7]) - (press * plain + pressed)
                drag = damped - raw * damped[6:7]
                total = (push[0:3] + drag[3:6]) * (raw[6:7] * (1.0 / TP))
                for c in range(3):
                    out[layer, c, pl.ds(column, 1), :] = total[c : c + 1]
            return carry

        lax.fori_loop(0, layers * columns // 2, step, 0)

    @pl.when(jnp.logical_not(fast))
    def _():
        def ring_sum(row, col):
            places = near(codes, row, col, row, col)
            keep(row, col, slow_sum(ext, row, col, places, eye))

        ring(ring_sum)

        def step(tile, carry):
            layer, column = tile // columns, tile % columns
            row, col = layer + 2, column + 2
            places = near(codes, row, col, row, col)
            rows = slow_accel(ext, press_ref, damp_ref, row, col, places, eye)
            scale = ext[row, col, 6:7, :] * (1.0 / TP)
            for c in range(3):
                out[layer, c, pl.ds(column, 1), :] = rows[c] * scale
            return carry

        lax.fori_loop(0, layers * columns, step, 0)


def marker_kernel(soil, extra, place, speed, tiles, owners, slots, out, table):
    layers, columns = soil.shape[0], soil.shape[2]
    count = layers * columns
    pairs = place.shape[1] // (2 * TP)
    owner_count = out.shape[0]
    groups = TP // 16
    for field in range(8):
        if field < 6:
            part = jnp.concatenate([soil[layer, field] for layer in range(layers)], axis=0)
        else:
            part = extra[field - 4]
        pieces = list(split3(part)) + [jnp.zeros((TP - 3 * count, TP), F32)]
        turned = jnp.transpose(jnp.concatenate(pieces, axis=0)).astype(BF16)
        for group in range(groups):
            at = group * TP + field * 16
            table[at : at + 16, :] = turned[group * 16 : group * 16 + 16]
    entry = lax.broadcasted_iota(jnp.int32, (TP, TP), 0)
    listed = jnp.where(entry < 3 * count, lax.rem(entry, count), -1)
    out[...] = jnp.zeros(out.shape, F32)

    def add_terms(pair, terms):
        left, right = [], []
        for part in range(2):
            block = pair * 2 + part
            high = terms[part].astype(BF16).astype(F32)
            low = terms[part] - high
            owner = jnp.broadcast_to(owners[pl.ds(block, 1), :], (8, TP))
            slot = jnp.broadcast_to(slots[pl.ds(block, 1), :], (TP, TP))
            hot = jnp.where(slot == entry, 1.0, 0.0).astype(BF16)
            masks = [owner == o for o in range(owner_count)]
            for piece in (high, low):
                left.append(
                    jnp.concatenate(
                        [jnp.where(mask, piece, 0.0) for mask in masks], axis=0
                    ).astype(BF16)
                )
                right.append(hot)
        summed = lax.dot_general(
            jnp.concatenate(left, axis=1),
            jnp.concatenate(right, axis=1),
            NT,
            preferred_element_type=F32,
        )
        out[...] = out[...] + summed.reshape(out.shape)

    def forces_on(block):
        lanes = pl.ds(pl.multiple_of(block * TP, TP), TP)
        which = jnp.broadcast_to(tiles[pl.ds(block, 1), :], (TP, TP))
        hot = jnp.where(which == listed, 1.0, 0.0).astype(BF16)
        y = place[:, lanes]
        u = speed[:, lanes]
        at = [jnp.broadcast_to(y[c : c + 1], (16, TP)) for c in range(3)]
        total = [jnp.zeros((16, TP), F32) for c in range(3)]
        drag = jnp.zeros((16, TP), F32)
        for group in range(groups):
            picked = lax.dot_general(
                table[group * TP : (group + 1) * TP, :],
                hot,
                (((1,), (0,)), ((), ())),
                preferred_element_type=F32,
            )
            fields = [picked[16 * field : 16 * field + 16] for field in range(8)]
            offsets = [at[c] - fields[c] for c in range(3)]
            distance = offsets[0] * offsets[0] + offsets[1] * offsets[1]
            distance = distance + offsets[2] * offsets[2]
            weight = jnp.exp2(distance * (-0.5 * SCALE * SCALE))
            press = weight * fields[6]
            damp = weight * fields[7]
            drag = drag + damp
            for c in range(3):
                total[c] = total[c] + (press * offsets[c] + damp * fields[3 + c])
        slowed = jnp.sum(drag, axis=0, keepdims=True)
        force = [
            (jnp.sum(total[c], axis=0, keepdims=True) - u[c : c + 1] * slowed) * (1.0 / TP)
            for c in range(3)
        ]
        where = [y[c : c + 1] for c in range(3)]
        moment = cross(where, force)
        return jnp.concatenate(force + moment + [jnp.zeros((2, TP), F32)], axis=0)

    def step(pair, terms):
        add_terms(jnp.maximum(pair - 1, 0), terms)
        return (forces_on(pair * 2), forces_on(pair * 2 + 1))

    blank = jnp.zeros((8, TP), F32)
    terms = lax.fori_loop(0, pairs, step, (blank, blank))
    add_terms(pairs - 1, terms)


def cross(a, b):
    return [
        a[1] * b[2] - a[2] * b[1],
        a[2] * b[0] - a[0] * b[2],
        a[0] * b[1] - a[1] * b[0],
    ]


def advance_kernel(first, second, third, fourth, state, inertia, out, sent):
    totals = (first[...] + second[...]) + (third[...] + fourth[...])
    row = lambda ref, r: ref[r : r + 1, :]
    force = [totals[c : c + 1] for c in range(3)]
    moments = [totals[3 + c : 4 + c] for c in range(3)]
    center = [row(state, c) for c in range(3)]
    velocity = [row(state, 3 + c) for c in range(3)]
    spin = [row(state, 6 + c) for c in range(3)]
    inv_mass = row(inertia, 0)
    moment = [row(inertia, 1 + c) for c in range(3)]
    arm = cross(center, force)
    gyro = cross(spin, [moment[c] * spin[c] for c in range(3)])
    pull = [0.0, 0.0, -gravity]
    new_vel = [velocity[c] + time_step * (inv_mass * force[c] + pull[c]) for c in range(3)]
    new_spin = [
        spin[c] + time_step * ((moments[c] - arm[c]) - gyro[c]) / moment[c] for c in range(3)
    ]
    new_center = [center[c] + time_step * new_vel[c] for c in range(3)]
    out[...] = jnp.concatenate(new_center + new_vel + new_spin, axis=0)
    swing = cross(new_spin, center)
    base = [new_vel[c] - swing[c] for c in range(3)]
    block = jnp.concatenate(base + new_spin + [jnp.zeros((2, TP), F32)], axis=0)
    sent[...] = jnp.broadcast_to(block[None], sent.shape)


def pick_kernel(states, place, owners, slots, out):
    pairs = place.shape[1] // (2 * TP)
    owner_count = states.shape[0]

    def step(pair, carry):
        for half in range(2):
            block = pair * 2 + half
            lanes = pl.ds(pl.multiple_of(block * TP, TP), TP)
            slot = jnp.broadcast_to(slots[pl.ds(block, 1), :], (8, TP))
            owner = jnp.broadcast_to(owners[pl.ds(block, 1), :], (8, TP))
            found = [jnp.zeros((8, TP), F32) for lane in range(4)]
            for o in range(owner_count):
                here = jnp.take_along_axis(states[o], slot, axis=1)
                found[o % 4] = jnp.where(owner == o, here, found[o % 4])
            picked = (found[0] + found[1]) + (found[2] + found[3])
            y = place[:, lanes]
            turn = cross(
                [picked[3 + c : 4 + c] for c in range(3)], [y[c : c + 1] for c in range(3)]
            )
            out[:, lanes] = picked[0:3] + jnp.concatenate(turn, axis=0)
        return carry

    lax.fori_loop(0, pairs, step, 0)


def shifted(shard, axis, dim, width):
    size, length = lax.axis_size(axis), shard.shape[dim]
    up = [(i, i + 1) for i in range(size - 1)]
    down = [(j, i) for i, j in up]
    last = lax.slice_in_dim(shard, length - width, length, axis=dim)
    first = lax.slice_in_dim(shard, 0, width, axis=dim)
    return lax.ppermute(last, axis, up), lax.ppermute(first, axis, down)


def local(
    soil_state,
    tile_count,
    tile_neighbors,
    marker_pos,
    marker_vel,
    marker_tile,
    marker_owner,
    marker_slot,
    body_state,
    body_inertia,
):
    layers, columns, fields, tile_size = soil_state.shape
    marker_count = marker_pos.shape[1]
    tile_devs = lax.axis_size("tile")
    depth_devs = lax.axis_size("depth")
    soil = jnp.transpose(soil_state, (0, 2, 1, 3))
    codes = jnp.transpose(tile_neighbors, (2, 0, 1))
    own = pl.pallas_call(
        prep_kernel,
        out_shape=jax.ShapeDtypeStruct((layers, columns, 8, TP), F32),
        in_specs=[sspec(), sspec(), vspec()],
        out_specs=vspec(),
        compiler_params=params(),
        name="prep",
    )(tile_count, codes, soil)
    west, east = shifted(own, "tile", 1, 2)
    top = jnp.concatenate([west[:2], own[:2], east[:2]], axis=1)
    bottom = jnp.concatenate([west[-2:], own[-2:], east[-2:]], axis=1)
    rim = jnp.concatenate([top, bottom], axis=0)
    up, down = shifted(rim, "depth", 0, 2)
    pieces = (own, west, east, up, down)
    span, width = layers + 4, columns + 4
    pairs = layers * columns * 6 * TP * TP
    extra = pl.pallas_call(
        density_kernel,
        out_shape=jax.ShapeDtypeStruct((4, layers * columns, TP), F32),
        in_specs=[sspec()] + [vspec()] * 5,
        out_specs=vspec(),
        scratch_shapes=[
            VMEM((span, width, 8, TP), F32),
            VMEM((span, width, AUG, TP), BF16),
            VMEM((layers * columns, TP), F32),
            VMEM((layers * columns, TP), F32),
        ],
        cost_estimate=cost(pairs * 12, 1 << 18, pairs),
        compiler_params=params(),
        name="density",
    )(codes, *pieces)
    owners = marker_owner.reshape((marker_count // TP, TP))
    slots = marker_slot.reshape((marker_count // TP, TP))
    tiles = marker_tile.reshape((marker_count // TP, TP))
    partial_sums = pl.pallas_call(
        marker_kernel,
        out_shape=jax.ShapeDtypeStruct((tile_devs, 8, TP), F32),
        in_specs=[vspec()] * 7,
        out_specs=vspec(),
        scratch_shapes=[VMEM((8 * TP, TP), BF16)],
        cost_estimate=cost(marker_count * TP * 25, 1 << 19, marker_count * TP),
        compiler_params=params(),
        name="markers",
    )(soil, extra, marker_pos, marker_vel, tiles, owners, slots)
    arrived = lax.all_to_all(partial_sums, "tile", 0, 0, tiled=True)
    ring_codes = jnp.concatenate(
        [
            part[:, :, 7, 0:6]
            for part in (up, jnp.concatenate([west, own, east], axis=1), down)
        ],
        axis=0,
    )
    ring_codes = jnp.transpose(ring_codes.astype(jnp.int32), (2, 0, 1))
    accel = pl.pallas_call(
        accel_kernel,
        out_shape=jax.ShapeDtypeStruct((layers, 3, columns, TP), F32),
        in_specs=[sspec()] + [vspec()] * 6,
        out_specs=vspec(),
        scratch_shapes=[
            VMEM((span, width, 8, TP), F32),
            VMEM((span, width, AUG, TP), BF16),
            VMEM((span, width, FACTORS, TP), BF16),
            VMEM((layers + 2, 16, TP), F32),
            VMEM((layers + 2, 16, TP), F32),
        ],
        cost_estimate=cost(pairs * 30, 1 << 19, pairs),
        compiler_params=params(),
        name="accel",
    )(ring_codes, *pieces, extra)
    soil_accel = jnp.transpose(accel, (0, 2, 1, 3))
    share = jnp.sum(arrived, axis=0)
    others = [
        lax.ppermute(share, "depth", [(i, (i + k) % depth_devs) for i in range(depth_devs)])
        for k in range(1, depth_devs)
    ]
    body_next, sent = pl.pallas_call(
        advance_kernel,
        out_shape=(
            jax.ShapeDtypeStruct((9, TP), F32),
            jax.ShapeDtypeStruct((tile_devs, 8, TP), F32),
        ),
        in_specs=[vspec()] * 6,
        out_specs=(vspec(), vspec()),
        compiler_params=params(),
        name="advance",
    )(share, *others, body_state, body_inertia)
    states = lax.all_to_all(sent, "tile", 0, 0, tiled=True)
    marker_vel_next = pl.pallas_call(
        pick_kernel,
        out_shape=jax.ShapeDtypeStruct((3, marker_count), F32),
        in_specs=[vspec()] * 4,
        out_specs=vspec(),
        compiler_params=params(),
        name="pick",
    )(states, marker_pos, owners, slots)
    return (soil_accel, body_next, marker_vel_next)


def solution(mesh):
    placed = (
        P("depth", "tile", None, None),
        P("depth", "tile"),
        P("depth", "tile", None),
        P(None, ("tile", "depth")),
        P(None, ("tile", "depth")),
        P(("tile", "depth")),
        P(("tile", "depth"), None),
        P(("tile", "depth")),
        P(None, "tile"),
        P(None, "tile"),
    )
    return jax.shard_map(
        local,
        mesh=mesh,
        in_specs=placed,
        out_specs=(P("depth", "tile", None, None), P(None, "tile"), P(None, ("tile", "depth"))),
        check_vma=False,
    )
```

time: 165 us -> 102 us (0.62)
  Pallas kernels: 85 us -> 41.7 us
  waiting for transfers between devices: 16.2 us -> 8.09 us
  starting transfers between devices: 30.7 us -> 24.4 us
  other arithmetic: 2.32 us -> 0.13 us
  local copies, waits for them, and re-layouts: 4.44 us -> 2.67 us
    pallas_call x4, Pallas kernels: 64.7 us -> 29.6 us  [the longest x1 19.8 us: local(): pl.pallas_call(accel_kernel, out_shape=jax.ShapeDtypeStruct((layers, 3, c...]
    ppermute x8 -> x4, waiting for transfers between devices: 12.7 us -> 4.87 us  [shifted(): return (lax.ppermute(last, axis, up), lax.ppermute(first, axis, down))]
    ppermute x8 -> x4, starting transfers between devices: 19.4 us -> 12.3 us  [shifted(): return (lax.ppermute(last, axis, up), lax.ppermute(first, axis, down))]
    pallas_call x1, Pallas kernels: 14 us -> 7.97 us  [local(): pl.pallas_call(marker_kernel, out_shape=jax.ShapeDtypeStruct((tile_devs,...]
    pallas_call x1, Pallas kernels: 6.29 us -> 4.14 us  [local(): pl.pallas_call(pick_kernel, out_shape=jax.ShapeDtypeStruct((3, marker_cou...]
    unnamed x17 -> x23, local copies, waits for them, and re-layouts: 4.42 us -> 2.43 us
  transfers between devices with their start and end apart: 12 -> 8, of which waited for: 6 -> 3; matrix products, arithmetic and copies ran while one was open for 2% -> 0% of each run, Pallas kernels for 26% -> 19%
where the time goes in v2:
time: 102 us
  Pallas kernels  41.7 us (41%)
  starting transfers between devices  24.4 us (24%)
  blocking collectives  24.1 us (24%)
  waiting for transfers between devices  8.09 us (8%)
  local copies, waits for them, and re-layouts  2.67 us (3%)
    all_to_all x1, blocking collectives, local(): arrived = lax.all_to_all(partial_sums, 'tile', 0, 0, tiled=True)  24.1 us
    pallas_call x1, Pallas kernels, local(): pl.pallas_call(accel_kernel, out_shape=jax.ShapeDtypeStruct((layers, 3, c...  19.8 us
    ppermute x4, starting transfers between devices, shifted(): return (lax.ppermute(last, axis, up), lax.ppermute(first, axis, down))  12.3 us
    pallas_call x1, Pallas kernels, local(): pl.pallas_call(density_kernel, out_shape=jax.ShapeDtypeStruct((4, layers...  8.12 us
    pallas_call x1, Pallas kernels, local(): pl.pallas_call(marker_kernel, out_shape=jax.ShapeDtypeStruct((tile_devs,...  7.97 us
    all_to_all x1, starting transfers between devices, local(): states = lax.all_to_all(sent, 'tile', 0, 0, tiled=True)  7.5 us
    ppermute x4, waiting for transfers between devices, shifted(): return (lax.ppermute(last, axis, up), lax.ppermute(first, axis, down))  4.87 us
    ppermute x3, starting transfers between devices, local(): lax.ppermute(share, 'depth', [(i, (i + k) % depth_devs) for i in range(de...  4.67 us
  transfers between devices with their start and end apart: 8, of which 3 were waited for; matrix products, arithmetic and copies ran while one was open for 0% of the time, Pallas kernels for 19%

profile of v2, /device:TPU:1, one launch (start us, length us, event | category | flops | bytes accessed | tf_op | source)
XLA Modules:
  0.0 102.0 jit_solution(2984099906110281906)
XLA Ops:
  0.6 0.7 copy-done.7
  1.3 0.9 copy-done
  2.2 0.7 copy-done.5
  2.9 0.9 prep.1.own
  3.8 4.9 %collective-permute-start = (f32[4,2,8,128]{3,2,1,0:T(8,128)S(1)}, f32[4,2,8,128]{3,2,1,0:T(8,128)S(1)}, u32[]{:S(2)}, u32[]{:S(2)}) collective-permute-start(f32[4,2,8,128]{3,2,1,0:T(8,128)S(1)} %get-tuple-element.9), channel_id=1, source_target_pairs={{0,4},{4,8},{8,12},{12,16},{16,20},{20,24},{24,28},{28,32},{32,36}... | collective-permute-start | bytes 98312 | tf_op jit(solution)/shard_map/ppermute | solution.py:518
  8.8 1.9 %collective-permute-start.1 = (f32[4,2,8,128]{3,2,1,0:T(8,128)S(1)}, f32[4,2,8,128]{3,2,1,0:T(8,128)S(1)}, u32[]{:S(2)}, u32[]{:S(2)}) collective-permute-start(f32[4,2,8,128]{3,2,1,0:T(8,128)S(1)} %get-tuple-element.10), channel_id=1, source_target_pairs={{4,0},{8,4},{12,8},{16,12},{20,16},{24,20},{28,24},{32,28},{36,32}... | collective-permute-start | bytes 98312 | tf_op jit(solution)/shard_map/ppermute | solution.py:518
  10.7 3.3 %collective-permute-done.1.east = f32[4,2,8,128]{3,2,1,0:T(8,128)S(1)} collective-permute-done((f32[4,2,8,128]{3,2,1,0:T(8,128)S(1)}, f32[4,2,8,128]{3,2,1,0:T(8,128)S(1)}, u32[]{:S(2)}, u32[]{:S(2)}) %collective-permute-start.1) | collective-permute-done | bytes 32800 | tf_op jit(solution)/shard_map/ppermute | solution.py:518
  14.0 1.3 %collective-permute-start.3 = (f32[2,12,8,128]{3,2,1,0:T(8,128)S(1)}, f32[2,12,8,128]{3,2,1,0:T(8,128)S(1)}, u32[]{:S(2)}, u32[]{:S(2)}) collective-permute-start(f32[2,12,8,128]{3,2,1,0:T(8,128)S(1)} %pad_maximum_fusion.1), channel_id=1, source_target_pairs={{1,0},{2,1},{3,2},{5,4},{6,5},{7,6},{9,8},{10,9},{11,10},{13,12},{... | collective-permute-start | bytes 294920 | tf_op jit(solution)/shard_map/ppermute | solution.py:518
  15.4 4.1 %collective-permute-start.2 = (f32[2,12,8,128]{3,2,1,0:T(8,128)S(1)}, f32[2,12,8,128]{3,2,1,0:T(8,128)S(1)}, u32[]{:S(2)}, u32[]{:S(2)}) collective-permute-start(f32[2,12,8,128]{3,2,1,0:T(8,128)S(1)} %pad_maximum_fusion), channel_id=1, source_target_pairs={{0,1},{1,2},{2,3},{4,5},{5,6},{6,7},{8,9},{9,10},{10,11},{12,13},{... | collective-permute-start | bytes 294920 | tf_op jit(solution)/shard_map/ppermute | solution.py:518
  19.5 1.6 %collective-permute-done.2.up = f32[2,12,8,128]{3,2,1,0:T(8,128)S(1)} collective-permute-done((f32[2,12,8,128]{3,2,1,0:T(8,128)S(1)}, f32[2,12,8,128]{3,2,1,0:T(8,128)S(1)}, u32[]{:S(2)}, u32[]{:S(2)}) %collective-permute-start.2) | collective-permute-done | bytes 98336 | tf_op jit(solution)/shard_map/ppermute | solution.py:518
  21.1 8.1 %density.1.extra = f32[4,32,128]{2,1,0:T(8,128)S(1)} custom-call(s32[6,4,8]{2,1,0:T(4,128)S(1)} %bitcast.18, f32[4,8,8,128]{3,2,1,0:T(8,128)S(1)} %prep.1.own, f32[4,2,8,128]{3,2,1,0:T(8,128)S(1)} %collective-permute-done.west, f32[4,2,8,128]{3,2,1,0:T(8,128)S(1)} %collective-permute-done.1.east, f32[2,12,8,128]{3,2,1,0:T(8,128)S(1)} %collective-permute-done.2.up, ...), custom_call_target="tpu_custom_call" | custom-call | flops 37748736 | bytes 262144 | tf_op jit(solution)/shard_map/density/pallas_call | solution.py:555
  29.3 8.0 %markers.1 = f32[64,8,128]{2,1,0:T(8,128)S(1)} custom-call(f32[4,6,8,128]{3,2,1,0:T(8,128)S(1)} %bitcast.12, f32[4,32,128]{2,1,0:T(8,128)S(1)} %density.1.extra, f32[3,4096]{1,0:T(4,128)S(1)} %copy-done.2, f32[3,4096]{1,0:T(4,128)S(1)} %copy-done.9, s32[32,128]{1,0:T(8,128)S(1)} %bitcast.19, s32[32,128]{1,0:T(8,128)S(1)} %bitcast.13, s32[32,128]{1,0:T(8,128)S(1)} %bitcast.15), custom_call_target="tpu_custom_call" | custom-call | flops 13107200 | bytes 524288 | tf_op jit(solution)/shard_map/markers/pallas_call | solution.py:573
  37.3 24.1 %all_to_all.10 = f32[64,8,128]{2,1,0:T(8,128)S(1)} all-to-all(f32[64,8,128]{2,1,0:T(8,128)S(1)} %markers.1), channel_id=1, replica_groups=mesh['tile'=64,'depth'=4] {'tile'}, dimensions={0} | all-to-all | bytes 524288 | tf_op jit(solution)/shard_map/all_to_all | solution.py:583
  61.4 0.1 reduce_sum.9.first
  61.4 3.9 %collective-permute-start.6 = (f32[8,128]{1,0:T(8,128)S(1)}, f32[8,128]{1,0:T(8,128)S(1)}, u32[]{:S(2)}, u32[]{:S(2)}) collective-permute-start(f32[8,128]{1,0:T(8,128)S(1)} %reduce_sum.9.first), channel_id=1, source_target_pairs={{0,3},{1,0},{2,1},{3,2},{4,7},{5,4},{6,5},{7,6},{8,11},{9,8},{10,9... | collective-permute-start | bytes 12296 | tf_op jit(solution)/shard_map/ppermute | solution.py:611
  65.4 0.7 collective-permute-start.4
  66.1 3.2 %collective-permute-done.5.third = f32[8,128]{1,0:T(8,128)S(1)} collective-permute-done((f32[8,128]{1,0:T(8,128)S(1)}, f32[8,128]{1,0:T(8,128)S(1)}, u32[]{:S(2)}, u32[]{:S(2)}) %collective-permute-start.5) | collective-permute-done | bytes 4128 | tf_op jit(solution)/shard_map/ppermute | solution.py:611
  69.3 0.7 advance.1
  70.1 7.5 %all-to-all-start.1 = ((f32[64,8,128]{2,1,0:T(8,128)}), f32[64,8,128]{2,1,0:T(8,128)S(1)}, u32[]{:S(2)}, u32[]{:S(2)}) async-start(f32[64,8,128]{2,1,0:T(8,128)} %get-tuple-element.6), calls=%async_computation.1 | async-start | bytes 524288 | tf_op jit(solution)/shard_map/all_to_all | solution.py:625
  77.6 0.1 copy.26
  77.8 0.1 copy.25
  77.9 0.1 copy.23
  78.0 19.8 %accel.1 = f32[4,3,8,128]{3,2,1,0:T(8,128)} custom-call(s32[6,8,12]{2,1,0:T(8,128)S(1)} %fusion.codes, f32[4,8,8,128]{3,2,1,0:T(8,128)S(1)} %prep.1.own, f32[4,2,8,128]{3,2,1,0:T(8,128)S(1)} %collective-permute-done.west, f32[4,2,8,128]{3,2,1,0:T(8,128)S(1)} %collective-permute-done.1.east, f32[2,12,8,128]{3,2,1,0:T(8,128)S(1)} %collective-permute-done.2.up, ...), custom_call_target="tpu_custom_call" | custom-call | flops 94371840 | bytes 524288 | tf_op jit(solution)/shard_map/accel/pallas_call | solution.py:592
  97.8 4.1 %pick.1 = f32[3,4096]{1,0:T(4,128)} custom-call(f32[64,8,128]{2,1,0:T(8,128)S(1)} %all-to-all-done.1.states, f32[3,4096]{1,0:T(4,128)S(1)} %copy-done.2, s32[32,128]{1,0:T(8,128)S(1)} %bitcast.14, s32[32,128]{1,0:T(8,128)S(1)} %bitcast.16), custom_call_target="tpu_custom_call" | custom-call | tf_op jit(solution)/shard_map/pick/pallas_call | solution.py:626
  (35 shorter events, 0.2 us)
Async XLA Ops:
  0.6 0.7 copy-start.7
  1.3 0.9 copy-start
  2.2 0.7 copy-start.5
  3.8 6.9 %collective-permute-start = (f32[4,2,8,128]{3,2,1,0:T(8,128)S(1)}, f32[4,2,8,128]{3,2,1,0:T(8,128)S(1)}, u32[]{:S(2)}, u32[]{:S(2)}) collective-permute-start(f32[4,2,8,128]{3,2,1,0:T(8,128)S(1)} %get-tuple-element.9), channel_id=1, source_target_pairs={{0,4},{4,8},{8,12},{12,16},{16,20},{20,24},{24,28},{28,32},{32,36}... | collective-permute-start | bytes 98312 | tf_op jit(solution)/shard_map/ppermute | solution.py:518
  8.8 5.2 %collective-permute-start.1 = (f32[4,2,8,128]{3,2,1,0:T(8,128)S(1)}, f32[4,2,8,128]{3,2,1,0:T(8,128)S(1)}, u32[]{:S(2)}, u32[]{:S(2)}) collective-permute-start(f32[4,2,8,128]{3,2,1,0:T(8,128)S(1)} %get-tuple-element.10), channel_id=1, source_target_pairs={{4,0},{8,4},{12,8},{16,12},{20,16},{24,20},{28,24},{32,28},{36,32}... | collective-permute-start | bytes 98312 | tf_op jit(solution)/shard_map/ppermute | solution.py:518
  14.0 5.5 %collective-permute-start.3 = (f32[2,12,8,128]{3,2,1,0:T(8,128)S(1)}, f32[2,12,8,128]{3,2,1,0:T(8,128)S(1)}, u32[]{:S(2)}, u32[]{:S(2)}) collective-permute-start(f32[2,12,8,128]{3,2,1,0:T(8,128)S(1)} %pad_maximum_fusion.1), channel_id=1, source_target_pairs={{1,0},{2,1},{3,2},{5,4},{6,5},{7,6},{9,8},{10,9},{11,10},{13,12},{... | collective-permute-start | bytes 294920 | tf_op jit(solution)/shard_map/ppermute | solution.py:518
  15.3 14.0 %copy-start.1 = (f32[4,8,6,128]{3,1,2,0:T(8,128)S(1)}, f32[4,8,6,128]{3,1,2,0:T(8,128)}, u32[]{:S(2)}) copy-start(f32[4,8,6,128]{3,1,2,0:T(8,128)} %param.10) | copy-start | bytes 294916
  15.3 13.9 %copy-start.2 = (f32[3,4096]{1,0:T(4,128)S(1)}, f32[3,4096]{1,0:T(4,128)}, u32[]{:S(2)}) copy-start(f32[3,4096]{1,0:T(4,128)} %place.3) | copy-start | bytes 147460
  15.3 13.9 %copy-start.3 = (s32[4096,1]{0,1:T(1,128)S(1)}, s32[4096,1]{0,1:T(1,128)}, u32[]{:S(2)}) copy-start(s32[4096,1]{0,1:T(1,128)} %param.16) | copy-start | bytes 49156
  15.4 13.9 %copy-start.4 = (s32[4096]{0:T(1024)S(1)}, s32[4096]{0:T(1024)}, u32[]{:S(2)}) copy-start(s32[4096]{0:T(1024)} %param.17) | copy-start | bytes 49156
  15.4 13.9 %copy-start.9 = (f32[3,4096]{1,0:T(4,128)S(1)}, f32[3,4096]{1,0:T(4,128)}, u32[]{:S(2)}) copy-start(f32[3,4096]{1,0:T(4,128)} %speed.1) | copy-start | bytes 147460
  15.4 13.9 %copy-start.10 = (s32[4096]{0:T(1024)S(1)}, s32[4096]{0:T(1024)}, u32[]{:S(2)}) copy-start(s32[4096]{0:T(1024)} %param.15) | copy-start | bytes 49156
  15.4 5.7 %collective-permute-start.2 = (f32[2,12,8,128]{3,2,1,0:T(8,128)S(1)}, f32[2,12,8,128]{3,2,1,0:T(8,128)S(1)}, u32[]{:S(2)}, u32[]{:S(2)}) collective-permute-start(f32[2,12,8,128]{3,2,1,0:T(8,128)S(1)} %pad_maximum_fusion), channel_id=1, source_target_pairs={{0,1},{1,2},{2,3},{4,5},{5,6},{6,7},{8,9},{9,10},{10,11},{12,13},{... | collective-permute-start | bytes 294920 | tf_op jit(solution)/shard_map/ppermute | solution.py:518
  61.4 8.0 %copy-start.6 = (f32[9,128]{1,0:T(8,128)S(1)}, f32[9,128]{1,0:T(8,128)}, u32[]{:S(2)}) copy-start(f32[9,128]{1,0:T(8,128)} %state.1) | copy-start | bytes 13828
  61.4 8.0 %copy-start.8 = (f32[4,128]{1,0:T(4,128)S(1)}, f32[4,128]{1,0:T(4,128)}, u32[]{:S(2)}) copy-start(f32[4,128]{1,0:T(4,128)} %inertia.1) | copy-start | bytes 6148
  61.4 4.7 %collective-permute-start.6 = (f32[8,128]{1,0:T(8,128)S(1)}, f32[8,128]{1,0:T(8,128)S(1)}, u32[]{:S(2)}, u32[]{:S(2)}) collective-permute-start(f32[8,128]{1,0:T(8,128)S(1)} %reduce_sum.9.first), channel_id=1, source_target_pairs={{0,3},{1,0},{2,1},{3,2},{4,7},{5,4},{6,5},{7,6},{8,11},{9,8},{10,9... | collective-permute-start | bytes 12296 | tf_op jit(solution)/shard_map/ppermute | solution.py:611
  65.4 4.0 %collective-permute-start.5 = (f32[8,128]{1,0:T(8,128)S(1)}, f32[8,128]{1,0:T(8,128)S(1)}, u32[]{:S(2)}, u32[]{:S(2)}) collective-permute-start(f32[8,128]{1,0:T(8,128)S(1)} %reduce_sum.9.first), channel_id=1, source_target_pairs={{0,2},{1,3},{2,0},{3,1},{4,6},{5,7},{6,4},{7,5},{8,10},{9,11},{10,... | collective-permute-start | bytes 12296 | tf_op jit(solution)/shard_map/ppermute | solution.py:611
  65.4 3.9 %collective-permute-start.4 = (f32[8,128]{1,0:T(8,128)S(1)}, f32[8,128]{1,0:T(8,128)S(1)}, u32[]{:S(2)}, u32[]{:S(2)}) collective-permute-start(f32[8,128]{1,0:T(8,128)S(1)} %reduce_sum.9.first), channel_id=1, source_target_pairs={{0,1},{1,2},{2,3},{3,0},{4,5},{5,6},{6,7},{7,4},{8,9},{9,10},{10,1... | collective-permute-start | bytes 12296 | tf_op jit(solution)/shard_map/ppermute | solution.py:611
  70.1 27.7 %all-to-all-start.1 = ((f32[64,8,128]{2,1,0:T(8,128)}), f32[64,8,128]{2,1,0:T(8,128)S(1)}, u32[]{:S(2)}, u32[]{:S(2)}) async-start(f32[64,8,128]{2,1,0:T(8,128)} %get-tuple-element.6), calls=%async_computation.1 | async-start | bytes 524288 | tf_op jit(solution)/shard_map/all_to_all | solution.py:625

commit v3 on v2

--- a/solution.py
+++ b/solution.py
@@ -18,9 +18,11 @@
 ROWS = 16
 AUG = 48
 FACTORS = 80
+TILES = 4
 SCALE = (2.0 * 1.4426950408889634) ** 0.5
 FAR = 1e30
 PLACE_LIMIT = 4.0
+CLIP = 1e4
 SPEED_LIMIT = 256.0
 F32 = jnp.float32
 BF16 = jnp.bfloat16
@@ -201,7 +203,16 @@
     return jnp.transpose(augmented(ext[row, col], False)).astype(BF16)
 
 
-def prep_kernel(counts, codes, soil, out):
+def prep_kernel(counts_in, codes_in, soil_in, out, counts, codes, soil, sems):
+    copies = [
+        pltpu.make_async_copy(counts_in, counts, sems.at[0]),
+        pltpu.make_async_copy(codes_in, codes, sems.at[1]),
+        pltpu.make_async_copy(soil_in, soil, sems.at[2]),
+    ]
+    for copy in copies:
+        copy.start()
+    for copy in copies:
+        copy.wait()
     layers, columns = out.shape[0], out.shape[1]
     lane = lax.broadcasted_iota(jnp.int32, (1, TP), 1)
     for layer in range(layers):
@@ -224,16 +235,16 @@
     def _():
         fill_sources(ext, btab, 1, layers + 3, 1, columns + 3)
 
-        def step(pair, carry):
-            for half in range(2):
-                tile = pair * 2 + half
+        def step(group, carry):
+            for part in range(TILES):
+                tile = group * TILES + part
                 layer, column = tile // columns, tile % columns
                 places = near(codes, layer, column, layer + 2, column + 2)
                 left = left_of(ext, layer + 2, column + 2)
                 sums[pl.ds(tile, 1), :] = fast_sum(left, btab, places, eye)
             return carry
 
-        lax.fori_loop(0, layers * columns // 2, step, 0)
+        lax.fori_loop(0, layers * columns // TILES, step, 0)
 
     @pl.when(jnp.logical_not(fast))
     def _():
@@ -257,8 +268,8 @@
     out[3] = damp * live
 
 
-def accel_kernel(
-    codes, own, west, east, up, down, extra, out, ext, btab, ftab, press_ref, damp_ref
+def ring_kernel(
+    codes, own, west, east, up, down, extra, ext, btab, ftab, press_ref, damp_ref
 ):
     layers, columns = own.shape[0], own.shape[1]
     assemble(own, west, east, up, down, ext)
@@ -312,12 +323,28 @@
 
         lax.fori_loop(0, (layers + 2) * (columns + 2), factors, 0, unroll=2)
 
+    @pl.when(jnp.logical_not(fast))
+    def _():
+        def ring_sum(row, col):
+            places = near(codes, row, col, row, col)
+            keep(row, col, slow_sum(ext, row, col, places, eye))
+
+        ring(ring_sum)
+
+
+def accel_kernel(codes, ext, btab, ftab, press_ref, damp_ref, out):
+    layers, columns = out.shape[0], out.shape[2]
+    eye = eye_mask()
+    fast = moderate(ext)
+
+    @pl.when(fast)
+    def _():
         def step(pair, carry):
             for half in range(2):
                 tile = pair * 2 + half
                 layer, column = tile // columns, tile % columns
                 row, col = layer + 2, column + 2
-                places = near(codes, row, col, row, col)
+                places = near(codes, layer, column, row, col)
                 weights = fast_weights(left_of(ext, row, col), btab, places)
                 highs = [w.astype(BF16) for w in weights]
                 lows = [(w - h.astype(F32)).astype(BF16) for w, h in zip(weights, highs)]
@@ -343,16 +370,10 @@
 
     @pl.when(jnp.logical_not(fast))
     def _():
-        def ring_sum(row, col):
-            places = near(codes, row, col, row, col)
-            keep(row, col, slow_sum(ext, row, col, places, eye))
-
-        ring(ring_sum)
-
         def step(tile, carry):
             layer, column = tile // columns, tile % columns
             row, col = layer + 2, column + 2
-            places = near(codes, row, col, row, col)
+            places = near(codes, layer, column, row, col)
             rows = slow_accel(ext, press_ref, damp_ref, row, col, places, eye)
             scale = ext[row, col, 6:7, :] * (1.0 / TP)
             for c in range(3):
@@ -368,15 +389,19 @@
     pairs = place.shape[1] // (2 * TP)
     owner_count = out.shape[0]
     groups = TP // 16
-    for field in range(8):
-        if field < 6:
-            part = jnp.concatenate([soil[layer, field] for layer in range(layers)], axis=0)
-        else:
-            part = extra[field - 4]
-        pieces = list(split3(part)) + [jnp.zeros((TP - 3 * count, TP), F32)]
+    field_of = lambda f: jnp.concatenate([soil[layer, f] for layer in range(layers)], axis=0)
+    spots = [field_of(c) for c in range(3)]
+    moves = [field_of(3 + c) for c in range(3)]
+    press, damp = extra[2], extra[3]
+    scaled = [jnp.clip(spot, -CLIP, CLIP) * SCALE for spot in spots]
+    norm = -0.5 * (scaled[0] * scaled[0] + scaled[1] * scaled[1] + scaled[2] * scaled[2])
+    fields = scaled + [norm, press, damp]
+    fields = fields + [damp * moves[c] - press * spots[c] for c in range(3)]
+    for number, field in enumerate(fields):
+        pieces = list(split3(field)) + [jnp.zeros((TP - 3 * count, TP), F32)]
         turned = jnp.transpose(jnp.concatenate(pieces, axis=0)).astype(BF16)
         for group in range(groups):
-            at = group * TP + field * 16
+            at = (group * 9 + number) * 16
             table[at : at + 16, :] = turned[group * 16 : group * 16 + 16]
     entry = lax.broadcasted_iota(jnp.int32, (TP, TP), 0)
     listed = jnp.where(entry < 3 * count, lax.rem(entry, count), -1)
@@ -386,8 +411,9 @@
         left, right = [], []
         for part in range(2):
             block = pair * 2 + part
-            high = terms[part].astype(BF16).astype(F32)
-            low = terms[part] - high
+            value = terms[:, part * TP : (part + 1) * TP]
+            high = value.astype(BF16).astype(F32)
+            low = value - high
             owner = jnp.broadcast_to(owners[pl.ds(block, 1), :], (8, TP))
             slot = jnp.broadcast_to(slots[pl.ds(block, 1), :], (TP, TP))
             hot = jnp.where(slot == entry, 1.0, 0.0).astype(BF16)
@@ -407,47 +433,47 @@
         )
         out[...] = out[...] + summed.reshape(out.shape)
 
-    def forces_on(block):
-        lanes = pl.ds(pl.multiple_of(block * TP, TP), TP)
-        which = jnp.broadcast_to(tiles[pl.ds(block, 1), :], (TP, TP))
-        hot = jnp.where(which == listed, 1.0, 0.0).astype(BF16)
+    def forces_on(pair):
+        wide = 2 * TP
+        lanes = pl.ds(pl.multiple_of(pair * wide, wide), wide)
+        hots = []
+        for part in range(2):
+            which = jnp.broadcast_to(tiles[pl.ds(pair * 2 + part, 1), :], (TP, TP))
+            hots.append(jnp.where(which == listed, 1.0, 0.0).astype(BF16))
+        hot = jnp.concatenate(hots, axis=1)
         y = place[:, lanes]
         u = speed[:, lanes]
-        at = [jnp.broadcast_to(y[c : c + 1], (16, TP)) for c in range(3)]
-        total = [jnp.zeros((16, TP), F32) for c in range(3)]
-        drag = jnp.zeros((16, TP), F32)
+        spread = y * SCALE
+        at = [jnp.broadcast_to(spread[c : c + 1], (16, wide)) for c in range(3)]
+        totals = [jnp.zeros((16, wide), F32) for number in range(5)]
         for group in range(groups):
             picked = lax.dot_general(
-                table[group * TP : (group + 1) * TP, :],
+                table[group * 144 : (group + 1) * 144, :],
                 hot,
                 (((1,), (0,)), ((), ())),
                 preferred_element_type=F32,
             )
-            fields = [picked[16 * field : 16 * field + 16] for field in range(8)]
-            offsets = [at[c] - fields[c] for c in range(3)]
-            distance = offsets[0] * offsets[0] + offsets[1] * offsets[1]
-            distance = distance + offsets[2] * offsets[2]
-            weight = jnp.exp2(distance * (-0.5 * SCALE * SCALE))
-            press = weight * fields[6]
-            damp = weight * fields[7]
-            drag = drag + damp
-            for c in range(3):
-                total[c] = total[c] + (press * offsets[c] + damp * fields[3 + c])
-        slowed = jnp.sum(drag, axis=0, keepdims=True)
+            got = [picked[16 * number : 16 * number + 16] for number in range(9)]
+            power = (got[3] + at[0] * got[0]) + (at[1] * got[1] + at[2] * got[2])
+            weight = jnp.exp2(power)
+            for number in range(5):
+                totals[number] = totals[number] + weight * got[4 + number]
+        sums = [jnp.sum(total, axis=0, keepdims=True) for total in totals]
+        square = spread * spread
+        scale = jnp.exp2(-0.5 * (square[0:1] + square[1:2] + square[2:3])) * (1.0 / TP)
+        where = [y[c : c + 1] for c in range(3)]
         force = [
-            (jnp.sum(total[c], axis=0, keepdims=True) - u[c : c + 1] * slowed) * (1.0 / TP)
+            (where[c] * sums[0] + (sums[2 + c] - u[c : c + 1] * sums[1])) * scale
             for c in range(3)
         ]
-        where = [y[c : c + 1] for c in range(3)]
         moment = cross(where, force)
-        return jnp.concatenate(force + moment + [jnp.zeros((2, TP), F32)], axis=0)
+        return jnp.concatenate(force + moment + [jnp.zeros((2, wide), F32)], axis=0)
 
     def step(pair, terms):
         add_terms(jnp.maximum(pair - 1, 0), terms)
-        return (forces_on(pair * 2), forces_on(pair * 2 + 1))
-
-    blank = jnp.zeros((8, TP), F32)
-    terms = lax.fori_loop(0, pairs, step, (blank, blank))
+        return forces_on(pair)
+
+    terms = lax.fori_loop(0, pairs, step, jnp.zeros((8, 2 * TP), F32))
     add_terms(pairs - 1, terms)
 
 
@@ -485,20 +511,20 @@
 
 
 def pick_kernel(states, place, owners, slots, out):
-    pairs = place.shape[1] // (2 * TP)
+    steps = place.shape[1] // (4 * TP)
     owner_count = states.shape[0]
 
-    def step(pair, carry):
-        for half in range(2):
-            block = pair * 2 + half
+    def step(quad, carry):
+        for part in range(4):
+            block = quad * 4 + part
             lanes = pl.ds(pl.multiple_of(block * TP, TP), TP)
             slot = jnp.broadcast_to(slots[pl.ds(block, 1), :], (8, TP))
             owner = jnp.broadcast_to(owners[pl.ds(block, 1), :], (8, TP))
-            found = [jnp.zeros((8, TP), F32) for lane in range(4)]
+            found = [jnp.zeros((8, TP), F32) for lane in range(2)]
             for o in range(owner_count):
                 here = jnp.take_along_axis(states[o], slot, axis=1)
-                found[o % 4] = jnp.where(owner == o, here, found[o % 4])
-            picked = (found[0] + found[1]) + (found[2] + found[3])
+                found[o % 2] = jnp.where(owner == o, here, found[o % 2])
+            picked = found[0] + found[1]
             y = place[:, lanes]
             turn = cross(
                 [picked[3 + c : 4 + c] for c in range(3)], [y[c : c + 1] for c in range(3)]
@@ -506,7 +532,7 @@
             out[:, lanes] = picked[0:3] + jnp.concatenate(turn, axis=0)
         return carry
 
-    lax.fori_loop(0, pairs, step, 0)
+    lax.fori_loop(0, steps, step, 0)
 
 
 def shifted(shard, axis, dim, width):
@@ -539,8 +565,14 @@
     own = pl.pallas_call(
         prep_kernel,
         out_shape=jax.ShapeDtypeStruct((layers, columns, 8, TP), F32),
-        in_specs=[sspec(), sspec(), vspec()],
+        in_specs=[pl.BlockSpec(memory_space=pltpu.HBM)] * 3,
         out_specs=vspec(),
+        scratch_shapes=[
+            SMEM((layers, columns), jnp.int32),
+            SMEM((6, layers, columns), jnp.int32),
+            VMEM((layers, fields, columns, TP), F32),
+            pltpu.SemaphoreType.DMA((3,)),
+        ],
         compiler_params=params(),
         name="prep",
     )(tile_count, codes, soil)
@@ -575,12 +607,15 @@
         out_shape=jax.ShapeDtypeStruct((tile_devs, 8, TP), F32),
         in_specs=[vspec()] * 7,
         out_specs=vspec(),
-        scratch_shapes=[VMEM((8 * TP, TP), BF16)],
+        scratch_shapes=[VMEM((9 * TP, TP), BF16)],
         cost_estimate=cost(marker_count * TP * 25, 1 << 19, marker_count * TP),
         compiler_params=params(),
         name="markers",
     )(soil, extra, marker_pos, marker_vel, tiles, owners, slots)
+    partial_sums, later = lax.optimization_barrier((partial_sums, (pieces, extra)))
     arrived = lax.all_to_all(partial_sums, "tile", 0, 0, tiled=True)
+    pieces, extra = later
+    own, west, east, up, down = pieces
     ring_codes = jnp.concatenate(
         [
             part[:, :, 7, 0:6]
@@ -589,23 +624,23 @@
         axis=0,
     )
     ring_codes = jnp.transpose(ring_codes.astype(jnp.int32), (2, 0, 1))
-    accel = pl.pallas_call(
-        accel_kernel,
-        out_shape=jax.ShapeDtypeStruct((layers, 3, columns, TP), F32),
+    shapes = (
+        jax.ShapeDtypeStruct((span, width, 8, TP), F32),
+        jax.ShapeDtypeStruct((span, width, AUG, TP), BF16),
+        jax.ShapeDtypeStruct((span, width, FACTORS, TP), BF16),
+        jax.ShapeDtypeStruct((layers + 2, 16, TP), F32),
+        jax.ShapeDtypeStruct((layers + 2, 16, TP), F32),
+    )
+    tables = pl.pallas_call(
+        ring_kernel,
+        out_shape=shapes,
         in_specs=[sspec()] + [vspec()] * 6,
-        out_specs=vspec(),
-        scratch_shapes=[
-            VMEM((span, width, 8, TP), F32),
-            VMEM((span, width, AUG, TP), BF16),
-            VMEM((span, width, FACTORS, TP), BF16),
-            VMEM((layers + 2, 16, TP), F32),
-            VMEM((layers + 2, 16, TP), F32),
-        ],
-        cost_estimate=cost(pairs * 30, 1 << 19, pairs),
+        out_specs=(vspec(),) * 5,
+        cost_estimate=cost(pairs * 15, 1 << 19, pairs),
         compiler_params=params(),
-        name="accel",
+        name="ring",
     )(ring_codes, *pieces, extra)
-    soil_accel = jnp.transpose(accel, (0, 2, 1, 3))
+    arrived, tables = lax.optimization_barrier((arrived, tables))
     share = jnp.sum(arrived, axis=0)
     others = [
         lax.ppermute(share, "depth", [(i, (i + k) % depth_devs) for i in range(depth_devs)])
@@ -622,7 +657,19 @@
         compiler_params=params(),
         name="advance",
     )(share, *others, body_state, body_inertia)
+    sent, tables = lax.optimization_barrier((sent, tables))
     states = lax.all_to_all(sent, "tile", 0, 0, tiled=True)
+    accel = pl.pallas_call(
+        accel_kernel,
+        out_shape=jax.ShapeDtypeStruct((layers, 3, columns, TP), F32),
+        in_specs=[sspec()] + [vspec()] * 5,
+        out_specs=vspec(),
+        cost_estimate=cost(pairs * 15, 1 << 19, pairs),
+        compiler_params=params(),
+        name="accel",
+    )(codes, *tables)
+    states, accel = lax.optimization_barrier((states, accel))
+    soil_accel = jnp.transpose(accel, (0, 2, 1, 3))
     marker_vel_next = pl.pallas_call(
         pick_kernel,
         out_shape=jax.ShapeDtypeStruct((3, marker_count), F32),

time: 102 us -> 97.3 us (0.954)
  blocking collectives: 24.1 us -> 0 us
  starting transfers between devices: 24.4 us -> 39.6 us
  waiting for transfers between devices: 8.09 us -> 10.6 us
  local copies, waits for them, and re-layouts: 2.67 us -> 4.99 us
  Pallas kernels: 41.7 us -> 40.6 us
    all_to_all x1 -> x0, blocking collectives: 24.1 us -> none  [local(): arrived = lax.all_to_all(partial_sums, 'tile', 0, 0, tiled=True)]
    all_to_all x0 -> x1, starting transfers between devices: none -> 14.3 us  [local(): arrived = lax.all_to_all(partial_sums, 'tile', 0, 0, tiled=True)]
    pallas_call x0 -> x1, Pallas kernels: none -> 9 us  [local(): pl.pallas_call(ring_kernel, out_shape=shapes, in_specs=[sspec()] + [vspec...]
    pallas_call x1, Pallas kernels: 19.8 us -> 11.8 us  [local(): pl.pallas_call(accel_kernel, out_shape=jax.ShapeDtypeStruct((layers, 3, c...]
    all_to_all x1, starting transfers between devices: 7.5 us -> 10.5 us  [local(): states = lax.all_to_all(sent, 'tile', 0, 0, tiled=True)]
    pallas_call x1, Pallas kernels: 8.12 us -> 5.76 us  [local(): pl.pallas_call(density_kernel, out_shape=jax.ShapeDtypeStruct((4, layers...]
    unnamed x23 -> x29, local copies, waits for them, and re-layouts: 2.43 us -> 4.75 us
    all_to_all x0 -> x1, waiting for transfers between devices: none -> 1.48 us  [local(): arrived = lax.all_to_all(partial_sums, 'tile', 0, 0, tiled=True)]
  transfers between devices with their start and end apart: 8 -> 9, of which waited for: 3 -> 6; matrix products, arithmetic and copies ran while one was open for 0% -> 0% of each run, Pallas kernels for 19% -> 21%
where the time goes in v3:
time: 97.3 us; the launch traced here: 96.8 us
  Pallas kernels  40.6 us (42%)
  starting transfers between devices  39.6 us (41%)
  waiting for transfers between devices  10.6 us (11%)
  local copies, waits for them, and re-layouts  4.99 us (5%)
    all_to_all x1, starting transfers between devices, local(): arrived = lax.all_to_all(partial_sums, 'tile', 0, 0, tiled=True)  14.3 us
    pallas_call x1, Pallas kernels, local(): pl.pallas_call(accel_kernel, out_shape=jax.ShapeDtypeStruct((layers, 3, c...  11.8 us
    ppermute x4, starting transfers between devices, shifted(): return (lax.ppermute(last, axis, up), lax.ppermute(first, axis, down))  11.3 us
    all_to_all x1, starting transfers between devices, local(): states = lax.all_to_all(sent, 'tile', 0, 0, tiled=True)  10.5 us
    pallas_call x1, Pallas kernels, local(): pl.pallas_call(ring_kernel, out_shape=shapes, in_specs=[sspec()] + [vspec...  9 us
    pallas_call x1, Pallas kernels, local(): pl.pallas_call(marker_kernel, out_shape=jax.ShapeDtypeStruct((tile_devs,...  8.88 us
    ppermute x4, waiting for transfers between devices, shifted(): return (lax.ppermute(last, axis, up), lax.ppermute(first, axis, down))  5.8 us
    pallas_call x1, Pallas kernels, local(): pl.pallas_call(density_kernel, out_shape=jax.ShapeDtypeStruct((4, layers...  5.76 us
  transfers between devices with their start and end apart: 9, of which 6 were waited for; matrix products, arithmetic and copies ran while one was open for 0% of the time, Pallas kernels for 21%

profile of v3, /device:TPU:1, one launch (start us, length us, event | category | flops | bytes accessed | tf_op | source)
XLA Modules:
  0.0 96.8 jit_solution(1505468366351167980)
XLA Ops:
  0.6 0.9 copy-done
  1.5 0.7 copy-done.5
  2.9 0.9 prep.1.own
  3.8 5.1 %collective-permute-start.1 = (f32[4,2,8,128]{3,2,1,0:T(8,128)S(1)}, f32[4,2,8,128]{3,2,1,0:T(8,128)S(1)}, u32[]{:S(2)}, u32[]{:S(2)}) collective-permute-start(f32[4,2,8,128]{3,2,1,0:T(8,128)S(1)} %get-tuple-element.61), channel_id=1, source_target_pairs={{4,0},{8,4},{12,8},{16,12},{20,16},{24,20},{28,24},{32,28},{36,32}... | collective-permute-start | bytes 98312 | tf_op jit(solution)/shard_map/ppermute | solution.py:544
  9.0 1.9 %collective-permute-start = (f32[4,2,8,128]{3,2,1,0:T(8,128)S(1)}, f32[4,2,8,128]{3,2,1,0:T(8,128)S(1)}, u32[]{:S(2)}, u32[]{:S(2)}) collective-permute-start(f32[4,2,8,128]{3,2,1,0:T(8,128)S(1)} %get-tuple-element.62), channel_id=1, source_target_pairs={{0,4},{4,8},{8,12},{12,16},{16,20},{20,24},{24,28},{28,32},{32,36}... | collective-permute-start | bytes 98312 | tf_op jit(solution)/shard_map/ppermute | solution.py:544
  10.9 1.1 %collective-permute-done.west = f32[4,2,8,128]{3,2,1,0:T(8,128)S(1)} collective-permute-done((f32[4,2,8,128]{3,2,1,0:T(8,128)S(1)}, f32[4,2,8,128]{3,2,1,0:T(8,128)S(1)}, u32[]{:S(2)}, u32[]{:S(2)}) %collective-permute-start) | collective-permute-done | bytes 32800 | tf_op jit(solution)/shard_map/ppermute | solution.py:544
  12.1 2.8 %collective-permute-start.2 = (f32[2,12,8,128]{3,2,1,0:T(8,128)S(1)}, f32[2,12,8,128]{3,2,1,0:T(8,128)S(1)}, u32[]{:S(2)}, u32[]{:S(2)}) collective-permute-start(f32[2,12,8,128]{3,2,1,0:T(8,128)S(1)} %pad_maximum_fusion), channel_id=1, source_target_pairs={{0,1},{1,2},{2,3},{4,5},{5,6},{6,7},{8,9},{9,10},{10,11},{12,13},{... | collective-permute-start | bytes 294920 | tf_op jit(solution)/shard_map/ppermute | solution.py:544
  15.0 1.4 %collective-permute-start.3 = (f32[2,12,8,128]{3,2,1,0:T(8,128)S(1)}, f32[2,12,8,128]{3,2,1,0:T(8,128)S(1)}, u32[]{:S(2)}, u32[]{:S(2)}) collective-permute-start(f32[2,12,8,128]{3,2,1,0:T(8,128)S(1)} %pad_maximum_fusion.1), channel_id=1, source_target_pairs={{1,0},{2,1},{3,2},{5,4},{6,5},{7,6},{9,8},{10,9},{11,10},{13,12},{... | collective-permute-start | bytes 294920 | tf_op jit(solution)/shard_map/ppermute | solution.py:544
  16.8 4.3 %collective-permute-done.3.down = f32[2,12,8,128]{3,2,1,0:T(8,128)S(1)} collective-permute-done((f32[2,12,8,128]{3,2,1,0:T(8,128)S(1)}, f32[2,12,8,128]{3,2,1,0:T(8,128)S(1)}, u32[]{:S(2)}, u32[]{:S(2)}) %collective-permute-start.3) | collective-permute-done | bytes 98336 | tf_op jit(solution)/shard_map/ppermute | solution.py:544
  21.1 5.8 %density.1.extra = f32[4,32,128]{2,1,0:T(8,128)S(1)} custom-call(s32[6,4,8]{2,1,0:T(4,128)S(1)} %bitcast.18, f32[4,8,8,128]{3,2,1,0:T(8,128)S(1)} %prep.1.own, f32[4,2,8,128]{3,2,1,0:T(8,128)S(1)} %collective-permute-done.west, f32[4,2,8,128]{3,2,1,0:T(8,128)S(1)} %collective-permute-done.1.east, f32[2,12,8,128]{3,2,1,0:T(8,128)S(1)} %collective-permute-done.2.up, ...), custom_call_target="tpu_custom_call" | custom-call | flops 37748736 | bytes 262144 | tf_op jit(solution)/shard_map/density/pallas_call | solution.py:587
  27.0 8.9 %markers.1 = f32[64,8,128]{2,1,0:T(8,128)} custom-call(f32[4,6,8,128]{3,2,1,0:T(8,128)S(1)} %bitcast.12, f32[4,32,128]{2,1,0:T(8,128)S(1)} %density.1.extra, f32[3,4096]{1,0:T(4,128)S(1)} %copy-done.2, f32[3,4096]{1,0:T(4,128)S(1)} %copy-done.10, s32[32,128]{1,0:T(8,128)S(1)} %bitcast.20, s32[32,128]{1,0:T(8,128)S(1)} %bitcast.13, s32[32,128]{1,0:T(8,128)S(1)} %bitcast.15), custom_call_target="tpu_custom_call" | custom-call | flops 13107200 | bytes 524288 | tf_op jit(solution)/shard_map/markers/pallas_call | solution.py:605
  35.8 14.3 %all-to-all-start = ((f32[64,8,128]{2,1,0:T(8,128)}), f32[64,8,128]{2,1,0:T(8,128)S(1)}, u32[]{:S(2)}, u32[]{:S(2)}) async-start(f32[64,8,128]{2,1,0:T(8,128)} %markers.1), calls=%async_computation | async-start | bytes 524288 | tf_op jit(solution)/shard_map/all_to_all | solution.py:616
  50.6 9.0 %ring.1 = (f32[8,12,8,128]{3,2,1,0:T(8,128)S(1)}, bf16[8,12,48,128]{3,2,1,0:T(8,128)(2,1)S(1)}, bf16[8,12,80,128]{3,2,1,0:T(8,128)(2,1)S(1)}, f32[6,16,128]{2,1,0:T(8,128)S(1)}, f32[6,16,128]{2,1,0:T(8,128)S(1)}) custom-call(s32[6,8,12]{2,1,0:T(8,128)S(1)} %fusion.codes, f32[4,8,8,128]{3,2,1,0:T(8,128)S(1)} %prep.1.own, ...), custom_call_target="tpu_custom_call" | custom-call | flops 47185920 | bytes 524288 | tf_op jit(solution)/shard_map/ring/pallas_call | solution.py:634
  59.6 1.0 %copy-done.12 = bf16[8,12,48,128]{3,2,1,0:T(8,128)(2,1)} copy-done((bf16[8,12,48,128]{3,2,1,0:T(8,128)(2,1)}, bf16[8,12,48,128]{3,2,1,0:T(8,128)(2,1)S(1)}, u32[]{:S(2)}) %copy-start.12) | copy-done | bytes 1179672
  60.6 1.5 %all-to-all-done = f32[64,8,128]{2,1,0:T(8,128)S(1)} async-done(((f32[64,8,128]{2,1,0:T(8,128)}), f32[64,8,128]{2,1,0:T(8,128)S(1)}, u32[]{:S(2)}, u32[]{:S(2)}) %all-to-all-start) | async-done | bytes 262176 | tf_op jit(solution)/shard_map/all_to_all | solution.py:616
  62.2 0.9 collective-permute-start.6
  63.1 2.3 %collective-permute-start.5 = (f32[8,128]{1,0:T(8,128)S(1)}, f32[8,128]{1,0:T(8,128)S(1)}, u32[]{:S(2)}, u32[]{:S(2)}) collective-permute-start(f32[8,128]{1,0:T(8,128)S(1)} %reduce_sum.9.first), channel_id=1, source_target_pairs={{0,2},{1,3},{2,0},{3,1},{4,6},{5,7},{6,4},{7,5},{8,10},{9,11},{10,... | collective-permute-start | bytes 12296 | tf_op jit(solution)/shard_map/ppermute | solution.py:646
  65.8 1.3 %collective-permute-done.5.third = f32[8,128]{1,0:T(8,128)S(1)} collective-permute-done((f32[8,128]{1,0:T(8,128)S(1)}, f32[8,128]{1,0:T(8,128)S(1)}, u32[]{:S(2)}, u32[]{:S(2)}) %collective-permute-start.5) | collective-permute-done | bytes 4128 | tf_op jit(solution)/shard_map/ppermute | solution.py:646
  67.0 2.0 %collective-permute-done.4.second = f32[8,128]{1,0:T(8,128)S(1)} collective-permute-done((f32[8,128]{1,0:T(8,128)S(1)}, f32[8,128]{1,0:T(8,128)S(1)}, u32[]{:S(2)}, u32[]{:S(2)}) %collective-permute-start.4) | collective-permute-done | bytes 4128 | tf_op jit(solution)/shard_map/ppermute | solution.py:646
  69.0 0.7 advance.1
  69.8 10.5 %all-to-all-start.1 = ((f32[64,8,128]{2,1,0:T(8,128)}), f32[64,8,128]{2,1,0:T(8,128)S(1)}, u32[]{:S(2)}, u32[]{:S(2)}) async-start(f32[64,8,128]{2,1,0:T(8,128)} %get-tuple-element.50), calls=%async_computation.1 | async-start | bytes 524288 | tf_op jit(solution)/shard_map/all_to_all | solution.py:661
  80.3 1.3 %copy-done.13 = bf16[8,12,48,128]{3,2,1,0:T(8,128)(2,1)S(1)} copy-done((bf16[8,12,48,128]{3,2,1,0:T(8,128)(2,1)S(1)}, bf16[8,12,48,128]{3,2,1,0:T(8,128)(2,1)}, u32[]{:S(2)}) %copy-start.13) | copy-done | bytes 1179672
  81.5 11.8 %accel.1 = f32[4,3,8,128]{3,2,1,0:T(8,128)} custom-call(s32[6,4,8]{2,1,0:T(4,128)S(1)} %bitcast.19, f32[8,12,8,128]{3,2,1,0:T(8,128)S(1)} %get-tuple-element.51.ext, bf16[8,12,48,128]{3,2,1,0:T(8,128)(2,1)S(1)} %copy-done.13, bf16[8,12,80,128]{3,2,1,0:T(8,128)(2,1)S(1)} %get-tuple-element.53.ftab, f32[6,16,128]{2,1,0:T(8,128)S(1)} %get-tuple-element.54.press_ref, ...), custom_call_target="tpu_custom_call" | custom-call | flops 47185920 | bytes 524288 | tf_op jit(solution)/shard_map/accel/pallas_call | solution.py:662
  93.3 3.5 %pick.1 = f32[3,4096]{1,0:T(4,128)} custom-call(f32[64,8,128]{2,1,0:T(8,128)S(1)} %all-to-all-done.1.states, f32[3,4096]{1,0:T(4,128)S(1)} %copy-done.2, s32[32,128]{1,0:T(8,128)S(1)} %bitcast.14, s32[32,128]{1,0:T(8,128)S(1)} %bitcast.16), custom_call_target="tpu_custom_call" | custom-call | tf_op jit(solution)/shard_map/pick/pallas_call | solution.py:673
  (43 shorter events, 2.0 us)
Async XLA Ops:
  0.6 0.9 copy-start
  1.5 0.7 copy-start.5
  2.2 0.7 copy-start.8
  3.8 7.1 %collective-permute-start.1 = (f32[4,2,8,128]{3,2,1,0:T(8,128)S(1)}, f32[4,2,8,128]{3,2,1,0:T(8,128)S(1)}, u32[]{:S(2)}, u32[]{:S(2)}) collective-permute-start(f32[4,2,8,128]{3,2,1,0:T(8,128)S(1)} %get-tuple-element.61), channel_id=1, source_target_pairs={{4,0},{8,4},{12,8},{16,12},{20,16},{24,20},{28,24},{32,28},{36,32}... | collective-permute-start | bytes 98312 | tf_op jit(solution)/shard_map/ppermute | solution.py:544
  9.0 3.1 %collective-permute-start = (f32[4,2,8,128]{3,2,1,0:T(8,128)S(1)}, f32[4,2,8,128]{3,2,1,0:T(8,128)S(1)}, u32[]{:S(2)}, u32[]{:S(2)}) collective-permute-start(f32[4,2,8,128]{3,2,1,0:T(8,128)S(1)} %get-tuple-element.62), channel_id=1, source_target_pairs={{0,4},{4,8},{8,12},{12,16},{16,20},{20,24},{24,28},{28,32},{32,36}... | collective-permute-start | bytes 98312 | tf_op jit(solution)/shard_map/ppermute | solution.py:544
  12.1 4.7 %collective-permute-start.2 = (f32[2,12,8,128]{3,2,1,0:T(8,128)S(1)}, f32[2,12,8,128]{3,2,1,0:T(8,128)S(1)}, u32[]{:S(2)}, u32[]{:S(2)}) collective-permute-start(f32[2,12,8,128]{3,2,1,0:T(8,128)S(1)} %pad_maximum_fusion), channel_id=1, source_target_pairs={{0,1},{1,2},{2,3},{4,5},{5,6},{6,7},{8,9},{9,10},{10,11},{12,13},{... | collective-permute-start | bytes 294920 | tf_op jit(solution)/shard_map/ppermute | solution.py:544
  15.0 11.9 %copy-start.1 = (f32[4,8,6,128]{3,1,2,0:T(8,128)S(1)}, f32[4,8,6,128]{3,1,2,0:T(8,128)}, u32[]{:S(2)}) copy-start(f32[4,8,6,128]{3,1,2,0:T(8,128)} %param.10) | copy-start | bytes 294916
  15.0 11.9 %copy-start.2 = (f32[3,4096]{1,0:T(4,128)S(1)}, f32[3,4096]{1,0:T(4,128)}, u32[]{:S(2)}) copy-start(f32[3,4096]{1,0:T(4,128)} %place.3) | copy-start | bytes 147460
  15.0 11.9 %copy-start.3 = (s32[4096,1]{0,1:T(1,128)S(1)}, s32[4096,1]{0,1:T(1,128)}, u32[]{:S(2)}) copy-start(s32[4096,1]{0,1:T(1,128)} %param.16) | copy-start | bytes 49156
  15.0 11.9 %copy-start.4 = (s32[4096]{0:T(1024)S(1)}, s32[4096]{0:T(1024)}, u32[]{:S(2)}) copy-start(s32[4096]{0:T(1024)} %param.17) | copy-start | bytes 49156
  15.0 11.9 %copy-start.10 = (f32[3,4096]{1,0:T(4,128)S(1)}, f32[3,4096]{1,0:T(4,128)}, u32[]{:S(2)}) copy-start(f32[3,4096]{1,0:T(4,128)} %speed.1) | copy-start | bytes 147460
  15.0 11.9 %copy-start.11 = (s32[4096]{0:T(1024)S(1)}, s32[4096]{0:T(1024)}, u32[]{:S(2)}) copy-start(s32[4096]{0:T(1024)} %param.15) | copy-start | bytes 49156
  15.0 6.1 %collective-permute-start.3 = (f32[2,12,8,128]{3,2,1,0:T(8,128)S(1)}, f32[2,12,8,128]{3,2,1,0:T(8,128)S(1)}, u32[]{:S(2)}, u32[]{:S(2)}) collective-permute-start(f32[2,12,8,128]{3,2,1,0:T(8,128)S(1)} %pad_maximum_fusion.1), channel_id=1, source_target_pairs={{1,0},{2,1},{3,2},{5,4},{6,5},{7,6},{9,8},{10,9},{11,10},{13,12},{... | collective-permute-start | bytes 294920 | tf_op jit(solution)/shard_map/ppermute | solution.py:544
  35.8 26.3 %all-to-all-start = ((f32[64,8,128]{2,1,0:T(8,128)}), f32[64,8,128]{2,1,0:T(8,128)S(1)}, u32[]{:S(2)}, u32[]{:S(2)}) async-start(f32[64,8,128]{2,1,0:T(8,128)} %markers.1), calls=%async_computation | async-start | bytes 524288 | tf_op jit(solution)/shard_map/all_to_all | solution.py:616
  50.5 18.5 %copy-start.7 = (f32[9,128]{1,0:T(8,128)S(1)}, f32[9,128]{1,0:T(8,128)}, u32[]{:S(2)}) copy-start(f32[9,128]{1,0:T(8,128)} %state.1) | copy-start | bytes 13828
  50.6 18.5 %copy-start.9 = (f32[4,128]{1,0:T(4,128)S(1)}, f32[4,128]{1,0:T(4,128)}, u32[]{:S(2)}) copy-start(f32[4,128]{1,0:T(4,128)} %inertia.1) | copy-start | bytes 6148
  50.6 29.7 %copy-start.6 = (s32[4,8,6]{1,0,2:T(4,128)S(1)}, s32[4,8,6]{1,0,2:T(4,128)}, u32[]{:S(2)}) copy-start(s32[4,8,6]{1,0,2:T(4,128)} %param.12) | copy-start | bytes 2308
  59.6 1.0 %copy-start.12 = (bf16[8,12,48,128]{3,2,1,0:T(8,128)(2,1)}, bf16[8,12,48,128]{3,2,1,0:T(8,128)(2,1)S(1)}, u32[]{:S(2)}) copy-start(bf16[8,12,48,128]{3,2,1,0:T(8,128)(2,1)S(1)} %get-tuple-element.52.btab) | copy-start | bytes 3538948
  62.2 3.6 %collective-permute-start.6 = (f32[8,128]{1,0:T(8,128)S(1)}, f32[8,128]{1,0:T(8,128)S(1)}, u32[]{:S(2)}, u32[]{:S(2)}) collective-permute-start(f32[8,128]{1,0:T(8,128)S(1)} %reduce_sum.9.first), channel_id=1, source_target_pairs={{0,3},{1,0},{2,1},{3,2},{4,7},{5,4},{6,5},{7,6},{8,11},{9,8},{10,9... | collective-permute-start | bytes 12296 | tf_op jit(solution)/shard_map/ppermute | solution.py:646
  63.1 4.0 %collective-permute-start.5 = (f32[8,128]{1,0:T(8,128)S(1)}, f32[8,128]{1,0:T(8,128)S(1)}, u32[]{:S(2)}, u32[]{:S(2)}) collective-permute-start(f32[8,128]{1,0:T(8,128)S(1)} %reduce_sum.9.first), channel_id=1, source_target_pairs={{0,2},{1,3},{2,0},{3,1},{4,6},{5,7},{6,4},{7,5},{8,10},{9,11},{10,... | collective-permute-start | bytes 12296 | tf_op jit(solution)/shard_map/ppermute | solution.py:646
  65.4 3.7 %collective-permute-start.4 = (f32[8,128]{1,0:T(8,128)S(1)}, f32[8,128]{1,0:T(8,128)S(1)}, u32[]{:S(2)}, u32[]{:S(2)}) collective-permute-start(f32[8,128]{1,0:T(8,128)S(1)} %reduce_sum.9.first), channel_id=1, source_target_pairs={{0,1},{1,2},{2,3},{3,0},{4,5},{5,6},{6,7},{7,4},{8,9},{9,10},{10,1... | collective-permute-start | bytes 12296 | tf_op jit(solution)/shard_map/ppermute | solution.py:646
  69.8 23.5 %all-to-all-start.1 = ((f32[64,8,128]{2,1,0:T(8,128)}), f32[64,8,128]{2,1,0:T(8,128)S(1)}, u32[]{:S(2)}, u32[]{:S(2)}) async-start(f32[64,8,128]{2,1,0:T(8,128)} %get-tuple-element.50), calls=%async_computation.1 | async-start | bytes 524288 | tf_op jit(solution)/shard_map/all_to_all | solution.py:661
  80.3 1.3 %copy-start.13 = (bf16[8,12,48,128]{3,2,1,0:T(8,128)(2,1)S(1)}, bf16[8,12,48,128]{3,2,1,0:T(8,128)(2,1)}, u32[]{:S(2)}) copy-start(bf16[8,12,48,128]{3,2,1,0:T(8,128)(2,1)} %copy-done.12) | copy-start | bytes 3538948

commit v4 on v3

--- a/solution.py
+++ b/solution.py
@@ -17,13 +17,14 @@
 TP = 128
 ROWS = 16
 AUG = 48
-FACTORS = 80
-TILES = 4
+FACTORS = 48
+TILES = 10
+ONEHOT = 9
 SCALE = (2.0 * 1.4426950408889634) ** 0.5
 FAR = 1e30
 PLACE_LIMIT = 4.0
 CLIP = 1e4
-SPEED_LIMIT = 256.0
+SPEED_LIMIT = 8.0
 F32 = jnp.float32
 BF16 = jnp.bfloat16
 NT = (((1,), (1,)), ((), ()))
@@ -191,12 +192,12 @@
 
 
 def fill_sources(ext, btab, first, last, left, right):
-    def step(index, carry):
-        row, col = first + index // (right - left), left + index % (right - left)
-        btab[row, col] = augmented(ext[row, col], True).astype(BF16)
+    def step(row, carry):
+        for col in range(left, right):
+            btab[row, col] = augmented(ext[row, col], True).astype(BF16)
         return carry
 
-    lax.fori_loop(0, (last - first) * (right - left), step, 0, unroll=4)
+    lax.fori_loop(first, last, step, 0)
 
 
 def left_of(ext, row, col):
@@ -225,51 +226,84 @@
             out[layer, column] = jnp.concatenate(rows + [live, listed.astype(F32)], axis=0)
 
 
-def density_kernel(codes, own, west, east, up, down, out, ext, btab, sums, lives):
+def rim_tile(index, layers, columns):
+    side = index - 2 * columns
+    on_side, last = side >= 0, index >= columns
+    layer = jnp.where(on_side, 1 + (side >> 1), jnp.where(last, layers - 1, 0))
+    column = jnp.where(
+        on_side, (columns - 1) * (side & 1), jnp.where(last, index - columns, index)
+    )
+    return layer, column
+
+
+def inner_kernel(codes, own, lefts, sums, btab):
+    layers, columns = own.shape[0], own.shape[1]
+    eye = eye_mask()
+    fill_sources(own, btab, 0, layers, 0, columns)
+
+    def turn(layer, carry):
+        for column in range(columns):
+            lefts[layer, column] = left_of(own, layer, column)
+        return carry
+
+    lax.fori_loop(0, layers, turn, 0)
+
+    def step(layer, carry):
+        for column in range(1, columns - 1):
+            places = near(codes, layer, column, layer, column)
+            row = fast_sum(lefts[layer, column], btab, places, eye)
+            sums[layer, column : column + 1, :] = row
+        return carry
+
+    lax.fori_loop(1, layers - 1, step, 0)
+
+
+def density_kernel(codes, own, west, east, up, down, lefts, inner, out, ext, btab, sums):
     layers, columns = own.shape[0], own.shape[1]
     assemble(own, west, east, up, down, ext)
     eye = eye_mask()
     fast = moderate(ext)
+    sums[...] = inner[...]
 
     @pl.when(fast)
     def _():
         fill_sources(ext, btab, 1, layers + 3, 1, columns + 3)
+        rim = 2 * columns + 2 * (layers - 2)
 
         def step(group, carry):
             for part in range(TILES):
-                tile = group * TILES + part
-                layer, column = tile // columns, tile % columns
+                index = group * TILES + part
+                layer, column = rim_tile(index, layers, columns)
                 places = near(codes, layer, column, layer + 2, column + 2)
-                left = left_of(ext, layer + 2, column + 2)
-                sums[pl.ds(tile, 1), :] = fast_sum(left, btab, places, eye)
+                row = fast_sum(lefts[layer, column], btab, places, eye)
+                sums[layer, pl.ds(column, 1), :] = row
             return carry
 
-        lax.fori_loop(0, layers * columns // TILES, step, 0)
+        lax.fori_loop(0, rim // TILES, step, 0)
 
     @pl.when(jnp.logical_not(fast))
     def _():
         def step(tile, carry):
             layer, column = tile // columns, tile % columns
             places = near(codes, layer, column, layer + 2, column + 2)
-            sums[pl.ds(tile, 1), :] = slow_sum(ext, layer + 2, column + 2, places, eye)
+            row = slow_sum(ext, layer + 2, column + 2, places, eye)
+            sums[layer, pl.ds(column, 1), :] = row
             return carry
 
         lax.fori_loop(0, layers * columns, step, 0)
 
     for layer in range(layers):
-        for column in range(columns):
-            tile = layer * columns + column
-            lives[tile : tile + 1, :] = own[layer, column, 6:7, :]
-    press, damp = state_of(sums[...])
-    live = lives[...]
-    out[0] = press
-    out[1] = damp
-    out[2] = press * live
-    out[3] = damp * live
+        span = slice(layer * columns, (layer + 1) * columns)
+        press, damp = state_of(sums[layer])
+        live = jnp.concatenate([own[layer, c, 6:7, :] for c in range(columns)], axis=0)
+        out[0, span, :] = press
+        out[1, span, :] = damp
+        out[2, span, :] = press * live
+        out[3, span, :] = damp * live
 
 
 def ring_kernel(
-    codes, own, west, east, up, down, extra, ext, btab, ftab, press_ref, damp_ref
+    codes, own, west, east, up, down, extra, ext, sources, ftab, press_ref, damp_ref, btab
 ):
     layers, columns = own.shape[0], own.shape[1]
     assemble(own, west, east, up, down, ext)
@@ -303,25 +337,25 @@
     def _():
         fill_sources(ext, btab, 0, layers + 4, 0, columns + 4)
 
+        sources[...] = btab[1 : layers + 3, 1 : columns + 3]
+
         def ring_sum(row, col):
             places = near(codes, row, col, row, col)
             keep(row, col, fast_sum(left_of(ext, row, col), btab, places, eye))
 
         ring(ring_sum)
 
-        def factors(index, carry):
-            row, col = 1 + index // (columns + 2), 1 + index % (columns + 2)
-            raw = ext[row, col]
-            press = jnp.broadcast_to(press_ref[row - 1, pl.ds(col - 1, 1), :], (8, TP))
-            damp = jnp.broadcast_to(damp_ref[row - 1, pl.ds(col - 1, 1), :], (8, TP))
-            value = jnp.concatenate([raw, press * raw, damp * raw], axis=0)
-            parts = split3(value)
-            ftab[row, col] = jnp.concatenate(
-                list(parts) + [jnp.zeros((FACTORS - 72, TP), F32)], axis=0
-            ).astype(BF16)
+        def factors(row, carry):
+            for col in range(1, columns + 3):
+                raw = ext[row, col]
+                press = jnp.broadcast_to(press_ref[row - 1, col - 1 : col, :], (8, TP))
+                damp = jnp.broadcast_to(damp_ref[row - 1, col - 1 : col, :], (8, TP))
+                value = jnp.concatenate([raw, press * raw, damp * raw], axis=0)
+                high = value.astype(BF16).astype(F32)
+                ftab[row - 1, col - 1] = jnp.concatenate([high, value - high], axis=0).astype(BF16)
             return carry
 
-        lax.fori_loop(0, (layers + 2) * (columns + 2), factors, 0, unroll=2)
+        lax.fori_loop(1, layers + 3, factors, 0)
 
     @pl.when(jnp.logical_not(fast))
     def _():
@@ -332,41 +366,53 @@
         ring(ring_sum)
 
 
-def accel_kernel(codes, ext, btab, ftab, press_ref, damp_ref, out):
+def accel_kernel(codes, ext, btab, ftab, press_ref, damp_ref, out, pairs, lefts):
     layers, columns = out.shape[0], out.shape[2]
     eye = eye_mask()
     fast = moderate(ext)
 
-    @pl.when(fast)
-    def _():
-        def step(pair, carry):
-            for half in range(2):
-                tile = pair * 2 + half
-                layer, column = tile // columns, tile % columns
-                row, col = layer + 2, column + 2
-                places = near(codes, layer, column, row, col)
-                weights = fast_weights(left_of(ext, row, col), btab, places)
-                highs = [w.astype(BF16) for w in weights]
-                lows = [(w - h.astype(F32)).astype(BF16) for w, h in zip(weights, highs)]
-                sources = [ftab[place] for place in places]
-                summed = lax.dot_general(
-                    jnp.concatenate(sources + sources, axis=1),
-                    jnp.concatenate(highs + lows, axis=1),
+    def weigh(layer):
+        for column in range(columns):
+            lefts[column] = left_of(ext, layer + 2, column + 2)
+        for column in range(columns):
+            places = near(codes, layer, column, layer + 1, column + 1)
+            for p, weight in enumerate(fast_weights(lefts[column], btab, places)):
+                high = weight.astype(BF16)
+                pairs[column, p, :, 0 : 2 * TP] = high
+                pairs[column, p, :, 2 * TP : 4 * TP] = (weight - high.astype(F32)).astype(BF16)
+
+    def gather(layer):
+        for column in range(columns):
+            row, col = layer + 2, column + 2
+            places = near(codes, layer, column, row - 1, col - 1)
+            summed = None
+            for p in range(3):
+                source = jnp.concatenate([ftab[places[2 * p]], ftab[places[2 * p + 1]]], axis=1)
+                part = lax.dot_general(
+                    jnp.concatenate([source, source], axis=1),
+                    pairs[column, p],
                     NT,
                     preferred_element_type=F32,
                 )
-                summed = summed[0:24] + summed[24:48] + summed[48:72]
-                plain, pressed, damped = summed[0:8], summed[8:16], summed[16:24]
-                raw = ext[row, col]
-                press = press_ref[row - 1, pl.ds(col - 1, 1), :]
-                push = raw * (press * plain[6:7] + pressed[6:7]) - (press * plain + pressed)
-                drag = damped - raw * damped[6:7]
-                total = (push[0:3] + drag[3:6]) * (raw[6:7] * (1.0 / TP))
-                for c in range(3):
-                    out[layer, c, pl.ds(column, 1), :] = total[c : c + 1]
+                summed = part if summed is None else summed + part
+            summed = summed[0:24] + summed[24:48]
+            plain, pressed, damped = summed[0:8], summed[8:16], summed[16:24]
+            raw = ext[row, col]
+            press = press_ref[row - 1, col - 1 : col, :]
+            push = raw * (press * plain[6:7] + pressed[6:7]) - (press * plain + pressed)
+            drag = damped - raw * damped[6:7]
+            total = (push[0:3] + drag[3:6]) * (raw[6:7] * (1.0 / TP))
+            for c in range(3):
+                out[layer, c, column : column + 1, :] = total[c : c + 1]
+
+    @pl.when(fast)
+    def _():
+        def step(layer, carry):
+            weigh(layer)
+            gather(layer)
             return carry
 
-        lax.fori_loop(0, layers * columns // 2, step, 0)
+        lax.fori_loop(0, layers, step, 0)
 
     @pl.when(jnp.logical_not(fast))
     def _():
@@ -383,7 +429,7 @@
         lax.fori_loop(0, layers * columns, step, 0)
 
 
-def marker_kernel(soil, extra, place, speed, tiles, owners, slots, out, table):
+def marker_kernel(soil, extra, place, speed, tiles, owners, slots, out, table, lookup):
     layers, columns = soil.shape[0], soil.shape[2]
     count = layers * columns
     pairs = place.shape[1] // (2 * TP)
@@ -398,11 +444,15 @@
     fields = scaled + [norm, press, damp]
     fields = fields + [damp * moves[c] - press * spots[c] for c in range(3)]
     for number, field in enumerate(fields):
-        pieces = list(split3(field)) + [jnp.zeros((TP - 3 * count, TP), F32)]
-        turned = jnp.transpose(jnp.concatenate(pieces, axis=0)).astype(BF16)
-        for group in range(groups):
-            at = (group * 9 + number) * 16
-            table[at : at + 16, :] = turned[group * 16 : group * 16 + 16]
+        if number < ONEHOT:
+            pieces = list(split3(field)) + [jnp.zeros((TP - 3 * count, TP), F32)]
+            turned = jnp.transpose(jnp.concatenate(pieces, axis=0)).astype(BF16)
+            for group in range(groups):
+                at = (group * ONEHOT + number) * 16
+                table[at : at + 16, :] = turned[group * 16 : group * 16 + 16]
+        else:
+            pieces = [field, jnp.zeros((TP - count, TP), F32)]
+            lookup[number - ONEHOT] = jnp.transpose(jnp.concatenate(pieces, axis=0))
     entry = lax.broadcasted_iota(jnp.int32, (TP, TP), 0)
     listed = jnp.where(entry < 3 * count, lax.rem(entry, count), -1)
     out[...] = jnp.zeros(out.shape, F32)
@@ -436,24 +486,33 @@
     def forces_on(pair):
         wide = 2 * TP
         lanes = pl.ds(pl.multiple_of(pair * wide, wide), wide)
-        hots = []
-        for part in range(2):
-            which = jnp.broadcast_to(tiles[pl.ds(pair * 2 + part, 1), :], (TP, TP))
-            hots.append(jnp.where(which == listed, 1.0, 0.0).astype(BF16))
-        hot = jnp.concatenate(hots, axis=1)
+        which = [
+            jnp.broadcast_to(tiles[pl.ds(pair * 2 + part, 1), :], (TP, TP)) for part in range(2)
+        ]
+        hot = jnp.concatenate(
+            [jnp.where(w == listed, 1.0, 0.0).astype(BF16) for w in which], axis=1
+        )
         y = place[:, lanes]
         u = speed[:, lanes]
         spread = y * SCALE
         at = [jnp.broadcast_to(spread[c : c + 1], (16, wide)) for c in range(3)]
         totals = [jnp.zeros((16, wide), F32) for number in range(5)]
         for group in range(groups):
-            picked = lax.dot_general(
-                table[group * 144 : (group + 1) * 144, :],
-                hot,
-                (((1,), (0,)), ((), ())),
-                preferred_element_type=F32,
-            )
-            got = [picked[16 * number : 16 * number + 16] for number in range(9)]
+            span = slice(group * 16, group * 16 + 16)
+            rows = slice(group * 16 * ONEHOT, (group + 1) * 16 * ONEHOT)
+            got = []
+            if ONEHOT:
+                picked = lax.dot_general(
+                    table[rows, :], hot, (((1,), (0,)), ((), ())), preferred_element_type=F32
+                )
+                got = [picked[16 * number : 16 * number + 16] for number in range(ONEHOT)]
+            for number in range(9 - ONEHOT):
+                source = lookup[number, span, :]
+                got.append(
+                    jnp.concatenate(
+                        [jnp.take_along_axis(source, w[0:16], axis=1) for w in which], axis=1
+                    )
+                )
             power = (got[3] + at[0] * got[0]) + (at[1] * got[1] + at[2] * got[2])
             weight = jnp.exp2(power)
             for number in range(5):
@@ -575,7 +634,20 @@
         ],
         compiler_params=params(),
         name="prep",
-    )(tile_count, codes, soil)
+    )(*[pltpu.with_memory_space_constraint(x, pltpu.HBM) for x in (tile_count, codes, soil)])
+    lefts, inner = pl.pallas_call(
+        inner_kernel,
+        out_shape=(
+            jax.ShapeDtypeStruct((layers, columns, TP, AUG), BF16),
+            jax.ShapeDtypeStruct((layers, columns, TP), F32),
+        ),
+        in_specs=[sspec(), vspec()],
+        out_specs=(vspec(), vspec()),
+        scratch_shapes=[VMEM((layers, columns, AUG, TP), BF16)],
+        cost_estimate=cost(4_000_000, 1 << 18, 1_000_000),
+        compiler_params=params(),
+        name="inner",
+    )(codes, own)
     west, east = shifted(own, "tile", 1, 2)
     top = jnp.concatenate([west[:2], own[:2], east[:2]], axis=1)
     bottom = jnp.concatenate([west[-2:], own[-2:], east[-2:]], axis=1)
@@ -587,18 +659,17 @@
     extra = pl.pallas_call(
         density_kernel,
         out_shape=jax.ShapeDtypeStruct((4, layers * columns, TP), F32),
-        in_specs=[sspec()] + [vspec()] * 5,
+        in_specs=[sspec()] + [vspec()] * 7,
         out_specs=vspec(),
         scratch_shapes=[
             VMEM((span, width, 8, TP), F32),
             VMEM((span, width, AUG, TP), BF16),
-            VMEM((layers * columns, TP), F32),
-            VMEM((layers * columns, TP), F32),
+            VMEM((layers, columns, TP), F32),
         ],
         cost_estimate=cost(pairs * 12, 1 << 18, pairs),
         compiler_params=params(),
         name="density",
-    )(codes, *pieces)
+    )(codes, *pieces, lefts, inner)
     owners = marker_owner.reshape((marker_count // TP, TP))
     slots = marker_slot.reshape((marker_count // TP, TP))
     tiles = marker_tile.reshape((marker_count // TP, TP))
@@ -607,14 +678,13 @@
         out_shape=jax.ShapeDtypeStruct((tile_devs, 8, TP), F32),
         in_specs=[vspec()] * 7,
         out_specs=vspec(),
-        scratch_shapes=[VMEM((9 * TP, TP), BF16)],
+        scratch_shapes=[VMEM((9 * TP, TP), BF16), VMEM((9, TP, TP), F32)],
         cost_estimate=cost(marker_count * TP * 25, 1 << 19, marker_count * TP),
         compiler_params=params(),
         name="markers",
     )(soil, extra, marker_pos, marker_vel, tiles, owners, slots)
-    partial_sums, later = lax.optimization_barrier((partial_sums, (pieces, extra)))
+    partial_sums, extra = lax.optimization_barrier((partial_sums, extra))
     arrived = lax.all_to_all(partial_sums, "tile", 0, 0, tiled=True)
-    pieces, extra = later
     own, west, east, up, down = pieces
     ring_codes = jnp.concatenate(
         [
@@ -626,8 +696,8 @@
     ring_codes = jnp.transpose(ring_codes.astype(jnp.int32), (2, 0, 1))
     shapes = (
         jax.ShapeDtypeStruct((span, width, 8, TP), F32),
-        jax.ShapeDtypeStruct((span, width, AUG, TP), BF16),
-        jax.ShapeDtypeStruct((span, width, FACTORS, TP), BF16),
+        jax.ShapeDtypeStruct((layers + 2, columns + 2, AUG, TP), BF16),
+        jax.ShapeDtypeStruct((layers + 2, columns + 2, FACTORS, TP), BF16),
         jax.ShapeDtypeStruct((layers + 2, 16, TP), F32),
         jax.ShapeDtypeStruct((layers + 2, 16, TP), F32),
     )
@@ -636,12 +706,14 @@
         out_shape=shapes,
         in_specs=[sspec()] + [vspec()] * 6,
         out_specs=(vspec(),) * 5,
+        scratch_shapes=[VMEM((span, width, AUG, TP), BF16)],
         cost_estimate=cost(pairs * 15, 1 << 19, pairs),
         compiler_params=params(),
         name="ring",
     )(ring_codes, *pieces, extra)
-    arrived, tables = lax.optimization_barrier((arrived, tables))
+    arrived, damp = lax.optimization_barrier((arrived, tables[4]))
     share = jnp.sum(arrived, axis=0)
+
     others = [
         lax.ppermute(share, "depth", [(i, (i + k) % depth_devs) for i in range(depth_devs)])
         for k in range(1, depth_devs)
@@ -657,17 +729,18 @@
         compiler_params=params(),
         name="advance",
     )(share, *others, body_state, body_inertia)
-    sent, tables = lax.optimization_barrier((sent, tables))
+    sent, damp = lax.optimization_barrier((sent, damp))
     states = lax.all_to_all(sent, "tile", 0, 0, tiled=True)
     accel = pl.pallas_call(
         accel_kernel,
         out_shape=jax.ShapeDtypeStruct((layers, 3, columns, TP), F32),
         in_specs=[sspec()] + [vspec()] * 5,
         out_specs=vspec(),
+        scratch_shapes=[VMEM((columns, 3, TP, 4 * TP), BF16), VMEM((columns, TP, AUG), BF16)],
         cost_estimate=cost(pairs * 15, 1 << 19, pairs),
         compiler_params=params(),
         name="accel",
-    )(codes, *tables)
+    )(codes, *tables[:4], damp)
     states, accel = lax.optimization_barrier((states, accel))
     soil_accel = jnp.transpose(accel, (0, 2, 1, 3))
     marker_vel_next = pl.pallas_call(

time: 97.3 us -> 88.4 us (0.909)
  Pallas kernels: 40.6 us -> 35.5 us
  local copies, waits for them, and re-layouts: 4.99 us -> 0.39 us
  waiting for transfers between devices: 10.6 us -> 13.9 us
  starting transfers between devices: 39.6 us -> 37.1 us
    unnamed x29 -> x19, local copies, waits for them, and re-layouts: 4.75 us -> 0.15 us
    all_to_all x1, waiting for transfers between devices: 0.01 us -> 3.52 us  [local(): states = lax.all_to_all(sent, 'tile', 0, 0, tiled=True)]
    pallas_call x1, Pallas kernels: 11.8 us -> 8.45 us  [local(): pl.pallas_call(accel_kernel, out_shape=jax.ShapeDtypeStruct((layers, 3, c...]
    pallas_call x1, Pallas kernels: 5.76 us -> 2.73 us  [local(): pl.pallas_call(density_kernel, out_shape=jax.ShapeDtypeStruct((4, layers...]
    ppermute x4, waiting for transfers between devices: 5.8 us -> 3.16 us  [shifted(): return (lax.ppermute(last, axis, up), lax.ppermute(first, axis, down))]
    pallas_call x0 -> x1, Pallas kernels: none -> 2.62 us  [local(): pl.pallas_call(inner_kernel, out_shape=(jax.ShapeDtypeStruct((layers, col...]
    all_to_all x1, waiting for transfers between devices: 1.48 us -> 4 us  [local(): arrived = lax.all_to_all(partial_sums, 'tile', 0, 0, tiled=True)]
    all_to_all x1, starting transfers between devices: 10.5 us -> 8.06 us  [local(): states = lax.all_to_all(sent, 'tile', 0, 0, tiled=True)]
where the time goes in v4:
time: 88.4 us; the launch traced here: 88 us
  starting transfers between devices  37.1 us (42%)
  Pallas kernels  35.5 us (40%)
  waiting for transfers between devices  13.9 us (16%)
    all_to_all x1, starting transfers between devices, local(): arrived = lax.all_to_all(partial_sums, 'tile', 0, 0, tiled=True)  14.3 us
    ppermute x4, starting transfers between devices, shifted(): return (lax.ppermute(last, axis, up), lax.ppermute(first, axis, down))  11.2 us
    pallas_call x1, Pallas kernels, local(): pl.pallas_call(marker_kernel, out_shape=jax.ShapeDtypeStruct((tile_devs,...  8.89 us
    pallas_call x1, Pallas kernels, local(): pl.pallas_call(accel_kernel, out_shape=jax.ShapeDtypeStruct((layers, 3, c...  8.45 us
    all_to_all x1, starting transfers between devices, local(): states = lax.all_to_all(sent, 'tile', 0, 0, tiled=True)  8.06 us
    pallas_call x1, Pallas kernels, local(): pl.pallas_call(ring_kernel, out_shape=shapes, in_specs=[sspec()] + [vspec...  7.57 us
    all_to_all x1, waiting for transfers between devices, local(): arrived = lax.all_to_all(partial_sums, 'tile', 0, 0, tiled=True)  4 us
    ppermute x3, starting transfers between devices, local(): lax.ppermute(share, 'depth', [(i, (i + k) % depth_devs) for i in range(de...  3.55 us
  transfers between devices with their start and end apart: 9, of which 6 were waited for; matrix products, arithmetic and copies ran while one was open for 0% of the time, Pallas kernels for 21%

profile of v4, /device:TPU:1, one launch (start us, length us, event | category | flops | bytes accessed | tf_op | source)
XLA Modules:
  0.0 88.0 jit_solution(36371245060388287)
XLA Ops:
  0.6 1.0 %prep.1.own = f32[4,8,8,128]{3,2,1,0:T(8,128)S(1)} custom-call(s32[4,8]{1,0:T(4,128)} %counts_in.1, s32[6,4,8]{2,1,0:T(4,128)} %bitcast.17, f32[4,6,8,128]{3,2,1,0:T(8,128)} %bitcast.11), custom_call_target="tpu_custom_call" | custom-call | tf_op jit(solution)/shard_map/prep/pallas_call | solution.py:624
  1.7 5.1 %collective-permute-start.1 = (f32[4,2,8,128]{3,2,1,0:T(8,128)S(1)}, f32[4,2,8,128]{3,2,1,0:T(8,128)S(1)}, u32[]{:S(2)}, u32[]{:S(2)}) collective-permute-start(f32[4,2,8,128]{3,2,1,0:T(8,128)S(1)} %get-tuple-element.39), channel_id=1, source_target_pairs={{4,0},{8,4},{12,8},{16,12},{20,16},{24,20},{28,24},{32,28},{36,32}... | collective-permute-start | bytes 98312 | tf_op jit(solution)/shard_map/ppermute | solution.py:603
  6.8 1.9 %collective-permute-start = (f32[4,2,8,128]{3,2,1,0:T(8,128)S(1)}, f32[4,2,8,128]{3,2,1,0:T(8,128)S(1)}, u32[]{:S(2)}, u32[]{:S(2)}) collective-permute-start(f32[4,2,8,128]{3,2,1,0:T(8,128)S(1)} %get-tuple-element.40), channel_id=1, source_target_pairs={{0,4},{4,8},{8,12},{12,16},{16,20},{20,24},{24,28},{28,32},{32,36}... | collective-permute-start | bytes 98312 | tf_op jit(solution)/shard_map/ppermute | solution.py:603
  8.8 1.1 %collective-permute-done.west = f32[4,2,8,128]{3,2,1,0:T(8,128)S(1)} collective-permute-done((f32[4,2,8,128]{3,2,1,0:T(8,128)S(1)}, f32[4,2,8,128]{3,2,1,0:T(8,128)S(1)}, u32[]{:S(2)}, u32[]{:S(2)}) %collective-permute-start) | collective-permute-done | bytes 32800 | tf_op jit(solution)/shard_map/ppermute | solution.py:603
  9.9 2.8 %collective-permute-start.2 = (f32[2,12,8,128]{3,2,1,0:T(8,128)S(1)}, f32[2,12,8,128]{3,2,1,0:T(8,128)S(1)}, u32[]{:S(2)}, u32[]{:S(2)}) collective-permute-start(f32[2,12,8,128]{3,2,1,0:T(8,128)S(1)} %pad_maximum_fusion), channel_id=1, source_target_pairs={{0,1},{1,2},{2,3},{4,5},{5,6},{6,7},{8,9},{9,10},{10,11},{12,13},{... | collective-permute-start | bytes 294920 | tf_op jit(solution)/shard_map/ppermute | solution.py:603
  12.8 1.3 %collective-permute-start.3 = (f32[2,12,8,128]{3,2,1,0:T(8,128)S(1)}, f32[2,12,8,128]{3,2,1,0:T(8,128)S(1)}, u32[]{:S(2)}, u32[]{:S(2)}) collective-permute-start(f32[2,12,8,128]{3,2,1,0:T(8,128)S(1)} %pad_maximum_fusion.1), channel_id=1, source_target_pairs={{1,0},{2,1},{3,2},{5,4},{6,5},{7,6},{9,8},{10,9},{11,10},{13,12},{... | collective-permute-start | bytes 294920 | tf_op jit(solution)/shard_map/ppermute | solution.py:603
  14.1 2.6 %inner.1 = (bf16[4,8,128,48]{3,2,1,0:T(8,128)(2,1)S(1)}, f32[4,8,128]{2,1,0:T(8,128)S(1)}) custom-call(s32[6,4,8]{2,1,0:T(4,128)S(1)} %bitcast.18, f32[4,8,8,128]{3,2,1,0:T(8,128)S(1)} %prep.1.own), custom_call_target="tpu_custom_call" | custom-call | flops 4000000 | bytes 262144 | tf_op jit(solution)/shard_map/inner/pallas_call | solution.py:638
  16.8 2.0 %collective-permute-done.3.down = f32[2,12,8,128]{3,2,1,0:T(8,128)S(1)} collective-permute-done((f32[2,12,8,128]{3,2,1,0:T(8,128)S(1)}, f32[2,12,8,128]{3,2,1,0:T(8,128)S(1)}, u32[]{:S(2)}, u32[]{:S(2)}) %collective-permute-start.3) | collective-permute-done | bytes 98336 | tf_op jit(solution)/shard_map/ppermute | solution.py:603
  18.8 2.7 %density.1.extra = f32[4,32,128]{2,1,0:T(8,128)S(1)} custom-call(s32[6,4,8]{2,1,0:T(4,128)S(1)} %bitcast.19, f32[4,8,8,128]{3,2,1,0:T(8,128)S(1)} %prep.1.own, f32[4,2,8,128]{3,2,1,0:T(8,128)S(1)} %collective-permute-done.west, f32[4,2,8,128]{3,2,1,0:T(8,128)S(1)} %collective-permute-done.1.east, f32[2,12,8,128]{3,2,1,0:T(8,128)S(1)} %collective-permute-done.2.up, ...), custom_call_target="tpu_custom_call" | custom-call | flops 37748736 | bytes 262144 | tf_op jit(solution)/shard_map/density/pallas_call | solution.py:659
  21.6 8.9 %markers.1 = f32[64,8,128]{2,1,0:T(8,128)} custom-call(f32[4,6,8,128]{3,2,1,0:T(8,128)S(1)} %bitcast.12, f32[4,32,128]{2,1,0:T(8,128)S(1)} %density.1.extra, f32[3,4096]{1,0:T(4,128)S(1)} %copy-done.1, f32[3,4096]{1,0:T(4,128)S(1)} %copy-done.7, s32[32,128]{1,0:T(8,128)S(1)} %bitcast.21, s32[32,128]{1,0:T(8,128)S(1)} %bitcast.13, s32[32,128]{1,0:T(8,128)S(1)} %bitcast.15), custom_call_target="tpu_custom_call" | custom-call | flops 13107200 | bytes 524288 | tf_op jit(solution)/shard_map/markers/pallas_call | solution.py:676
  30.5 14.3 %all-to-all-start = ((f32[64,8,128]{2,1,0:T(8,128)}), f32[64,8,128]{2,1,0:T(8,128)S(1)}, u32[]{:S(2)}, u32[]{:S(2)}) async-start(f32[64,8,128]{2,1,0:T(8,128)} %markers.1), calls=%async_computation | async-start | bytes 524288 | tf_op jit(solution)/shard_map/all_to_all | solution.py:687
  44.9 0.1 copy.26
  45.2 7.6 %ring.1 = (f32[8,12,8,128]{3,2,1,0:T(8,128)S(1)}, bf16[6,10,48,128]{3,2,1,0:T(8,128)(2,1)S(1)}, bf16[6,10,48,128]{3,2,1,0:T(8,128)(2,1)S(1)}, f32[6,16,128]{2,1,0:T(8,128)S(1)}, f32[6,16,128]{2,1,0:T(8,128)S(1)}) custom-call(s32[6,8,12]{2,1,0:T(8,128)S(1)} %fusion.codes, f32[4,8,8,128]{3,2,1,0:T(8,128)S(1)} %prep.1.own, ...), custom_call_target="tpu_custom_call" | custom-call | flops 47185920 | bytes 524288 | tf_op jit(solution)/shard_map/ring/pallas_call | solution.py:704
  52.8 4.0 %all-to-all-done = f32[64,8,128]{2,1,0:T(8,128)S(1)} async-done(((f32[64,8,128]{2,1,0:T(8,128)}), f32[64,8,128]{2,1,0:T(8,128)S(1)}, u32[]{:S(2)}, u32[]{:S(2)}) %all-to-all-start) | async-done | bytes 262176 | tf_op jit(solution)/shard_map/all_to_all | solution.py:687
  56.9 1.3 %collective-permute-start.6 = (f32[8,128]{1,0:T(8,128)S(1)}, f32[8,128]{1,0:T(8,128)S(1)}, u32[]{:S(2)}, u32[]{:S(2)}) collective-permute-start(f32[8,128]{1,0:T(8,128)S(1)} %reduce_sum.9.first), channel_id=1, source_target_pairs={{0,3},{1,0},{2,1},{3,2},{4,7},{5,4},{6,5},{7,6},{8,11},{9,8},{10,9... | collective-permute-start | bytes 12296 | tf_op jit(solution)/shard_map/ppermute | solution.py:718
  58.2 1.8 %collective-permute-start.5 = (f32[8,128]{1,0:T(8,128)S(1)}, f32[8,128]{1,0:T(8,128)S(1)}, u32[]{:S(2)}, u32[]{:S(2)}) collective-permute-start(f32[8,128]{1,0:T(8,128)S(1)} %reduce_sum.9.first), channel_id=1, source_target_pairs={{0,2},{1,3},{2,0},{3,1},{4,6},{5,7},{6,4},{7,5},{8,10},{9,11},{10,... | collective-permute-start | bytes 12296 | tf_op jit(solution)/shard_map/ppermute | solution.py:718
  60.0 0.4 collective-permute-start.4
  60.4 1.8 %collective-permute-done.5.third = f32[8,128]{1,0:T(8,128)S(1)} collective-permute-done((f32[8,128]{1,0:T(8,128)S(1)}, f32[8,128]{1,0:T(8,128)S(1)}, u32[]{:S(2)}, u32[]{:S(2)}) %collective-permute-start.5) | collective-permute-done | bytes 4128 | tf_op jit(solution)/shard_map/ppermute | solution.py:718
  62.2 1.5 %collective-permute-done.4.second = f32[8,128]{1,0:T(8,128)S(1)} collective-permute-done((f32[8,128]{1,0:T(8,128)S(1)}, f32[8,128]{1,0:T(8,128)S(1)}, u32[]{:S(2)}, u32[]{:S(2)}) %collective-permute-start.4) | collective-permute-done | bytes 4128 | tf_op jit(solution)/shard_map/ppermute | solution.py:718
  63.7 0.8 advance.1
  64.5 8.1 %all-to-all-start.1 = ((f32[64,8,128]{2,1,0:T(8,128)}), f32[64,8,128]{2,1,0:T(8,128)S(1)}, u32[]{:S(2)}, u32[]{:S(2)}) async-start(f32[64,8,128]{2,1,0:T(8,128)} %get-tuple-element.28), calls=%async_computation.1 | async-start | bytes 524288 | tf_op jit(solution)/shard_map/all_to_all | solution.py:733
  72.5 8.4 %accel.1 = f32[4,3,8,128]{3,2,1,0:T(8,128)} custom-call(s32[6,4,8]{2,1,0:T(4,128)S(1)} %bitcast.20, f32[8,12,8,128]{3,2,1,0:T(8,128)S(1)} %get-tuple-element.29.ext, bf16[6,10,48,128]{3,2,1,0:T(8,128)(2,1)S(1)} %get-tuple-element.30.btab, bf16[6,10,48,128]{3,2,1,0:T(8,128)(2,1)S(1)} %get-tuple-element.31.ftab, ...), custom_call_target="tpu_custom_call" | custom-call | flops 47185920 | bytes 524288 | tf_op jit(solution)/shard_map/accel/pallas_call | solution.py:734
  81.0 3.5 %all-to-all-done.1.states = f32[64,8,128]{2,1,0:T(8,128)S(1)} async-done(((f32[64,8,128]{2,1,0:T(8,128)}), f32[64,8,128]{2,1,0:T(8,128)S(1)}, u32[]{:S(2)}, u32[]{:S(2)}) %all-to-all-start.1) | async-done | bytes 262176 | tf_op jit(solution)/shard_map/all_to_all | solution.py:733
  84.5 3.5 %pick.1 = f32[3,4096]{1,0:T(4,128)} custom-call(f32[64,8,128]{2,1,0:T(8,128)S(1)} %all-to-all-done.1.states, f32[3,4096]{1,0:T(4,128)S(1)} %copy-done.1, s32[32,128]{1,0:T(8,128)S(1)} %bitcast.14, s32[32,128]{1,0:T(8,128)S(1)} %bitcast.16), custom_call_target="tpu_custom_call" | custom-call | tf_op jit(solution)/shard_map/pick/pallas_call | solution.py:746
  (34 shorter events, 0.4 us)
Async XLA Ops:
  1.7 7.1 %collective-permute-start.1 = (f32[4,2,8,128]{3,2,1,0:T(8,128)S(1)}, f32[4,2,8,128]{3,2,1,0:T(8,128)S(1)}, u32[]{:S(2)}, u32[]{:S(2)}) collective-permute-start(f32[4,2,8,128]{3,2,1,0:T(8,128)S(1)} %get-tuple-element.39), channel_id=1, source_target_pairs={{4,0},{8,4},{12,8},{16,12},{20,16},{24,20},{28,24},{32,28},{36,32}... | collective-permute-start | bytes 98312 | tf_op jit(solution)/shard_map/ppermute | solution.py:603
  6.8 3.1 %collective-permute-start = (f32[4,2,8,128]{3,2,1,0:T(8,128)S(1)}, f32[4,2,8,128]{3,2,1,0:T(8,128)S(1)}, u32[]{:S(2)}, u32[]{:S(2)}) collective-permute-start(f32[4,2,8,128]{3,2,1,0:T(8,128)S(1)} %get-tuple-element.40), channel_id=1, source_target_pairs={{0,4},{4,8},{8,12},{12,16},{16,20},{20,24},{24,28},{28,32},{32,36}... | collective-permute-start | bytes 98312 | tf_op jit(solution)/shard_map/ppermute | solution.py:603
  9.9 6.8 %collective-permute-start.2 = (f32[2,12,8,128]{3,2,1,0:T(8,128)S(1)}, f32[2,12,8,128]{3,2,1,0:T(8,128)S(1)}, u32[]{:S(2)}, u32[]{:S(2)}) collective-permute-start(f32[2,12,8,128]{3,2,1,0:T(8,128)S(1)} %pad_maximum_fusion), channel_id=1, source_target_pairs={{0,1},{1,2},{2,3},{4,5},{5,6},{6,7},{8,9},{9,10},{10,11},{12,13},{... | collective-permute-start | bytes 294920 | tf_op jit(solution)/shard_map/ppermute | solution.py:603
  12.8 1.3 %copy-start.4 = (s32[4,8,6]{1,0,2:T(4,128)S(1)}, s32[4,8,6]{1,0,2:T(4,128)}, u32[]{:S(2)}) copy-start(s32[4,8,6]{1,0,2:T(4,128)} %param.12) | copy-start | bytes 2308
  12.8 6.0 %collective-permute-start.3 = (f32[2,12,8,128]{3,2,1,0:T(8,128)S(1)}, f32[2,12,8,128]{3,2,1,0:T(8,128)S(1)}, u32[]{:S(2)}, u32[]{:S(2)}) collective-permute-start(f32[2,12,8,128]{3,2,1,0:T(8,128)S(1)} %pad_maximum_fusion.1), channel_id=1, source_target_pairs={{1,0},{2,1},{3,2},{5,4},{6,5},{7,6},{9,8},{10,9},{11,10},{13,12},{... | collective-permute-start | bytes 294920 | tf_op jit(solution)/shard_map/ppermute | solution.py:603
  18.8 2.8 %copy-start = (f32[4,8,6,128]{3,1,2,0:T(8,128)S(1)}, f32[4,8,6,128]{3,1,2,0:T(8,128)}, u32[]{:S(2)}) copy-start(f32[4,8,6,128]{3,1,2,0:T(8,128)} %param.10) | copy-start | bytes 294916
  18.8 2.8 %copy-start.1 = (f32[3,4096]{1,0:T(4,128)S(1)}, f32[3,4096]{1,0:T(4,128)}, u32[]{:S(2)}) copy-start(f32[3,4096]{1,0:T(4,128)} %place.3) | copy-start | bytes 147460
  18.8 2.8 %copy-start.2 = (s32[4096,1]{0,1:T(1,128)S(1)}, s32[4096,1]{0,1:T(1,128)}, u32[]{:S(2)}) copy-start(s32[4096,1]{0,1:T(1,128)} %param.16) | copy-start | bytes 49156
  18.8 2.8 %copy-start.3 = (s32[4096]{0:T(1024)S(1)}, s32[4096]{0:T(1024)}, u32[]{:S(2)}) copy-start(s32[4096]{0:T(1024)} %param.17) | copy-start | bytes 49156
  18.8 2.8 %copy-start.7 = (f32[3,4096]{1,0:T(4,128)S(1)}, f32[3,4096]{1,0:T(4,128)}, u32[]{:S(2)}) copy-start(f32[3,4096]{1,0:T(4,128)} %speed.1) | copy-start | bytes 147460
  18.8 2.8 %copy-start.8 = (s32[4096]{0:T(1024)S(1)}, s32[4096]{0:T(1024)}, u32[]{:S(2)}) copy-start(s32[4096]{0:T(1024)} %param.15) | copy-start | bytes 49156
  30.5 26.3 %all-to-all-start = ((f32[64,8,128]{2,1,0:T(8,128)}), f32[64,8,128]{2,1,0:T(8,128)S(1)}, u32[]{:S(2)}, u32[]{:S(2)}) async-start(f32[64,8,128]{2,1,0:T(8,128)} %markers.1), calls=%async_computation | async-start | bytes 524288 | tf_op jit(solution)/shard_map/all_to_all | solution.py:687
  56.8 6.9 %copy-start.5 = (f32[9,128]{1,0:T(8,128)S(1)}, f32[9,128]{1,0:T(8,128)}, u32[]{:S(2)}) copy-start(f32[9,128]{1,0:T(8,128)} %state.1) | copy-start | bytes 13828
  56.8 6.9 %copy-start.6 = (f32[4,128]{1,0:T(4,128)S(1)}, f32[4,128]{1,0:T(4,128)}, u32[]{:S(2)}) copy-start(f32[4,128]{1,0:T(4,128)} %inertia.1) | copy-start | bytes 6148
  56.9 3.5 %collective-permute-start.6 = (f32[8,128]{1,0:T(8,128)S(1)}, f32[8,128]{1,0:T(8,128)S(1)}, u32[]{:S(2)}, u32[]{:S(2)}) collective-permute-start(f32[8,128]{1,0:T(8,128)S(1)} %reduce_sum.9.first), channel_id=1, source_target_pairs={{0,3},{1,0},{2,1},{3,2},{4,7},{5,4},{6,5},{7,6},{8,11},{9,8},{10,9... | collective-permute-start | bytes 12296 | tf_op jit(solution)/shard_map/ppermute | solution.py:718
  58.2 4.0 %collective-permute-start.5 = (f32[8,128]{1,0:T(8,128)S(1)}, f32[8,128]{1,0:T(8,128)S(1)}, u32[]{:S(2)}, u32[]{:S(2)}) collective-permute-start(f32[8,128]{1,0:T(8,128)S(1)} %reduce_sum.9.first), channel_id=1, source_target_pairs={{0,2},{1,3},{2,0},{3,1},{4,6},{5,7},{6,4},{7,5},{8,10},{9,11},{10,... | collective-permute-start | bytes 12296 | tf_op jit(solution)/shard_map/ppermute | solution.py:718
  60.0 3.7 %collective-permute-start.4 = (f32[8,128]{1,0:T(8,128)S(1)}, f32[8,128]{1,0:T(8,128)S(1)}, u32[]{:S(2)}, u32[]{:S(2)}) collective-permute-start(f32[8,128]{1,0:T(8,128)S(1)} %reduce_sum.9.first), channel_id=1, source_target_pairs={{0,1},{1,2},{2,3},{3,0},{4,5},{5,6},{6,7},{7,4},{8,9},{9,10},{10,1... | collective-permute-start | bytes 12296 | tf_op jit(solution)/shard_map/ppermute | solution.py:718
  64.5 20.0 %all-to-all-start.1 = ((f32[64,8,128]{2,1,0:T(8,128)}), f32[64,8,128]{2,1,0:T(8,128)S(1)}, u32[]{:S(2)}, u32[]{:S(2)}) async-start(f32[64,8,128]{2,1,0:T(8,128)} %get-tuple-element.28), calls=%async_computation.1 | async-start | bytes 524288 | tf_op jit(solution)/shard_map/all_to_all | solution.py:733

commit v5 on v4

--- a/solution.py
+++ b/solution.py
@@ -20,6 +20,7 @@
 FACTORS = 48
 TILES = 10
 ONEHOT = 9
+PICK = 4
 SCALE = (2.0 * 1.4426950408889634) ** 0.5
 FAR = 1e30
 PLACE_LIMIT = 4.0
@@ -429,11 +430,26 @@
         lax.fori_loop(0, layers * columns, step, 0)
 
 
+def owner_lags():
+    row = row_mask()
+    return [(row + 8 * k) // 6 for k in range(3)]
+
+
+def folded(rows):
+    return (rows[0:6] + rows[6:12]) + (rows[12:18] + rows[18:24])
+
+
+def share_kernel(blocks, out):
+    quads = blocks.shape[0] // 24
+    rows = folded(jnp.sum(blocks[...].reshape((quads, 24, TP)), axis=0))
+    out[...] = jnp.concatenate([rows, jnp.zeros((2, TP), F32)], axis=0)
+
+
 def marker_kernel(soil, extra, place, speed, tiles, owners, slots, out, table, lookup):
     layers, columns = soil.shape[0], soil.shape[2]
     count = layers * columns
     pairs = place.shape[1] // (2 * TP)
-    owner_count = out.shape[0]
+    quads = out.shape[0] // 24
     groups = TP // 16
     field_of = lambda f: jnp.concatenate([soil[layer, f] for layer in range(layers)], axis=0)
     spots = [field_of(c) for c in range(3)]
@@ -457,31 +473,39 @@
     listed = jnp.where(entry < 3 * count, lax.rem(entry, count), -1)
     out[...] = jnp.zeros(out.shape, F32)
 
+    lags = owner_lags()
+
     def add_terms(pair, terms):
         left, right = [], []
         for part in range(2):
             block = pair * 2 + part
             value = terms[:, part * TP : (part + 1) * TP]
             high = value.astype(BF16).astype(F32)
-            low = value - high
             owner = jnp.broadcast_to(owners[pl.ds(block, 1), :], (8, TP))
+            late = [owner - lag for lag in lags]
             slot = jnp.broadcast_to(slots[pl.ds(block, 1), :], (TP, TP))
             hot = jnp.where(slot == entry, 1.0, 0.0).astype(BF16)
-            masks = [owner == o for o in range(owner_count)]
-            for piece in (high, low):
+            masks = [late[k] == 4 * quad for quad in range(quads) for k in range(3)]
+            for piece in (high, value - high):
+                turned = [
+                    jnp.concatenate(
+                        [piece[(8 * k + r) % 6 : (8 * k + r) % 6 + 1] for r in range(8)], axis=0
+                    )
+                    for k in range(3)
+                ]
                 left.append(
                     jnp.concatenate(
-                        [jnp.where(mask, piece, 0.0) for mask in masks], axis=0
+                        [jnp.where(mask, turned[n % 3], 0.0) for n, mask in enumerate(masks)],
+                        axis=0,
                     ).astype(BF16)
                 )
                 right.append(hot)
-        summed = lax.dot_general(
+        out[...] = out[...] + lax.dot_general(
             jnp.concatenate(left, axis=1),
             jnp.concatenate(right, axis=1),
             NT,
             preferred_element_type=F32,
         )
-        out[...] = out[...] + summed.reshape(out.shape)
 
     def forces_on(pair):
         wide = 2 * TP
@@ -565,25 +589,30 @@
     out[...] = jnp.concatenate(new_center + new_vel + new_spin, axis=0)
     swing = cross(new_spin, center)
     base = [new_vel[c] - swing[c] for c in range(3)]
-    block = jnp.concatenate(base + new_spin + [jnp.zeros((2, TP), F32)], axis=0)
-    sent[...] = jnp.broadcast_to(block[None], sent.shape)
+    block = jnp.concatenate((base + new_spin) * 4, axis=0)
+    quads = sent.shape[0] // 24
+    sent[...] = jnp.broadcast_to(block[None], (quads, 24, TP)).reshape(sent.shape)
 
 
 def pick_kernel(states, place, owners, slots, out):
-    steps = place.shape[1] // (4 * TP)
-    owner_count = states.shape[0]
-
-    def step(quad, carry):
-        for part in range(4):
-            block = quad * 4 + part
+    steps = place.shape[1] // (PICK * TP)
+    quads = states.shape[0] // 24
+    lags = owner_lags()
+
+    def step(index, carry):
+        for part in range(PICK):
+            block = index * PICK + part
             lanes = pl.ds(pl.multiple_of(block * TP, TP), TP)
             slot = jnp.broadcast_to(slots[pl.ds(block, 1), :], (8, TP))
             owner = jnp.broadcast_to(owners[pl.ds(block, 1), :], (8, TP))
-            found = [jnp.zeros((8, TP), F32) for lane in range(2)]
-            for o in range(owner_count):
-                here = jnp.take_along_axis(states[o], slot, axis=1)
-                found[o % 2] = jnp.where(owner == o, here, found[o % 2])
-            picked = found[0] + found[1]
+            late = [owner - lag for lag in lags]
+            found = [jnp.zeros((8, TP), F32) for k in range(3)]
+            for quad in range(quads):
+                for k in range(3):
+                    at = 24 * quad + 8 * k
+                    here = jnp.take_along_axis(states[at : at + 8, :], slot, axis=1)
+                    found[k] = jnp.where(late[k] == 4 * quad, here, found[k])
+            picked = folded(jnp.concatenate(found, axis=0))
             y = place[:, lanes]
             turn = cross(
                 [picked[3 + c : 4 + c] for c in range(3)], [y[c : c + 1] for c in range(3)]
@@ -675,7 +704,7 @@
     tiles = marker_tile.reshape((marker_count // TP, TP))
     partial_sums = pl.pallas_call(
         marker_kernel,
-        out_shape=jax.ShapeDtypeStruct((tile_devs, 8, TP), F32),
+        out_shape=jax.ShapeDtypeStruct((tile_devs * 6, TP), F32),
         in_specs=[vspec()] * 7,
         out_specs=vspec(),
         scratch_shapes=[VMEM((9 * TP, TP), BF16), VMEM((9, TP, TP), F32)],
@@ -684,7 +713,8 @@
         name="markers",
     )(soil, extra, marker_pos, marker_vel, tiles, owners, slots)
     partial_sums, extra = lax.optimization_barrier((partial_sums, extra))
-    arrived = lax.all_to_all(partial_sums, "tile", 0, 0, tiled=True)
+    flat = (tile_devs, 1, 6 * TP)
+    arrived = lax.all_to_all(partial_sums.reshape(flat), "tile", 0, 0, tiled=True)
     own, west, east, up, down = pieces
     ring_codes = jnp.concatenate(
         [
@@ -712,7 +742,14 @@
         name="ring",
     )(ring_codes, *pieces, extra)
     arrived, damp = lax.optimization_barrier((arrived, tables[4]))
-    share = jnp.sum(arrived, axis=0)
+    share = pl.pallas_call(
+        share_kernel,
+        out_shape=jax.ShapeDtypeStruct((8, TP), F32),
+        in_specs=[vspec()],
+        out_specs=vspec(),
+        compiler_params=params(),
+        name="share",
+    )(arrived.reshape((tile_devs * 6, TP)))
 
     others = [
         lax.ppermute(share, "depth", [(i, (i + k) % depth_devs) for i in range(depth_devs)])
@@ -722,7 +759,7 @@
         advance_kernel,
         out_shape=(
             jax.ShapeDtypeStruct((9, TP), F32),
-            jax.ShapeDtypeStruct((tile_devs, 8, TP), F32),
+            jax.ShapeDtypeStruct((tile_devs * 6, TP), F32),
         ),
         in_specs=[vspec()] * 6,
         out_specs=(vspec(), vspec()),
@@ -730,7 +767,7 @@
         name="advance",
     )(share, *others, body_state, body_inertia)
     sent, damp = lax.optimization_barrier((sent, damp))
-    states = lax.all_to_all(sent, "tile", 0, 0, tiled=True)
+    states = lax.all_to_all(sent.reshape(flat), "tile", 0, 0, tiled=True)
     accel = pl.pallas_call(
         accel_kernel,
         out_shape=jax.ShapeDtypeStruct((layers, 3, columns, TP), F32),
@@ -750,7 +787,7 @@
         out_specs=vspec(),
         compiler_params=params(),
         name="pick",
-    )(states, marker_pos, owners, slots)
+    )(states.reshape((tile_devs * 6, TP)), marker_pos, owners, slots)
     return (soil_accel, body_next, marker_vel_next)
 
 

time: 88.4 us -> 86.2 us (0.975)
  waiting for transfers between devices: 13.9 us -> 11.9 us
  Pallas kernels: 35.5 us -> 34.4 us
  starting transfers between devices: 37.1 us -> 38.1 us
    all_to_all x2, waiting for transfers between devices: 7.52 us -> 5.49 us  [the longest x1 2.98 us: local(): lax.all_to_all(partial_sums.reshape(flat), 'tile', 0, 0, tiled=True)]
    all_to_all x2, starting transfers between devices: 22.4 us -> 23.4 us  [the longest x1 14.3 us: local(): lax.all_to_all(partial_sums.reshape(flat), 'tile', 0, 0, tiled=True)]
    pallas_call x1 -> x2, Pallas kernels: 8.89 us -> 8.33 us  [the longest x1 8.31 us: local(): pl.pallas_call(marker_kernel, out_shape=jax.ShapeDtypeStruct((tile_devs *...]
  transfers between devices with their start and end apart: 9 -> 9, of which waited for: 6 -> 6; matrix products, arithmetic and copies ran while one was open for 0% -> 0% of each run, Pallas kernels for 21% -> 22%
where the time goes in v5:
time: 86.2 us; the launch traced here: 85.8 us
  starting transfers between devices  38.1 us (44%)
  Pallas kernels  34.4 us (40%)
  waiting for transfers between devices  11.9 us (14%)
    all_to_all x1, starting transfers between devices, local(): lax.all_to_all(partial_sums.reshape(flat), 'tile', 0, 0, tiled=True)  14.3 us
    ppermute x4, starting transfers between devices, shifted(): return (lax.ppermute(last, axis, up), lax.ppermute(first, axis, down))  11.2 us
    all_to_all x1, starting transfers between devices, local(): states = lax.all_to_all(sent.reshape(flat), 'tile', 0, 0, tiled=True)  9.05 us
    pallas_call x1, Pallas kernels, local(): pl.pallas_call(accel_kernel, out_shape=jax.ShapeDtypeStruct((layers, 3, c...  8.44 us
    pallas_call x1, Pallas kernels, local(): pl.pallas_call(marker_kernel, out_shape=jax.ShapeDtypeStruct((tile_devs *...  8.31 us
    pallas_call x1, Pallas kernels, local(): pl.pallas_call(ring_kernel, out_shape=shapes, in_specs=[sspec()] + [vspec...  7.57 us
    ppermute x3, starting transfers between devices, local(): lax.ppermute(share, 'depth', [(i, (i + k) % depth_devs) for i in range(de...  3.55 us
    ppermute x3, waiting for transfers between devices, local(): lax.ppermute(share, 'depth', [(i, (i + k) % depth_devs) for i in range(de...  3.28 us
  transfers between devices with their start and end apart: 9, of which 6 were waited for; matrix products, arithmetic and copies ran while one was open for 0% of the time, Pallas kernels for 22%

profile of v5, /device:TPU:1, one launch (start us, length us, event | category | flops | bytes accessed | tf_op | source)
XLA Modules:
  0.0 85.8 jit_solution(9096984469251202814)
XLA Ops:
  0.6 1.0 %prep.1.own = f32[4,8,8,128]{3,2,1,0:T(8,128)S(1)} custom-call(s32[4,8]{1,0:T(4,128)} %counts_in.1, s32[6,4,8]{2,1,0:T(4,128)} %bitcast.23, f32[4,6,8,128]{3,2,1,0:T(8,128)} %bitcast.17), custom_call_target="tpu_custom_call" | custom-call | tf_op jit(solution)/shard_map/prep/pallas_call | solution.py:653
  1.7 5.1 %collective-permute-start.1 = (f32[4,2,8,128]{3,2,1,0:T(8,128)S(1)}, f32[4,2,8,128]{3,2,1,0:T(8,128)S(1)}, u32[]{:S(2)}, u32[]{:S(2)}) collective-permute-start(f32[4,2,8,128]{3,2,1,0:T(8,128)S(1)} %get-tuple-element.39), channel_id=1, source_target_pairs={{4,0},{8,4},{12,8},{16,12},{20,16},{24,20},{28,24},{32,28},{36,32}... | collective-permute-start | bytes 98312 | tf_op jit(solution)/shard_map/ppermute | solution.py:632
  6.8 1.9 %collective-permute-start = (f32[4,2,8,128]{3,2,1,0:T(8,128)S(1)}, f32[4,2,8,128]{3,2,1,0:T(8,128)S(1)}, u32[]{:S(2)}, u32[]{:S(2)}) collective-permute-start(f32[4,2,8,128]{3,2,1,0:T(8,128)S(1)} %get-tuple-element.40), channel_id=1, source_target_pairs={{0,4},{4,8},{8,12},{12,16},{16,20},{20,24},{24,28},{28,32},{32,36}... | collective-permute-start | bytes 98312 | tf_op jit(solution)/shard_map/ppermute | solution.py:632
  8.8 1.1 %collective-permute-done.west = f32[4,2,8,128]{3,2,1,0:T(8,128)S(1)} collective-permute-done((f32[4,2,8,128]{3,2,1,0:T(8,128)S(1)}, f32[4,2,8,128]{3,2,1,0:T(8,128)S(1)}, u32[]{:S(2)}, u32[]{:S(2)}) %collective-permute-start) | collective-permute-done | bytes 32800 | tf_op jit(solution)/shard_map/ppermute | solution.py:632
  9.9 2.8 %collective-permute-start.2 = (f32[2,12,8,128]{3,2,1,0:T(8,128)S(1)}, f32[2,12,8,128]{3,2,1,0:T(8,128)S(1)}, u32[]{:S(2)}, u32[]{:S(2)}) collective-permute-start(f32[2,12,8,128]{3,2,1,0:T(8,128)S(1)} %pad_maximum_fusion), channel_id=1, source_target_pairs={{0,1},{1,2},{2,3},{4,5},{5,6},{6,7},{8,9},{9,10},{10,11},{12,13},{... | collective-permute-start | bytes 294920 | tf_op jit(solution)/shard_map/ppermute | solution.py:632
  12.8 1.3 %collective-permute-start.3 = (f32[2,12,8,128]{3,2,1,0:T(8,128)S(1)}, f32[2,12,8,128]{3,2,1,0:T(8,128)S(1)}, u32[]{:S(2)}, u32[]{:S(2)}) collective-permute-start(f32[2,12,8,128]{3,2,1,0:T(8,128)S(1)} %pad_maximum_fusion.1), channel_id=1, source_target_pairs={{1,0},{2,1},{3,2},{5,4},{6,5},{7,6},{9,8},{10,9},{11,10},{13,12},{... | collective-permute-start | bytes 294920 | tf_op jit(solution)/shard_map/ppermute | solution.py:632
  14.1 2.6 %inner.1 = (bf16[4,8,128,48]{3,2,1,0:T(8,128)(2,1)S(1)}, f32[4,8,128]{2,1,0:T(8,128)S(1)}) custom-call(s32[6,4,8]{2,1,0:T(4,128)S(1)} %bitcast.24, f32[4,8,8,128]{3,2,1,0:T(8,128)S(1)} %prep.1.own), custom_call_target="tpu_custom_call" | custom-call | flops 4000000 | bytes 262144 | tf_op jit(solution)/shard_map/inner/pallas_call | solution.py:667
  16.8 2.0 %collective-permute-done.3.down = f32[2,12,8,128]{3,2,1,0:T(8,128)S(1)} collective-permute-done((f32[2,12,8,128]{3,2,1,0:T(8,128)S(1)}, f32[2,12,8,128]{3,2,1,0:T(8,128)S(1)}, u32[]{:S(2)}, u32[]{:S(2)}) %collective-permute-start.3) | collective-permute-done | bytes 98336 | tf_op jit(solution)/shard_map/ppermute | solution.py:632
  18.8 2.7 %density.1.extra = f32[4,32,128]{2,1,0:T(8,128)S(1)} custom-call(s32[6,4,8]{2,1,0:T(4,128)S(1)} %bitcast.25, f32[4,8,8,128]{3,2,1,0:T(8,128)S(1)} %prep.1.own, f32[4,2,8,128]{3,2,1,0:T(8,128)S(1)} %collective-permute-done.west, f32[4,2,8,128]{3,2,1,0:T(8,128)S(1)} %collective-permute-done.1.east, f32[2,12,8,128]{3,2,1,0:T(8,128)S(1)} %collective-permute-done.2.up, ...), custom_call_target="tpu_custom_call" | custom-call | flops 37748736 | bytes 262144 | tf_op jit(solution)/shard_map/density/pallas_call | solution.py:688
  21.6 8.3 %markers.1 = f32[384,128]{1,0:T(8,128)} custom-call(f32[4,6,8,128]{3,2,1,0:T(8,128)S(1)} %bitcast.18, f32[4,32,128]{2,1,0:T(8,128)S(1)} %density.1.extra, f32[3,4096]{1,0:T(4,128)S(1)} %copy-done.1, f32[3,4096]{1,0:T(4,128)S(1)} %copy-done.7, s32[32,128]{1,0:T(8,128)S(1)} %bitcast.27, s32[32,128]{1,0:T(8,128)S(1)} %bitcast.19, s32[32,128]{1,0:T(8,128)S(1)} %bitcast.21), custom_call_target="tpu_custom_call" | custom-call | flops 13107200 | bytes 524288 | tf_op jit(solution)/shard_map/markers/pallas_call | solution.py:705
  29.9 14.3 %all-to-all-start = ((f32[64,1,768]{2,1,0:T(1,128)}), f32[64,1,768]{2,1,0:T(1,128)S(1)}, u32[]{:S(2)}, u32[]{:S(2)}) async-start(f32[64,1,768]{2,1,0:T(1,128)} %bitcast.5), calls=%async_computation | async-start | bytes 393216 | tf_op jit(solution)/shard_map/all_to_all | solution.py:717
  44.3 0.1 copy.28
  44.6 7.6 %ring.1 = (f32[8,12,8,128]{3,2,1,0:T(8,128)S(1)}, bf16[6,10,48,128]{3,2,1,0:T(8,128)(2,1)S(1)}, bf16[6,10,48,128]{3,2,1,0:T(8,128)(2,1)S(1)}, f32[6,16,128]{2,1,0:T(8,128)S(1)}, f32[6,16,128]{2,1,0:T(8,128)S(1)}) custom-call(s32[6,8,12]{2,1,0:T(8,128)S(1)} %fusion.codes, f32[4,8,8,128]{3,2,1,0:T(8,128)S(1)} %prep.1.own, ...), custom_call_target="tpu_custom_call" | custom-call | flops 47185920 | bytes 524288 | tf_op jit(solution)/shard_map/ring/pallas_call | solution.py:734
  52.2 3.0 %all-to-all-done = f32[64,1,768]{2,1,0:T(1,128)S(1)} async-done(((f32[64,1,768]{2,1,0:T(1,128)}), f32[64,1,768]{2,1,0:T(1,128)S(1)}, u32[]{:S(2)}, u32[]{:S(2)}) %all-to-all-start) | async-done | bytes 196640 | tf_op jit(solution)/shard_map/all_to_all | solution.py:717
  55.2 1.4 %collective-permute-start.6 = (f32[8,128]{1,0:T(8,128)S(1)}, f32[8,128]{1,0:T(8,128)S(1)}, u32[]{:S(2)}, u32[]{:S(2)}) collective-permute-start(f32[8,128]{1,0:T(8,128)S(1)} %share.1.first), channel_id=1, source_target_pairs={{0,3},{1,0},{2,1},{3,2},{4,7},{5,4},{6,5},{7,6},{8,11},{9,8},{10,9... | collective-permute-start | bytes 12296 | tf_op jit(solution)/shard_map/ppermute | solution.py:755
  56.6 1.8 %collective-permute-start.5 = (f32[8,128]{1,0:T(8,128)S(1)}, f32[8,128]{1,0:T(8,128)S(1)}, u32[]{:S(2)}, u32[]{:S(2)}) collective-permute-start(f32[8,128]{1,0:T(8,128)S(1)} %share.1.first), channel_id=1, source_target_pairs={{0,2},{1,3},{2,0},{3,1},{4,6},{5,7},{6,4},{7,5},{8,10},{9,11},{10,... | collective-permute-start | bytes 12296 | tf_op jit(solution)/shard_map/ppermute | solution.py:755
  58.4 0.4 collective-permute-start.4
  58.8 1.8 %collective-permute-done.5.third = f32[8,128]{1,0:T(8,128)S(1)} collective-permute-done((f32[8,128]{1,0:T(8,128)S(1)}, f32[8,128]{1,0:T(8,128)S(1)}, u32[]{:S(2)}, u32[]{:S(2)}) %collective-permute-start.5) | collective-permute-done | bytes 4128 | tf_op jit(solution)/shard_map/ppermute | solution.py:755
  60.5 1.5 %collective-permute-done.4.second = f32[8,128]{1,0:T(8,128)S(1)} collective-permute-done((f32[8,128]{1,0:T(8,128)S(1)}, f32[8,128]{1,0:T(8,128)S(1)}, u32[]{:S(2)}, u32[]{:S(2)}) %collective-permute-start.4) | collective-permute-done | bytes 4128 | tf_op jit(solution)/shard_map/ppermute | solution.py:755
  62.1 0.7 advance.1
  62.8 9.0 %all-to-all-start.1 = ((f32[64,1,768]{2,1,0:T(1,128)}), f32[64,1,768]{2,1,0:T(1,128)S(1)}, u32[]{:S(2)}, u32[]{:S(2)}) async-start(f32[64,1,768]{2,1,0:T(1,128)} %bitcast.11), calls=%async_computation.1 | async-start | bytes 393216 | tf_op jit(solution)/shard_map/all_to_all | solution.py:770
  71.8 8.4 %accel.1 = f32[4,3,8,128]{3,2,1,0:T(8,128)} custom-call(s32[6,4,8]{2,1,0:T(4,128)S(1)} %bitcast.26, f32[8,12,8,128]{3,2,1,0:T(8,128)S(1)} %get-tuple-element.29.ext, bf16[6,10,48,128]{3,2,1,0:T(8,128)(2,1)S(1)} %get-tuple-element.30.btab, bf16[6,10,48,128]{3,2,1,0:T(8,128)(2,1)S(1)} %get-tuple-element.31.ftab, ...), custom_call_target="tpu_custom_call" | custom-call | flops 47185920 | bytes 524288 | tf_op jit(solution)/shard_map/accel/pallas_call | solution.py:771
  80.3 2.5 %all-to-all-done.1 = f32[64,1,768]{2,1,0:T(1,128)S(1)} async-done(((f32[64,1,768]{2,1,0:T(1,128)}), f32[64,1,768]{2,1,0:T(1,128)S(1)}, u32[]{:S(2)}, u32[]{:S(2)}) %all-to-all-start.1) | async-done | bytes 196640 | tf_op jit(solution)/shard_map/all_to_all | solution.py:770
  82.8 3.0 %pick.1 = f32[3,4096]{1,0:T(4,128)} custom-call(f32[384,128]{1,0:T(8,128)S(1)} %bitcast.16, f32[3,4096]{1,0:T(4,128)S(1)} %copy-done.1, s32[32,128]{1,0:T(8,128)S(1)} %bitcast.20, s32[32,128]{1,0:T(8,128)S(1)} %bitcast.22), custom_call_target="tpu_custom_call" | custom-call | tf_op jit(solution)/shard_map/pick/pallas_call | solution.py:783
  (34 shorter events, 0.4 us)
Async XLA Ops:
  1.7 7.1 %collective-permute-start.1 = (f32[4,2,8,128]{3,2,1,0:T(8,128)S(1)}, f32[4,2,8,128]{3,2,1,0:T(8,128)S(1)}, u32[]{:S(2)}, u32[]{:S(2)}) collective-permute-start(f32[4,2,8,128]{3,2,1,0:T(8,128)S(1)} %get-tuple-element.39), channel_id=1, source_target_pairs={{4,0},{8,4},{12,8},{16,12},{20,16},{24,20},{28,24},{32,28},{36,32}... | collective-permute-start | bytes 98312 | tf_op jit(solution)/shard_map/ppermute | solution.py:632
  6.8 3.1 %collective-permute-start = (f32[4,2,8,128]{3,2,1,0:T(8,128)S(1)}, f32[4,2,8,128]{3,2,1,0:T(8,128)S(1)}, u32[]{:S(2)}, u32[]{:S(2)}) collective-permute-start(f32[4,2,8,128]{3,2,1,0:T(8,128)S(1)} %get-tuple-element.40), channel_id=1, source_target_pairs={{0,4},{4,8},{8,12},{12,16},{16,20},{20,24},{24,28},{28,32},{32,36}... | collective-permute-start | bytes 98312 | tf_op jit(solution)/shard_map/ppermute | solution.py:632
  9.9 6.8 %collective-permute-start.2 = (f32[2,12,8,128]{3,2,1,0:T(8,128)S(1)}, f32[2,12,8,128]{3,2,1,0:T(8,128)S(1)}, u32[]{:S(2)}, u32[]{:S(2)}) collective-permute-start(f32[2,12,8,128]{3,2,1,0:T(8,128)S(1)} %pad_maximum_fusion), channel_id=1, source_target_pairs={{0,1},{1,2},{2,3},{4,5},{5,6},{6,7},{8,9},{9,10},{10,11},{12,13},{... | collective-permute-start | bytes 294920 | tf_op jit(solution)/shard_map/ppermute | solution.py:632
  12.8 1.3 %copy-start.4 = (s32[4,8,6]{1,0,2:T(4,128)S(1)}, s32[4,8,6]{1,0,2:T(4,128)}, u32[]{:S(2)}) copy-start(s32[4,8,6]{1,0,2:T(4,128)} %param.12) | copy-start | bytes 2308
  12.8 6.0 %collective-permute-start.3 = (f32[2,12,8,128]{3,2,1,0:T(8,128)S(1)}, f32[2,12,8,128]{3,2,1,0:T(8,128)S(1)}, u32[]{:S(2)}, u32[]{:S(2)}) collective-permute-start(f32[2,12,8,128]{3,2,1,0:T(8,128)S(1)} %pad_maximum_fusion.1), channel_id=1, source_target_pairs={{1,0},{2,1},{3,2},{5,4},{6,5},{7,6},{9,8},{10,9},{11,10},{13,12},{... | collective-permute-start | bytes 294920 | tf_op jit(solution)/shard_map/ppermute | solution.py:632
  18.8 2.8 %copy-start = (f32[4,8,6,128]{3,1,2,0:T(8,128)S(1)}, f32[4,8,6,128]{3,1,2,0:T(8,128)}, u32[]{:S(2)}) copy-start(f32[4,8,6,128]{3,1,2,0:T(8,128)} %param.10) | copy-start | bytes 294916
  18.8 2.8 %copy-start.1 = (f32[3,4096]{1,0:T(4,128)S(1)}, f32[3,4096]{1,0:T(4,128)}, u32[]{:S(2)}) copy-start(f32[3,4096]{1,0:T(4,128)} %place.3) | copy-start | bytes 147460
  18.8 2.8 %copy-start.2 = (s32[4096,1]{0,1:T(1,128)S(1)}, s32[4096,1]{0,1:T(1,128)}, u32[]{:S(2)}) copy-start(s32[4096,1]{0,1:T(1,128)} %param.16) | copy-start | bytes 49156
  18.8 2.8 %copy-start.3 = (s32[4096]{0:T(1024)S(1)}, s32[4096]{0:T(1024)}, u32[]{:S(2)}) copy-start(s32[4096]{0:T(1024)} %param.17) | copy-start | bytes 49156
  18.8 2.8 %copy-start.7 = (f32[3,4096]{1,0:T(4,128)S(1)}, f32[3,4096]{1,0:T(4,128)}, u32[]{:S(2)}) copy-start(f32[3,4096]{1,0:T(4,128)} %speed.1) | copy-start | bytes 147460
  18.8 2.8 %copy-start.8 = (s32[4096]{0:T(1024)S(1)}, s32[4096]{0:T(1024)}, u32[]{:S(2)}) copy-start(s32[4096]{0:T(1024)} %param.15) | copy-start | bytes 49156
  29.9 25.3 %all-to-all-start = ((f32[64,1,768]{2,1,0:T(1,128)}), f32[64,1,768]{2,1,0:T(1,128)S(1)}, u32[]{:S(2)}, u32[]{:S(2)}) async-start(f32[64,1,768]{2,1,0:T(1,128)} %bitcast.5), calls=%async_computation | async-start | bytes 393216 | tf_op jit(solution)/shard_map/all_to_all | solution.py:717
  55.2 6.9 %copy-start.5 = (f32[9,128]{1,0:T(8,128)S(1)}, f32[9,128]{1,0:T(8,128)}, u32[]{:S(2)}) copy-start(f32[9,128]{1,0:T(8,128)} %state.1) | copy-start | bytes 13828
  55.2 6.9 %copy-start.6 = (f32[4,128]{1,0:T(4,128)S(1)}, f32[4,128]{1,0:T(4,128)}, u32[]{:S(2)}) copy-start(f32[4,128]{1,0:T(4,128)} %inertia.1) | copy-start | bytes 6148
  55.2 3.6 %collective-permute-start.6 = (f32[8,128]{1,0:T(8,128)S(1)}, f32[8,128]{1,0:T(8,128)S(1)}, u32[]{:S(2)}, u32[]{:S(2)}) collective-permute-start(f32[8,128]{1,0:T(8,128)S(1)} %share.1.first), channel_id=1, source_target_pairs={{0,3},{1,0},{2,1},{3,2},{4,7},{5,4},{6,5},{7,6},{8,11},{9,8},{10,9... | collective-permute-start | bytes 12296 | tf_op jit(solution)/shard_map/ppermute | solution.py:755
  56.6 4.0 %collective-permute-start.5 = (f32[8,128]{1,0:T(8,128)S(1)}, f32[8,128]{1,0:T(8,128)S(1)}, u32[]{:S(2)}, u32[]{:S(2)}) collective-permute-start(f32[8,128]{1,0:T(8,128)S(1)} %share.1.first), channel_id=1, source_target_pairs={{0,2},{1,3},{2,0},{3,1},{4,6},{5,7},{6,4},{7,5},{8,10},{9,11},{10,... | collective-permute-start | bytes 12296 | tf_op jit(solution)/shard_map/ppermute | solution.py:755
  58.4 3.7 %collective-permute-start.4 = (f32[8,128]{1,0:T(8,128)S(1)}, f32[8,128]{1,0:T(8,128)S(1)}, u32[]{:S(2)}, u32[]{:S(2)}) collective-permute-start(f32[8,128]{1,0:T(8,128)S(1)} %share.1.first), channel_id=1, source_target_pairs={{0,1},{1,2},{2,3},{3,0},{4,5},{5,6},{6,7},{7,4},{8,9},{9,10},{10,1... | collective-permute-start | bytes 12296 | tf_op jit(solution)/shard_map/ppermute | solution.py:755
  62.8 20.0 %all-to-all-start.1 = ((f32[64,1,768]{2,1,0:T(1,128)}), f32[64,1,768]{2,1,0:T(1,128)S(1)}, u32[]{:S(2)}, u32[]{:S(2)}) async-start(f32[64,1,768]{2,1,0:T(1,128)} %bitcast.11), calls=%async_computation.1 | async-start | bytes 393216 | tf_op jit(solution)/shard_map/all_to_all | solution.py:770

commit v6 on v5

--- a/solution.py
+++ b/solution.py
@@ -20,7 +20,7 @@
 FACTORS = 48
 TILES = 10
 ONEHOT = 9
-PICK = 4
+PICK = 8
 SCALE = (2.0 * 1.4426950408889634) ** 0.5
 FAR = 1e30
 PLACE_LIMIT = 4.0
@@ -552,11 +552,16 @@
         moment = cross(where, force)
         return jnp.concatenate(force + moment + [jnp.zeros((2, wide), F32)], axis=0)
 
-    def step(pair, terms):
-        add_terms(jnp.maximum(pair - 1, 0), terms)
-        return forces_on(pair)
-
-    terms = lax.fori_loop(0, pairs, step, jnp.zeros((8, 2 * TP), F32))
+    def step(turn, terms):
+        first, second = terms
+        ahead = forces_on(2 * turn)
+        add_terms(jnp.maximum(2 * turn - 1, 0), second)
+        behind = forces_on(2 * turn + 1)
+        add_terms(2 * turn, ahead)
+        return ahead, behind
+
+    blank = jnp.zeros((8, 2 * TP), F32)
+    _, terms = lax.fori_loop(0, pairs // 2, step, (blank, blank))
     add_terms(pairs - 1, terms)
 
 

time: 86.2 us -> 84 us (0.974)
  Pallas kernels: 34.4 us -> 32.3 us
    pallas_call x1, Pallas kernels: 8.31 us -> 6.44 us  [local(): pl.pallas_call(marker_kernel, out_shape=jax.ShapeDtypeStruct((tile_devs *...]
where the time goes in v6:
time: 84 us; the launch traced here: 83.6 us
  starting transfers between devices  38.1 us (45%)
  Pallas kernels  32.3 us (38%)
  waiting for transfers between devices  11.9 us (14%)
  between operations  0.86 us (1%)
    all_to_all x1, starting transfers between devices, local(): lax.all_to_all(partial_sums.reshape(flat), 'tile', 0, 0, tiled=True)  14.3 us
    ppermute x4, starting transfers between devices, shifted(): return (lax.ppermute(last, axis, up), lax.ppermute(first, axis, down))  11.2 us
    all_to_all x1, starting transfers between devices, local(): states = lax.all_to_all(sent.reshape(flat), 'tile', 0, 0, tiled=True)  9.06 us
    pallas_call x1, Pallas kernels, local(): pl.pallas_call(accel_kernel, out_shape=jax.ShapeDtypeStruct((layers, 3, c...  8.44 us
    pallas_call x1, Pallas kernels, local(): pl.pallas_call(ring_kernel, out_shape=shapes, in_specs=[sspec()] + [vspec...  7.58 us
    pallas_call x1, Pallas kernels, local(): pl.pallas_call(marker_kernel, out_shape=jax.ShapeDtypeStruct((tile_devs *...  6.44 us
    ppermute x3, starting transfers between devices, local(): lax.ppermute(share, 'depth', [(i, (i + k) % depth_devs) for i in range(de...  3.56 us
    ppermute x3, waiting for transfers between devices, local(): lax.ppermute(share, 'depth', [(i, (i + k) % depth_devs) for i in range(de...  3.27 us
  transfers between devices with their start and end apart: 9, of which 6 were waited for; matrix products, arithmetic and copies ran while one was open for 0% of the time, Pallas kernels for 22%

profile of v6, /device:TPU:1, one launch (start us, length us, event | category | flops | bytes accessed | tf_op | source)
XLA Modules:
  0.0 83.6 jit_solution(9288592421656317757)
XLA Ops:
  0.6 1.0 %prep.1.own = f32[4,8,8,128]{3,2,1,0:T(8,128)S(1)} custom-call(s32[4,8]{1,0:T(4,128)} %counts_in.1, s32[6,4,8]{2,1,0:T(4,128)} %bitcast.23, f32[4,6,8,128]{3,2,1,0:T(8,128)} %bitcast.17), custom_call_target="tpu_custom_call" | custom-call | tf_op jit(solution)/shard_map/prep/pallas_call | solution.py:658
  1.7 5.1 %collective-permute-start.1 = (f32[4,2,8,128]{3,2,1,0:T(8,128)S(1)}, f32[4,2,8,128]{3,2,1,0:T(8,128)S(1)}, u32[]{:S(2)}, u32[]{:S(2)}) collective-permute-start(f32[4,2,8,128]{3,2,1,0:T(8,128)S(1)} %get-tuple-element.39), channel_id=1, source_target_pairs={{4,0},{8,4},{12,8},{16,12},{20,16},{24,20},{28,24},{32,28},{36,32}... | collective-permute-start | bytes 98312 | tf_op jit(solution)/shard_map/ppermute | solution.py:637
  6.8 1.9 %collective-permute-start = (f32[4,2,8,128]{3,2,1,0:T(8,128)S(1)}, f32[4,2,8,128]{3,2,1,0:T(8,128)S(1)}, u32[]{:S(2)}, u32[]{:S(2)}) collective-permute-start(f32[4,2,8,128]{3,2,1,0:T(8,128)S(1)} %get-tuple-element.40), channel_id=1, source_target_pairs={{0,4},{4,8},{8,12},{12,16},{16,20},{20,24},{24,28},{28,32},{32,36}... | collective-permute-start | bytes 98312 | tf_op jit(solution)/shard_map/ppermute | solution.py:637
  8.8 1.1 %collective-permute-done.west = f32[4,2,8,128]{3,2,1,0:T(8,128)S(1)} collective-permute-done((f32[4,2,8,128]{3,2,1,0:T(8,128)S(1)}, f32[4,2,8,128]{3,2,1,0:T(8,128)S(1)}, u32[]{:S(2)}, u32[]{:S(2)}) %collective-permute-start) | collective-permute-done | bytes 32800 | tf_op jit(solution)/shard_map/ppermute | solution.py:637
  9.9 2.8 %collective-permute-start.2 = (f32[2,12,8,128]{3,2,1,0:T(8,128)S(1)}, f32[2,12,8,128]{3,2,1,0:T(8,128)S(1)}, u32[]{:S(2)}, u32[]{:S(2)}) collective-permute-start(f32[2,12,8,128]{3,2,1,0:T(8,128)S(1)} %pad_maximum_fusion), channel_id=1, source_target_pairs={{0,1},{1,2},{2,3},{4,5},{5,6},{6,7},{8,9},{9,10},{10,11},{12,13},{... | collective-permute-start | bytes 294920 | tf_op jit(solution)/shard_map/ppermute | solution.py:637
  12.8 1.3 %collective-permute-start.3 = (f32[2,12,8,128]{3,2,1,0:T(8,128)S(1)}, f32[2,12,8,128]{3,2,1,0:T(8,128)S(1)}, u32[]{:S(2)}, u32[]{:S(2)}) collective-permute-start(f32[2,12,8,128]{3,2,1,0:T(8,128)S(1)} %pad_maximum_fusion.1), channel_id=1, source_target_pairs={{1,0},{2,1},{3,2},{5,4},{6,5},{7,6},{9,8},{10,9},{11,10},{13,12},{... | collective-permute-start | bytes 294920 | tf_op jit(solution)/shard_map/ppermute | solution.py:637
  14.1 2.6 %inner.1 = (bf16[4,8,128,48]{3,2,1,0:T(8,128)(2,1)S(1)}, f32[4,8,128]{2,1,0:T(8,128)S(1)}) custom-call(s32[6,4,8]{2,1,0:T(4,128)S(1)} %bitcast.24, f32[4,8,8,128]{3,2,1,0:T(8,128)S(1)} %prep.1.own), custom_call_target="tpu_custom_call" | custom-call | flops 4000000 | bytes 262144 | tf_op jit(solution)/shard_map/inner/pallas_call | solution.py:672
  16.8 2.0 %collective-permute-done.3.down = f32[2,12,8,128]{3,2,1,0:T(8,128)S(1)} collective-permute-done((f32[2,12,8,128]{3,2,1,0:T(8,128)S(1)}, f32[2,12,8,128]{3,2,1,0:T(8,128)S(1)}, u32[]{:S(2)}, u32[]{:S(2)}) %collective-permute-start.3) | collective-permute-done | bytes 98336 | tf_op jit(solution)/shard_map/ppermute | solution.py:637
  18.8 2.7 %density.1.extra = f32[4,32,128]{2,1,0:T(8,128)S(1)} custom-call(s32[6,4,8]{2,1,0:T(4,128)S(1)} %bitcast.25, f32[4,8,8,128]{3,2,1,0:T(8,128)S(1)} %prep.1.own, f32[4,2,8,128]{3,2,1,0:T(8,128)S(1)} %collective-permute-done.west, f32[4,2,8,128]{3,2,1,0:T(8,128)S(1)} %collective-permute-done.1.east, f32[2,12,8,128]{3,2,1,0:T(8,128)S(1)} %collective-permute-done.2.up, ...), custom_call_target="tpu_custom_call" | custom-call | flops 37748736 | bytes 262144 | tf_op jit(solution)/shard_map/density/pallas_call | solution.py:693
  21.6 6.4 %markers.1 = f32[384,128]{1,0:T(8,128)} custom-call(f32[4,6,8,128]{3,2,1,0:T(8,128)S(1)} %bitcast.18, f32[4,32,128]{2,1,0:T(8,128)S(1)} %density.1.extra, f32[3,4096]{1,0:T(4,128)S(1)} %copy-done.1, f32[3,4096]{1,0:T(4,128)S(1)} %copy-done.7, s32[32,128]{1,0:T(8,128)S(1)} %bitcast.27, s32[32,128]{1,0:T(8,128)S(1)} %bitcast.19, s32[32,128]{1,0:T(8,128)S(1)} %bitcast.21), custom_call_target="tpu_custom_call" | custom-call | flops 13107200 | bytes 524288 | tf_op jit(solution)/shard_map/markers/pallas_call | solution.py:710
  28.1 14.3 %all-to-all-start = ((f32[64,1,768]{2,1,0:T(1,128)}), f32[64,1,768]{2,1,0:T(1,128)S(1)}, u32[]{:S(2)}, u32[]{:S(2)}) async-start(f32[64,1,768]{2,1,0:T(1,128)} %bitcast.5), calls=%async_computation | async-start | bytes 393216 | tf_op jit(solution)/shard_map/all_to_all | solution.py:722
  42.4 0.1 copy.28
  42.8 7.6 %ring.1 = (f32[8,12,8,128]{3,2,1,0:T(8,128)S(1)}, bf16[6,10,48,128]{3,2,1,0:T(8,128)(2,1)S(1)}, bf16[6,10,48,128]{3,2,1,0:T(8,128)(2,1)S(1)}, f32[6,16,128]{2,1,0:T(8,128)S(1)}, f32[6,16,128]{2,1,0:T(8,128)S(1)}) custom-call(s32[6,8,12]{2,1,0:T(8,128)S(1)} %fusion.codes, f32[4,8,8,128]{3,2,1,0:T(8,128)S(1)} %prep.1.own, ...), custom_call_target="tpu_custom_call" | custom-call | flops 47185920 | bytes 524288 | tf_op jit(solution)/shard_map/ring/pallas_call | solution.py:739
  50.4 3.0 %all-to-all-done = f32[64,1,768]{2,1,0:T(1,128)S(1)} async-done(((f32[64,1,768]{2,1,0:T(1,128)}), f32[64,1,768]{2,1,0:T(1,128)S(1)}, u32[]{:S(2)}, u32[]{:S(2)}) %all-to-all-start) | async-done | bytes 196640 | tf_op jit(solution)/shard_map/all_to_all | solution.py:722
  53.3 1.4 %collective-permute-start.6 = (f32[8,128]{1,0:T(8,128)S(1)}, f32[8,128]{1,0:T(8,128)S(1)}, u32[]{:S(2)}, u32[]{:S(2)}) collective-permute-start(f32[8,128]{1,0:T(8,128)S(1)} %share.1.first), channel_id=1, source_target_pairs={{0,3},{1,0},{2,1},{3,2},{4,7},{5,4},{6,5},{7,6},{8,11},{9,8},{10,9... | collective-permute-start | bytes 12296 | tf_op jit(solution)/shard_map/ppermute | solution.py:760
  54.7 1.8 %collective-permute-start.5 = (f32[8,128]{1,0:T(8,128)S(1)}, f32[8,128]{1,0:T(8,128)S(1)}, u32[]{:S(2)}, u32[]{:S(2)}) collective-permute-start(f32[8,128]{1,0:T(8,128)S(1)} %share.1.first), channel_id=1, source_target_pairs={{0,2},{1,3},{2,0},{3,1},{4,6},{5,7},{6,4},{7,5},{8,10},{9,11},{10,... | collective-permute-start | bytes 12296 | tf_op jit(solution)/shard_map/ppermute | solution.py:760
  56.5 0.4 collective-permute-start.4
  56.9 1.8 %collective-permute-done.5.third = f32[8,128]{1,0:T(8,128)S(1)} collective-permute-done((f32[8,128]{1,0:T(8,128)S(1)}, f32[8,128]{1,0:T(8,128)S(1)}, u32[]{:S(2)}, u32[]{:S(2)}) %collective-permute-start.5) | collective-permute-done | bytes 4128 | tf_op jit(solution)/shard_map/ppermute | solution.py:760
  58.7 1.5 %collective-permute-done.4.second = f32[8,128]{1,0:T(8,128)S(1)} collective-permute-done((f32[8,128]{1,0:T(8,128)S(1)}, f32[8,128]{1,0:T(8,128)S(1)}, u32[]{:S(2)}, u32[]{:S(2)}) %collective-permute-start.4) | collective-permute-done | bytes 4128 | tf_op jit(solution)/shard_map/ppermute | solution.py:760
  60.2 0.7 advance.1
  60.9 9.1 %all-to-all-start.1 = ((f32[64,1,768]{2,1,0:T(1,128)}), f32[64,1,768]{2,1,0:T(1,128)S(1)}, u32[]{:S(2)}, u32[]{:S(2)}) async-start(f32[64,1,768]{2,1,0:T(1,128)} %bitcast.11), calls=%async_computation.1 | async-start | bytes 393216 | tf_op jit(solution)/shard_map/all_to_all | solution.py:775
  70.0 8.4 %accel.1 = f32[4,3,8,128]{3,2,1,0:T(8,128)} custom-call(s32[6,4,8]{2,1,0:T(4,128)S(1)} %bitcast.26, f32[8,12,8,128]{3,2,1,0:T(8,128)S(1)} %get-tuple-element.29.ext, bf16[6,10,48,128]{3,2,1,0:T(8,128)(2,1)S(1)} %get-tuple-element.30.btab, bf16[6,10,48,128]{3,2,1,0:T(8,128)(2,1)S(1)} %get-tuple-element.31.ftab, ...), custom_call_target="tpu_custom_call" | custom-call | flops 47185920 | bytes 524288 | tf_op jit(solution)/shard_map/accel/pallas_call | solution.py:776
  78.4 2.5 %all-to-all-done.1 = f32[64,1,768]{2,1,0:T(1,128)S(1)} async-done(((f32[64,1,768]{2,1,0:T(1,128)}), f32[64,1,768]{2,1,0:T(1,128)S(1)}, u32[]{:S(2)}, u32[]{:S(2)}) %all-to-all-start.1) | async-done | bytes 196640 | tf_op jit(solution)/shard_map/all_to_all | solution.py:775
  80.9 2.7 %pick.1 = f32[3,4096]{1,0:T(4,128)} custom-call(f32[384,128]{1,0:T(8,128)S(1)} %bitcast.16, f32[3,4096]{1,0:T(4,128)S(1)} %copy-done.1, s32[32,128]{1,0:T(8,128)S(1)} %bitcast.20, s32[32,128]{1,0:T(8,128)S(1)} %bitcast.22), custom_call_target="tpu_custom_call" | custom-call | tf_op jit(solution)/shard_map/pick/pallas_call | solution.py:788
  (34 shorter events, 0.4 us)
Async XLA Ops:
  1.7 7.1 %collective-permute-start.1 = (f32[4,2,8,128]{3,2,1,0:T(8,128)S(1)}, f32[4,2,8,128]{3,2,1,0:T(8,128)S(1)}, u32[]{:S(2)}, u32[]{:S(2)}) collective-permute-start(f32[4,2,8,128]{3,2,1,0:T(8,128)S(1)} %get-tuple-element.39), channel_id=1, source_target_pairs={{4,0},{8,4},{12,8},{16,12},{20,16},{24,20},{28,24},{32,28},{36,32}... | collective-permute-start | bytes 98312 | tf_op jit(solution)/shard_map/ppermute | solution.py:637
  6.8 3.1 %collective-permute-start = (f32[4,2,8,128]{3,2,1,0:T(8,128)S(1)}, f32[4,2,8,128]{3,2,1,0:T(8,128)S(1)}, u32[]{:S(2)}, u32[]{:S(2)}) collective-permute-start(f32[4,2,8,128]{3,2,1,0:T(8,128)S(1)} %get-tuple-element.40), channel_id=1, source_target_pairs={{0,4},{4,8},{8,12},{12,16},{16,20},{20,24},{24,28},{28,32},{32,36}... | collective-permute-start | bytes 98312 | tf_op jit(solution)/shard_map/ppermute | solution.py:637
  9.9 6.8 %collective-permute-start.2 = (f32[2,12,8,128]{3,2,1,0:T(8,128)S(1)}, f32[2,12,8,128]{3,2,1,0:T(8,128)S(1)}, u32[]{:S(2)}, u32[]{:S(2)}) collective-permute-start(f32[2,12,8,128]{3,2,1,0:T(8,128)S(1)} %pad_maximum_fusion), channel_id=1, source_target_pairs={{0,1},{1,2},{2,3},{4,5},{5,6},{6,7},{8,9},{9,10},{10,11},{12,13},{... | collective-permute-start | bytes 294920 | tf_op jit(solution)/shard_map/ppermute | solution.py:637
  12.8 1.3 %copy-start.4 = (s32[4,8,6]{1,0,2:T(4,128)S(1)}, s32[4,8,6]{1,0,2:T(4,128)}, u32[]{:S(2)}) copy-start(s32[4,8,6]{1,0,2:T(4,128)} %param.12) | copy-start | bytes 2308
  12.8 6.0 %collective-permute-start.3 = (f32[2,12,8,128]{3,2,1,0:T(8,128)S(1)}, f32[2,12,8,128]{3,2,1,0:T(8,128)S(1)}, u32[]{:S(2)}, u32[]{:S(2)}) collective-permute-start(f32[2,12,8,128]{3,2,1,0:T(8,128)S(1)} %pad_maximum_fusion.1), channel_id=1, source_target_pairs={{1,0},{2,1},{3,2},{5,4},{6,5},{7,6},{9,8},{10,9},{11,10},{13,12},{... | collective-permute-start | bytes 294920 | tf_op jit(solution)/shard_map/ppermute | solution.py:637
  18.8 2.8 %copy-start = (f32[4,8,6,128]{3,1,2,0:T(8,128)S(1)}, f32[4,8,6,128]{3,1,2,0:T(8,128)}, u32[]{:S(2)}) copy-start(f32[4,8,6,128]{3,1,2,0:T(8,128)} %param.10) | copy-start | bytes 294916
  18.8 2.8 %copy-start.1 = (f32[3,4096]{1,0:T(4,128)S(1)}, f32[3,4096]{1,0:T(4,128)}, u32[]{:S(2)}) copy-start(f32[3,4096]{1,0:T(4,128)} %place.3) | copy-start | bytes 147460
  18.8 2.8 %copy-start.2 = (s32[4096,1]{0,1:T(1,128)S(1)}, s32[4096,1]{0,1:T(1,128)}, u32[]{:S(2)}) copy-start(s32[4096,1]{0,1:T(1,128)} %param.16) | copy-start | bytes 49156
  18.8 2.8 %copy-start.3 = (s32[4096]{0:T(1024)S(1)}, s32[4096]{0:T(1024)}, u32[]{:S(2)}) copy-start(s32[4096]{0:T(1024)} %param.17) | copy-start | bytes 49156
  18.8 2.8 %copy-start.7 = (f32[3,4096]{1,0:T(4,128)S(1)}, f32[3,4096]{1,0:T(4,128)}, u32[]{:S(2)}) copy-start(f32[3,4096]{1,0:T(4,128)} %speed.1) | copy-start | bytes 147460
  18.8 2.8 %copy-start.8 = (s32[4096]{0:T(1024)S(1)}, s32[4096]{0:T(1024)}, u32[]{:S(2)}) copy-start(s32[4096]{0:T(1024)} %param.15) | copy-start | bytes 49156
  28.1 25.3 %all-to-all-start = ((f32[64,1,768]{2,1,0:T(1,128)}), f32[64,1,768]{2,1,0:T(1,128)S(1)}, u32[]{:S(2)}, u32[]{:S(2)}) async-start(f32[64,1,768]{2,1,0:T(1,128)} %bitcast.5), calls=%async_computation | async-start | bytes 393216 | tf_op jit(solution)/shard_map/all_to_all | solution.py:722
  53.3 6.9 %copy-start.5 = (f32[9,128]{1,0:T(8,128)S(1)}, f32[9,128]{1,0:T(8,128)}, u32[]{:S(2)}) copy-start(f32[9,128]{1,0:T(8,128)} %state.1) | copy-start | bytes 13828
  53.3 6.9 %copy-start.6 = (f32[4,128]{1,0:T(4,128)S(1)}, f32[4,128]{1,0:T(4,128)}, u32[]{:S(2)}) copy-start(f32[4,128]{1,0:T(4,128)} %inertia.1) | copy-start | bytes 6148
  53.3 3.6 %collective-permute-start.6 = (f32[8,128]{1,0:T(8,128)S(1)}, f32[8,128]{1,0:T(8,128)S(1)}, u32[]{:S(2)}, u32[]{:S(2)}) collective-permute-start(f32[8,128]{1,0:T(8,128)S(1)} %share.1.first), channel_id=1, source_target_pairs={{0,3},{1,0},{2,1},{3,2},{4,7},{5,4},{6,5},{7,6},{8,11},{9,8},{10,9... | collective-permute-start | bytes 12296 | tf_op jit(solution)/shard_map/ppermute | solution.py:760
  54.7 4.0 %collective-permute-start.5 = (f32[8,128]{1,0:T(8,128)S(1)}, f32[8,128]{1,0:T(8,128)S(1)}, u32[]{:S(2)}, u32[]{:S(2)}) collective-permute-start(f32[8,128]{1,0:T(8,128)S(1)} %share.1.first), channel_id=1, source_target_pairs={{0,2},{1,3},{2,0},{3,1},{4,6},{5,7},{6,4},{7,5},{8,10},{9,11},{10,... | collective-permute-start | bytes 12296 | tf_op jit(solution)/shard_map/ppermute | solution.py:760
  56.5 3.7 %collective-permute-start.4 = (f32[8,128]{1,0:T(8,128)S(1)}, f32[8,128]{1,0:T(8,128)S(1)}, u32[]{:S(2)}, u32[]{:S(2)}) collective-permute-start(f32[8,128]{1,0:T(8,128)S(1)} %share.1.first), channel_id=1, source_target_pairs={{0,1},{1,2},{2,3},{3,0},{4,5},{5,6},{6,7},{7,4},{8,9},{9,10},{10,1... | collective-permute-start | bytes 12296 | tf_op jit(solution)/shard_map/ppermute | solution.py:760
  60.9 20.0 %all-to-all-start.1 = ((f32[64,1,768]{2,1,0:T(1,128)}), f32[64,1,768]{2,1,0:T(1,128)S(1)}, u32[]{:S(2)}, u32[]{:S(2)}) async-start(f32[64,1,768]{2,1,0:T(1,128)} %bitcast.11), calls=%async_computation.1 | async-start | bytes 393216 | tf_op jit(solution)/shard_map/all_to_all | solution.py:775

commit v7 on v6

--- a/solution.py
+++ b/solution.py
@@ -237,9 +237,8 @@
     return layer, column
 
 
-def inner_kernel(codes, own, lefts, sums, btab):
+def turn_kernel(own, lefts, btab):
     layers, columns = own.shape[0], own.shape[1]
-    eye = eye_mask()
     fill_sources(own, btab, 0, layers, 0, columns)
 
     def turn(layer, carry):
@@ -248,6 +247,11 @@
         return carry
 
     lax.fori_loop(0, layers, turn, 0)
+
+
+def inner_kernel(codes, lefts, btab, sums):
+    layers, columns = lefts.shape[0], lefts.shape[1]
+    eye = eye_mask()
 
     def step(layer, carry):
         for column in range(1, columns - 1):
@@ -259,7 +263,9 @@
     lax.fori_loop(1, layers - 1, step, 0)
 
 
-def density_kernel(codes, own, west, east, up, down, lefts, inner, out, ext, btab, sums):
+def density_kernel(
+    codes, own, west, east, up, down, lefts, mine, inner, out, ext, btab, sums
+):
     layers, columns = own.shape[0], own.shape[1]
     assemble(own, west, east, up, down, ext)
     eye = eye_mask()
@@ -268,7 +274,11 @@
 
     @pl.when(fast)
     def _():
-        fill_sources(ext, btab, 1, layers + 3, 1, columns + 3)
+        btab[2 : layers + 2, 2 : columns + 2] = mine[...]
+        for row in range(1, layers + 3):
+            edge = row in (1, layers + 2)
+            for col in range(1, columns + 3) if edge else (1, columns + 2):
+                btab[row, col] = augmented(ext[row, col], True).astype(BF16)
         rim = 2 * columns + 2 * (layers - 2)
 
         def step(group, carry):
@@ -669,20 +679,29 @@
         compiler_params=params(),
         name="prep",
     )(*[pltpu.with_memory_space_constraint(x, pltpu.HBM) for x in (tile_count, codes, soil)])
-    lefts, inner = pl.pallas_call(
-        inner_kernel,
+    west, east = shifted(own, "tile", 1, 2)
+    lefts, mine = pl.pallas_call(
+        turn_kernel,
         out_shape=(
             jax.ShapeDtypeStruct((layers, columns, TP, AUG), BF16),
-            jax.ShapeDtypeStruct((layers, columns, TP), F32),
+            jax.ShapeDtypeStruct((layers, columns, AUG, TP), BF16),
         ),
-        in_specs=[sspec(), vspec()],
+        in_specs=[vspec()],
         out_specs=(vspec(), vspec()),
-        scratch_shapes=[VMEM((layers, columns, AUG, TP), BF16)],
+        cost_estimate=cost(1_000_000, 1 << 18),
+        compiler_params=params(),
+        name="turn",
+    )(own)
+    west, east, mine = lax.optimization_barrier((west, east, mine))
+    inner = pl.pallas_call(
+        inner_kernel,
+        out_shape=jax.ShapeDtypeStruct((layers, columns, TP), F32),
+        in_specs=[sspec(), vspec(), vspec()],
+        out_specs=vspec(),
         cost_estimate=cost(4_000_000, 1 << 18, 1_000_000),
         compiler_params=params(),
         name="inner",
-    )(codes, own)
-    west, east = shifted(own, "tile", 1, 2)
+    )(codes, lefts, mine)
     top = jnp.concatenate([west[:2], own[:2], east[:2]], axis=1)
     bottom = jnp.concatenate([west[-2:], own[-2:], east[-2:]], axis=1)
     rim = jnp.concatenate([top, bottom], axis=0)
@@ -693,7 +712,7 @@
     extra = pl.pallas_call(
         density_kernel,
         out_shape=jax.ShapeDtypeStruct((4, layers * columns, TP), F32),
-        in_specs=[sspec()] + [vspec()] * 7,
+        in_specs=[sspec()] + [vspec()] * 8,
         out_specs=vspec(),
         scratch_shapes=[
             VMEM((span, width, 8, TP), F32),
@@ -703,7 +722,7 @@
         cost_estimate=cost(pairs * 12, 1 << 18, pairs),
         compiler_params=params(),
         name="density",
-    )(codes, *pieces, lefts, inner)
+    )(codes, *pieces, lefts, mine, inner)
     owners = marker_owner.reshape((marker_count // TP, TP))
     slots = marker_slot.reshape((marker_count // TP, TP))
     tiles = marker_tile.reshape((marker_count // TP, TP))

time: 84 us -> 83.8 us (level)
    pallas_call x1 -> x2, Pallas kernels: 2.62 us -> 2.61 us  [the longest x1 1.87 us: local(): pl.pallas_call(inner_kernel, out_shape=jax.ShapeDtypeStruct((layers, colu...]
where the time goes in v7:
time: 83.8 us; the launch traced here: 83.5 us
  starting transfers between devices  38.1 us (45%)
  Pallas kernels  32.1 us (38%)
  waiting for transfers between devices  11.9 us (14%)
  between operations  0.89 us (1%)
    all_to_all x1, starting transfers between devices, local(): lax.all_to_all(partial_sums.reshape(flat), 'tile', 0, 0, tiled=True)  14.3 us
    ppermute x4, starting transfers between devices, shifted(): return (lax.ppermute(last, axis, up), lax.ppermute(first, axis, down))  11.2 us
    all_to_all x1, starting transfers between devices, local(): states = lax.all_to_all(sent.reshape(flat), 'tile', 0, 0, tiled=True)  9.09 us
    pallas_call x1, Pallas kernels, local(): pl.pallas_call(accel_kernel, out_shape=jax.ShapeDtypeStruct((layers, 3, c...  8.44 us
    pallas_call x1, Pallas kernels, local(): pl.pallas_call(ring_kernel, out_shape=shapes, in_specs=[sspec()] + [vspec...  7.56 us
    pallas_call x1, Pallas kernels, local(): pl.pallas_call(marker_kernel, out_shape=jax.ShapeDtypeStruct((tile_devs *...  6.44 us
    ppermute x3, starting transfers between devices, local(): lax.ppermute(share, 'depth', [(i, (i + k) % depth_devs) for i in range(de...  3.56 us
    ppermute x3, waiting for transfers between devices, local(): lax.ppermute(share, 'depth', [(i, (i + k) % depth_devs) for i in range(de...  3.28 us
  transfers between devices with their start and end apart: 9, of which 6 were waited for; matrix products, arithmetic and copies ran while one was open for 0% of the time, Pallas kernels for 22%

profile of v7, /device:TPU:1, one launch (start us, length us, event | category | flops | bytes accessed | tf_op | source)
XLA Modules:
  0.0 83.5 jit_solution(367039204164726205)
XLA Ops:
  0.6 1.0 %prep.1.own = f32[4,8,8,128]{3,2,1,0:T(8,128)S(1)} custom-call(s32[4,8]{1,0:T(4,128)} %counts_in.1, s32[6,4,8]{2,1,0:T(4,128)} %bitcast.23, f32[4,6,8,128]{3,2,1,0:T(8,128)} %bitcast.17), custom_call_target="tpu_custom_call" | custom-call | tf_op jit(solution)/shard_map/prep/pallas_call | solution.py:668
  1.7 5.1 %collective-permute-start.1 = (f32[4,2,8,128]{3,2,1,0:T(8,128)S(1)}, f32[4,2,8,128]{3,2,1,0:T(8,128)S(1)}, u32[]{:S(2)}, u32[]{:S(2)}) collective-permute-start(f32[4,2,8,128]{3,2,1,0:T(8,128)S(1)} %get-tuple-element.45), channel_id=1, source_target_pairs={{4,0},{8,4},{12,8},{16,12},{20,16},{24,20},{28,24},{32,28},{36,32}... | collective-permute-start | bytes 98312 | tf_op jit(solution)/shard_map/ppermute | solution.py:647
  6.8 1.9 %collective-permute-start = (f32[4,2,8,128]{3,2,1,0:T(8,128)S(1)}, f32[4,2,8,128]{3,2,1,0:T(8,128)S(1)}, u32[]{:S(2)}, u32[]{:S(2)}) collective-permute-start(f32[4,2,8,128]{3,2,1,0:T(8,128)S(1)} %get-tuple-element.46), channel_id=1, source_target_pairs={{0,4},{4,8},{8,12},{12,16},{16,20},{20,24},{24,28},{28,32},{32,36}... | collective-permute-start | bytes 98312 | tf_op jit(solution)/shard_map/ppermute | solution.py:647
  8.8 0.7 turn.1
  9.5 0.4 collective-permute-done.west
  9.9 2.8 %collective-permute-start.2 = (f32[2,12,8,128]{3,2,1,0:T(8,128)S(1)}, f32[2,12,8,128]{3,2,1,0:T(8,128)S(1)}, u32[]{:S(2)}, u32[]{:S(2)}) collective-permute-start(f32[2,12,8,128]{3,2,1,0:T(8,128)S(1)} %pad_maximum_fusion), channel_id=1, source_target_pairs={{0,1},{1,2},{2,3},{4,5},{5,6},{6,7},{8,9},{9,10},{10,11},{12,13},{... | collective-permute-start | bytes 294920 | tf_op jit(solution)/shard_map/ppermute | solution.py:647
  12.8 1.3 %collective-permute-start.3 = (f32[2,12,8,128]{3,2,1,0:T(8,128)S(1)}, f32[2,12,8,128]{3,2,1,0:T(8,128)S(1)}, u32[]{:S(2)}, u32[]{:S(2)}) collective-permute-start(f32[2,12,8,128]{3,2,1,0:T(8,128)S(1)} %pad_maximum_fusion.1), channel_id=1, source_target_pairs={{1,0},{2,1},{3,2},{5,4},{6,5},{7,6},{9,8},{10,9},{11,10},{13,12},{... | collective-permute-start | bytes 294920 | tf_op jit(solution)/shard_map/ppermute | solution.py:647
  14.1 1.9 %inner.1 = f32[4,8,128]{2,1,0:T(8,128)S(1)} custom-call(s32[6,4,8]{2,1,0:T(4,128)S(1)} %bitcast.24, bf16[4,8,128,48]{3,2,1,0:T(8,128)(2,1)S(1)} %get-tuple-element.26.lefts, bf16[4,8,48,128]{3,2,1,0:T(8,128)(2,1)S(1)} %get-tuple-element.27.btab.mine), custom_call_target="tpu_custom_call" | custom-call | flops 4000000 | bytes 262144 | tf_op jit(solution)/shard_map/inner/pallas_call | solution.py:696
  16.1 2.7 %collective-permute-done.3.down = f32[2,12,8,128]{3,2,1,0:T(8,128)S(1)} collective-permute-done((f32[2,12,8,128]{3,2,1,0:T(8,128)S(1)}, f32[2,12,8,128]{3,2,1,0:T(8,128)S(1)}, u32[]{:S(2)}, u32[]{:S(2)}) %collective-permute-start.3) | collective-permute-done | bytes 98336 | tf_op jit(solution)/shard_map/ppermute | solution.py:647
  18.8 2.6 %density.1.extra = f32[4,32,128]{2,1,0:T(8,128)S(1)} custom-call(s32[6,4,8]{2,1,0:T(4,128)S(1)} %bitcast.25, f32[4,8,8,128]{3,2,1,0:T(8,128)S(1)} %prep.1.own, f32[4,2,8,128]{3,2,1,0:T(8,128)S(1)} %collective-permute-done.west, f32[4,2,8,128]{3,2,1,0:T(8,128)S(1)} %collective-permute-done.1.east, f32[2,12,8,128]{3,2,1,0:T(8,128)S(1)} %collective-permute-done.2.up, ...), custom_call_target="tpu_custom_call" | custom-call | flops 37748736 | bytes 262144 | tf_op jit(solution)/shard_map/density/pallas_call | solution.py:712
  21.5 6.4 %markers.1 = f32[384,128]{1,0:T(8,128)} custom-call(f32[4,6,8,128]{3,2,1,0:T(8,128)S(1)} %bitcast.18, f32[4,32,128]{2,1,0:T(8,128)S(1)} %density.1.extra, f32[3,4096]{1,0:T(4,128)S(1)} %copy-done.1, f32[3,4096]{1,0:T(4,128)S(1)} %copy-done.7, s32[32,128]{1,0:T(8,128)S(1)} %bitcast.27, s32[32,128]{1,0:T(8,128)S(1)} %bitcast.19, s32[32,128]{1,0:T(8,128)S(1)} %bitcast.21), custom_call_target="tpu_custom_call" | custom-call | flops 13107200 | bytes 524288 | tf_op jit(solution)/shard_map/markers/pallas_call | solution.py:729
  27.9 14.3 %all-to-all-start = ((f32[64,1,768]{2,1,0:T(1,128)}), f32[64,1,768]{2,1,0:T(1,128)S(1)}, u32[]{:S(2)}, u32[]{:S(2)}) async-start(f32[64,1,768]{2,1,0:T(1,128)} %bitcast.5), calls=%async_computation | async-start | bytes 393216 | tf_op jit(solution)/shard_map/all_to_all | solution.py:741
  42.6 7.6 %ring.1 = (f32[8,12,8,128]{3,2,1,0:T(8,128)S(1)}, bf16[6,10,48,128]{3,2,1,0:T(8,128)(2,1)S(1)}, bf16[6,10,48,128]{3,2,1,0:T(8,128)(2,1)S(1)}, f32[6,16,128]{2,1,0:T(8,128)S(1)}, f32[6,16,128]{2,1,0:T(8,128)S(1)}) custom-call(s32[6,8,12]{2,1,0:T(8,128)S(1)} %fusion.codes, f32[4,8,8,128]{3,2,1,0:T(8,128)S(1)} %prep.1.own, ...), custom_call_target="tpu_custom_call" | custom-call | flops 47185920 | bytes 524288 | tf_op jit(solution)/shard_map/ring/pallas_call | solution.py:758
  50.2 3.0 %all-to-all-done = f32[64,1,768]{2,1,0:T(1,128)S(1)} async-done(((f32[64,1,768]{2,1,0:T(1,128)}), f32[64,1,768]{2,1,0:T(1,128)S(1)}, u32[]{:S(2)}, u32[]{:S(2)}) %all-to-all-start) | async-done | bytes 196640 | tf_op jit(solution)/shard_map/all_to_all | solution.py:741
  53.2 0.9 %collective-permute-start.6 = (f32[8,128]{1,0:T(8,128)S(1)}, f32[8,128]{1,0:T(8,128)S(1)}, u32[]{:S(2)}, u32[]{:S(2)}) collective-permute-start(f32[8,128]{1,0:T(8,128)S(1)} %share.1.first), channel_id=1, source_target_pairs={{0,3},{1,0},{2,1},{3,2},{4,7},{5,4},{6,5},{7,6},{8,11},{9,8},{10,9... | collective-permute-start | bytes 12296 | tf_op jit(solution)/shard_map/ppermute | solution.py:779
  54.0 2.3 %collective-permute-start.5 = (f32[8,128]{1,0:T(8,128)S(1)}, f32[8,128]{1,0:T(8,128)S(1)}, u32[]{:S(2)}, u32[]{:S(2)}) collective-permute-start(f32[8,128]{1,0:T(8,128)S(1)} %share.1.first), channel_id=1, source_target_pairs={{0,2},{1,3},{2,0},{3,1},{4,6},{5,7},{6,4},{7,5},{8,10},{9,11},{10,... | collective-permute-start | bytes 12296 | tf_op jit(solution)/shard_map/ppermute | solution.py:779
  56.3 0.4 collective-permute-start.4
  56.7 1.3 %collective-permute-done.5.third = f32[8,128]{1,0:T(8,128)S(1)} collective-permute-done((f32[8,128]{1,0:T(8,128)S(1)}, f32[8,128]{1,0:T(8,128)S(1)}, u32[]{:S(2)}, u32[]{:S(2)}) %collective-permute-start.5) | collective-permute-done | bytes 4128 | tf_op jit(solution)/shard_map/ppermute | solution.py:779
  58.0 2.0 %collective-permute-done.4.second = f32[8,128]{1,0:T(8,128)S(1)} collective-permute-done((f32[8,128]{1,0:T(8,128)S(1)}, f32[8,128]{1,0:T(8,128)S(1)}, u32[]{:S(2)}, u32[]{:S(2)}) %collective-permute-start.4) | collective-permute-done | bytes 4128 | tf_op jit(solution)/shard_map/ppermute | solution.py:779
  60.0 0.7 advance.1
  60.7 9.1 %all-to-all-start.1 = ((f32[64,1,768]{2,1,0:T(1,128)}), f32[64,1,768]{2,1,0:T(1,128)S(1)}, u32[]{:S(2)}, u32[]{:S(2)}) async-start(f32[64,1,768]{2,1,0:T(1,128)} %bitcast.11), calls=%async_computation.1 | async-start | bytes 393216 | tf_op jit(solution)/shard_map/all_to_all | solution.py:794
  69.8 8.4 %accel.1 = f32[4,3,8,128]{3,2,1,0:T(8,128)} custom-call(s32[6,4,8]{2,1,0:T(4,128)S(1)} %bitcast.26, f32[8,12,8,128]{3,2,1,0:T(8,128)S(1)} %get-tuple-element.35.ext, bf16[6,10,48,128]{3,2,1,0:T(8,128)(2,1)S(1)} %get-tuple-element.36.btab, bf16[6,10,48,128]{3,2,1,0:T(8,128)(2,1)S(1)} %get-tuple-element.37.ftab, ...), custom_call_target="tpu_custom_call" | custom-call | flops 47185920 | bytes 524288 | tf_op jit(solution)/shard_map/accel/pallas_call | solution.py:795
  78.3 2.5 %all-to-all-done.1 = f32[64,1,768]{2,1,0:T(1,128)S(1)} async-done(((f32[64,1,768]{2,1,0:T(1,128)}), f32[64,1,768]{2,1,0:T(1,128)S(1)}, u32[]{:S(2)}, u32[]{:S(2)}) %all-to-all-start.1) | async-done | bytes 196640 | tf_op jit(solution)/shard_map/all_to_all | solution.py:794
  80.8 2.7 %pick.1 = f32[3,4096]{1,0:T(4,128)} custom-call(f32[384,128]{1,0:T(8,128)S(1)} %bitcast.16, f32[3,4096]{1,0:T(4,128)S(1)} %copy-done.1, s32[32,128]{1,0:T(8,128)S(1)} %bitcast.20, s32[32,128]{1,0:T(8,128)S(1)} %bitcast.22), custom_call_target="tpu_custom_call" | custom-call | tf_op jit(solution)/shard_map/pick/pallas_call | solution.py:807
  (34 shorter events, 0.5 us)
Async XLA Ops:
  1.7 7.8 %collective-permute-start.1 = (f32[4,2,8,128]{3,2,1,0:T(8,128)S(1)}, f32[4,2,8,128]{3,2,1,0:T(8,128)S(1)}, u32[]{:S(2)}, u32[]{:S(2)}) collective-permute-start(f32[4,2,8,128]{3,2,1,0:T(8,128)S(1)} %get-tuple-element.45), channel_id=1, source_target_pairs={{4,0},{8,4},{12,8},{16,12},{20,16},{24,20},{28,24},{32,28},{36,32}... | collective-permute-start | bytes 98312 | tf_op jit(solution)/shard_map/ppermute | solution.py:647
  6.8 3.1 %collective-permute-start = (f32[4,2,8,128]{3,2,1,0:T(8,128)S(1)}, f32[4,2,8,128]{3,2,1,0:T(8,128)S(1)}, u32[]{:S(2)}, u32[]{:S(2)}) collective-permute-start(f32[4,2,8,128]{3,2,1,0:T(8,128)S(1)} %get-tuple-element.46), channel_id=1, source_target_pairs={{0,4},{4,8},{8,12},{12,16},{16,20},{20,24},{24,28},{28,32},{32,36}... | collective-permute-start | bytes 98312 | tf_op jit(solution)/shard_map/ppermute | solution.py:647
  9.9 6.1 %collective-permute-start.2 = (f32[2,12,8,128]{3,2,1,0:T(8,128)S(1)}, f32[2,12,8,128]{3,2,1,0:T(8,128)S(1)}, u32[]{:S(2)}, u32[]{:S(2)}) collective-permute-start(f32[2,12,8,128]{3,2,1,0:T(8,128)S(1)} %pad_maximum_fusion), channel_id=1, source_target_pairs={{0,1},{1,2},{2,3},{4,5},{5,6},{6,7},{8,9},{9,10},{10,11},{12,13},{... | collective-permute-start | bytes 294920 | tf_op jit(solution)/shard_map/ppermute | solution.py:647
  12.8 1.3 %copy-start.4 = (s32[4,8,6]{1,0,2:T(4,128)S(1)}, s32[4,8,6]{1,0,2:T(4,128)}, u32[]{:S(2)}) copy-start(s32[4,8,6]{1,0,2:T(4,128)} %param.12) | copy-start | bytes 2308
  12.8 6.0 %collective-permute-start.3 = (f32[2,12,8,128]{3,2,1,0:T(8,128)S(1)}, f32[2,12,8,128]{3,2,1,0:T(8,128)S(1)}, u32[]{:S(2)}, u32[]{:S(2)}) collective-permute-start(f32[2,12,8,128]{3,2,1,0:T(8,128)S(1)} %pad_maximum_fusion.1), channel_id=1, source_target_pairs={{1,0},{2,1},{3,2},{5,4},{6,5},{7,6},{9,8},{10,9},{11,10},{13,12},{... | collective-permute-start | bytes 294920 | tf_op jit(solution)/shard_map/ppermute | solution.py:647
  16.0 5.4 %copy-start = (f32[4,8,6,128]{3,1,2,0:T(8,128)S(1)}, f32[4,8,6,128]{3,1,2,0:T(8,128)}, u32[]{:S(2)}) copy-start(f32[4,8,6,128]{3,1,2,0:T(8,128)} %param.10) | copy-start | bytes 294916
  16.0 5.4 %copy-start.1 = (f32[3,4096]{1,0:T(4,128)S(1)}, f32[3,4096]{1,0:T(4,128)}, u32[]{:S(2)}) copy-start(f32[3,4096]{1,0:T(4,128)} %place.3) | copy-start | bytes 147460
  16.0 5.4 %copy-start.2 = (s32[4096,1]{0,1:T(1,128)S(1)}, s32[4096,1]{0,1:T(1,128)}, u32[]{:S(2)}) copy-start(s32[4096,1]{0,1:T(1,128)} %param.16) | copy-start | bytes 49156
  16.0 5.4 %copy-start.3 = (s32[4096]{0:T(1024)S(1)}, s32[4096]{0:T(1024)}, u32[]{:S(2)}) copy-start(s32[4096]{0:T(1024)} %param.17) | copy-start | bytes 49156
  16.1 5.4 %copy-start.7 = (f32[3,4096]{1,0:T(4,128)S(1)}, f32[3,4096]{1,0:T(4,128)}, u32[]{:S(2)}) copy-start(f32[3,4096]{1,0:T(4,128)} %speed.1) | copy-start | bytes 147460
  16.1 5.4 %copy-start.8 = (s32[4096]{0:T(1024)S(1)}, s32[4096]{0:T(1024)}, u32[]{:S(2)}) copy-start(s32[4096]{0:T(1024)} %param.15) | copy-start | bytes 49156
  27.9 25.3 %all-to-all-start = ((f32[64,1,768]{2,1,0:T(1,128)}), f32[64,1,768]{2,1,0:T(1,128)S(1)}, u32[]{:S(2)}, u32[]{:S(2)}) async-start(f32[64,1,768]{2,1,0:T(1,128)} %bitcast.5), calls=%async_computation | async-start | bytes 393216 | tf_op jit(solution)/shard_map/all_to_all | solution.py:741
  53.1 6.9 %copy-start.5 = (f32[9,128]{1,0:T(8,128)S(1)}, f32[9,128]{1,0:T(8,128)}, u32[]{:S(2)}) copy-start(f32[9,128]{1,0:T(8,128)} %state.1) | copy-start | bytes 13828
  53.2 6.9 %copy-start.6 = (f32[4,128]{1,0:T(4,128)S(1)}, f32[4,128]{1,0:T(4,128)}, u32[]{:S(2)}) copy-start(f32[4,128]{1,0:T(4,128)} %inertia.1) | copy-start | bytes 6148
  53.2 3.6 %collective-permute-start.6 = (f32[8,128]{1,0:T(8,128)S(1)}, f32[8,128]{1,0:T(8,128)S(1)}, u32[]{:S(2)}, u32[]{:S(2)}) collective-permute-start(f32[8,128]{1,0:T(8,128)S(1)} %share.1.first), channel_id=1, source_target_pairs={{0,3},{1,0},{2,1},{3,2},{4,7},{5,4},{6,5},{7,6},{8,11},{9,8},{10,9... | collective-permute-start | bytes 12296 | tf_op jit(solution)/shard_map/ppermute | solution.py:779
  54.0 4.0 %collective-permute-start.5 = (f32[8,128]{1,0:T(8,128)S(1)}, f32[8,128]{1,0:T(8,128)S(1)}, u32[]{:S(2)}, u32[]{:S(2)}) collective-permute-start(f32[8,128]{1,0:T(8,128)S(1)} %share.1.first), channel_id=1, source_target_pairs={{0,2},{1,3},{2,0},{3,1},{4,6},{5,7},{6,4},{7,5},{8,10},{9,11},{10,... | collective-permute-start | bytes 12296 | tf_op jit(solution)/shard_map/ppermute | solution.py:779
  56.3 3.7 %collective-permute-start.4 = (f32[8,128]{1,0:T(8,128)S(1)}, f32[8,128]{1,0:T(8,128)S(1)}, u32[]{:S(2)}, u32[]{:S(2)}) collective-permute-start(f32[8,128]{1,0:T(8,128)S(1)} %share.1.first), channel_id=1, source_target_pairs={{0,1},{1,2},{2,3},{3,0},{4,5},{5,6},{6,7},{7,4},{8,9},{9,10},{10,1... | collective-permute-start | bytes 12296 | tf_op jit(solution)/shard_map/ppermute | solution.py:779
  60.7 20.0 %all-to-all-start.1 = ((f32[64,1,768]{2,1,0:T(1,128)}), f32[64,1,768]{2,1,0:T(1,128)S(1)}, u32[]{:S(2)}, u32[]{:S(2)}) async-start(f32[64,1,768]{2,1,0:T(1,128)} %bitcast.11), calls=%async_computation.1 | async-start | bytes 393216 | tf_op jit(solution)/shard_map/all_to_all | solution.py:794

commit v8 on v7

--- a/solution.py
+++ b/solution.py
@@ -82,10 +82,10 @@
 
 def assemble(own, west, east, up, down, ext):
     layers, columns = own.shape[0], own.shape[1]
-    ext[0:2] = up[...]
-    ext[layers + 2 : layers + 4] = down[...]
-    ext[2 : layers + 2, 0:2] = west[...]
-    ext[2 : layers + 2, columns + 2 : columns + 4] = east[...]
+    ext[0:2, 2 : columns + 2] = up[...]
+    ext[layers + 2 : layers + 4, 2 : columns + 2] = down[...]
+    ext[:, 0:2] = west[...]
+    ext[:, columns + 2 : columns + 4] = east[...]
     ext[2 : layers + 2, 2 : columns + 2] = own[...]
 
 
@@ -679,7 +679,7 @@
         compiler_params=params(),
         name="prep",
     )(*[pltpu.with_memory_space_constraint(x, pltpu.HBM) for x in (tile_count, codes, soil)])
-    west, east = shifted(own, "tile", 1, 2)
+    up, down = shifted(own, "depth", 0, 2)
     lefts, mine = pl.pallas_call(
         turn_kernel,
         out_shape=(
@@ -692,7 +692,8 @@
         compiler_params=params(),
         name="turn",
     )(own)
-    west, east, mine = lax.optimization_barrier((west, east, mine))
+    up, down, mine = lax.optimization_barrier((up, down, mine))
+    west, east = shifted(jnp.concatenate([up, own, down], axis=0), "tile", 1, 2)
     inner = pl.pallas_call(
         inner_kernel,
         out_shape=jax.ShapeDtypeStruct((layers, columns, TP), F32),
@@ -702,10 +703,6 @@
         compiler_params=params(),
         name="inner",
     )(codes, lefts, mine)
-    top = jnp.concatenate([west[:2], own[:2], east[:2]], axis=1)
-    bottom = jnp.concatenate([west[-2:], own[-2:], east[-2:]], axis=1)
-    rim = jnp.concatenate([top, bottom], axis=0)
-    up, down = shifted(rim, "depth", 0, 2)
     pieces = (own, west, east, up, down)
     span, width = layers + 4, columns + 4
     pairs = layers * columns * 6 * TP * TP
@@ -743,9 +740,9 @@
     ring_codes = jnp.concatenate(
         [
             part[:, :, 7, 0:6]
-            for part in (up, jnp.concatenate([west, own, east], axis=1), down)
+            for part in (west, jnp.concatenate([up, own, down], axis=0), east)
         ],
-        axis=0,
+        axis=1,
     )
     ring_codes = jnp.transpose(ring_codes.astype(jnp.int32), (2, 0, 1))
     shapes = (

time: 83.8 us -> 82.9 us (0.989)
  waiting for transfers between devices: 11.9 us -> 9.08 us
  starting transfers between devices: 38.1 us -> 39.8 us
    ppermute x4, waiting for transfers between devices: 3.09 us -> 0.56 us  [shifted(): return (lax.ppermute(last, axis, up), lax.ppermute(first, axis, down))]
    ppermute x4, starting transfers between devices: 11.2 us -> 13.4 us  [shifted(): return (lax.ppermute(last, axis, up), lax.ppermute(first, axis, down))]
    all_to_all x1, starting transfers between devices: 14.3 us -> 12.7 us  [local(): lax.all_to_all(partial_sums.reshape(flat), 'tile', 0, 0, tiled=True)]
    ppermute x3, starting transfers between devices: 3.56 us -> 4.63 us  [local(): lax.ppermute(share, 'depth', [(i, (i + k) % depth_devs) for i in range(de...]
  transfers between devices with their start and end apart: 9 -> 9, of which waited for: 6 -> 4; matrix products, arithmetic and copies ran while one was open for 0% -> 1% of each run, Pallas kernels for 22% -> 23%
where the time goes in v8:
time: 82.9 us; the launch traced here: 82.5 us
  starting transfers between devices  39.8 us (48%)
  Pallas kernels  32.1 us (39%)
  waiting for transfers between devices  9.08 us (11%)
  between operations  0.88 us (1%)
    ppermute x4, starting transfers between devices, shifted(): return (lax.ppermute(last, axis, up), lax.ppermute(first, axis, down))  13.4 us
    all_to_all x1, starting transfers between devices, local(): lax.all_to_all(partial_sums.reshape(flat), 'tile', 0, 0, tiled=True)  12.7 us
    all_to_all x1, starting transfers between devices, local(): states = lax.all_to_all(sent.reshape(flat), 'tile', 0, 0, tiled=True)  9.02 us
    pallas_call x1, Pallas kernels, local(): pl.pallas_call(accel_kernel, out_shape=jax.ShapeDtypeStruct((layers, 3, c...  8.43 us
    pallas_call x1, Pallas kernels, local(): pl.pallas_call(ring_kernel, out_shape=shapes, in_specs=[sspec()] + [vspec...  7.58 us
    pallas_call x1, Pallas kernels, local(): pl.pallas_call(marker_kernel, out_shape=jax.ShapeDtypeStruct((tile_devs *...  6.44 us
    ppermute x3, starting transfers between devices, local(): lax.ppermute(share, 'depth', [(i, (i + k) % depth_devs) for i in range(de...  4.63 us
    ppermute x3, waiting for transfers between devices, local(): lax.ppermute(share, 'depth', [(i, (i + k) % depth_devs) for i in range(de...  3.21 us
  transfers between devices with their start and end apart: 9, of which 4 were waited for; matrix products, arithmetic and copies ran while one was open for 1% of the time, Pallas kernels for 23%

profile of v8, /device:TPU:1, one launch (start us, length us, event | category | flops | bytes accessed | tf_op | source)
XLA Modules:
  0.0 82.5 jit_solution(1804131720057971063)
XLA Ops:
  0.6 1.0 %prep.1.own = f32[4,8,8,128]{3,2,1,0:T(8,128)S(1)} custom-call(s32[4,8]{1,0:T(4,128)} %counts_in.1, s32[6,4,8]{2,1,0:T(4,128)} %bitcast.23, f32[4,6,8,128]{3,2,1,0:T(8,128)} %bitcast.17), custom_call_target="tpu_custom_call" | custom-call | tf_op jit(solution)/shard_map/prep/pallas_call | solution.py:668
  1.7 1.3 %collective-permute-start.1 = (f32[2,8,8,128]{3,2,1,0:T(8,128)S(1)}, f32[2,8,8,128]{3,2,1,0:T(8,128)S(1)}, u32[]{:S(2)}, u32[]{:S(2)}) collective-permute-start(f32[2,8,8,128]{3,2,1,0:T(8,128)S(1)} %get-tuple-element.45), channel_id=1, source_target_pairs={{1,0},{2,1},{3,2},{5,4},{6,5},{7,6},{9,8},{10,9},{11,10},{13,12},{... | collective-permute-start | bytes 196616 | tf_op jit(solution)/shard_map/ppermute | solution.py:647
  3.0 4.7 %collective-permute-start = (f32[2,8,8,128]{3,2,1,0:T(8,128)S(1)}, f32[2,8,8,128]{3,2,1,0:T(8,128)S(1)}, u32[]{:S(2)}, u32[]{:S(2)}) collective-permute-start(f32[2,8,8,128]{3,2,1,0:T(8,128)S(1)} %get-tuple-element.46), channel_id=1, source_target_pairs={{0,1},{1,2},{2,3},{4,5},{5,6},{6,7},{8,9},{9,10},{10,11},{12,13},{... | collective-permute-start | bytes 196616 | tf_op jit(solution)/shard_map/ppermute | solution.py:647
  7.7 0.7 turn.1
  8.4 0.6 collective-permute-done.up
  9.0 5.6 %collective-permute-start.3 = (f32[8,2,8,128]{3,2,1,0:T(8,128)S(1)}, f32[8,2,8,128]{3,2,1,0:T(8,128)S(1)}, u32[]{:S(2)}, u32[]{:S(2)}) collective-permute-start(f32[8,2,8,128]{3,2,1,0:T(8,128)S(1)} %get-tuple-element.43), channel_id=1, source_target_pairs={{4,0},{8,4},{12,8},{16,12},{20,16},{24,20},{28,24},{32,28},{36,32}... | collective-permute-start | bytes 196616 | tf_op jit(solution)/shard_map/ppermute | solution.py:647
  14.6 1.9 %collective-permute-start.2 = (f32[8,2,8,128]{3,2,1,0:T(8,128)S(1)}, f32[8,2,8,128]{3,2,1,0:T(8,128)S(1)}, u32[]{:S(2)}, u32[]{:S(2)}) collective-permute-start(f32[8,2,8,128]{3,2,1,0:T(8,128)S(1)} %get-tuple-element.44), channel_id=1, source_target_pairs={{0,4},{4,8},{8,12},{12,16},{16,20},{20,24},{24,28},{28,32},{32,36}... | collective-permute-start | bytes 196616 | tf_op jit(solution)/shard_map/ppermute | solution.py:647
  16.5 1.9 %inner.1 = f32[4,8,128]{2,1,0:T(8,128)S(1)} custom-call(s32[6,4,8]{2,1,0:T(4,128)S(1)} %bitcast.24, bf16[4,8,128,48]{3,2,1,0:T(8,128)(2,1)S(1)} %get-tuple-element.26.lefts, bf16[4,8,48,128]{3,2,1,0:T(8,128)(2,1)S(1)} %get-tuple-element.27.btab.mine), custom_call_target="tpu_custom_call" | custom-call | flops 4000000 | bytes 262144 | tf_op jit(solution)/shard_map/inner/pallas_call | solution.py:697
  18.5 2.6 %density.1.extra = f32[4,32,128]{2,1,0:T(8,128)S(1)} custom-call(s32[6,4,8]{2,1,0:T(4,128)S(1)} %bitcast.25, f32[4,8,8,128]{3,2,1,0:T(8,128)S(1)} %prep.1.own, f32[8,2,8,128]{3,2,1,0:T(8,128)S(1)} %collective-permute-done.2.west, f32[8,2,8,128]{3,2,1,0:T(8,128)S(1)} %collective-permute-done.3.east, f32[2,8,8,128]{3,2,1,0:T(8,128)S(1)} %collective-permute-done.up, ...), custom_call_target="tpu_custom_call" | custom-call | flops 37748736 | bytes 262144 | tf_op jit(solution)/shard_map/density/pallas_call | solution.py:709
  21.2 6.4 %markers.1 = f32[384,128]{1,0:T(8,128)} custom-call(f32[4,6,8,128]{3,2,1,0:T(8,128)S(1)} %bitcast.18, f32[4,32,128]{2,1,0:T(8,128)S(1)} %density.1.extra, f32[3,4096]{1,0:T(4,128)S(1)} %copy-done.1, f32[3,4096]{1,0:T(4,128)S(1)} %copy-done.7, s32[32,128]{1,0:T(8,128)S(1)} %bitcast.27, s32[32,128]{1,0:T(8,128)S(1)} %bitcast.19, s32[32,128]{1,0:T(8,128)S(1)} %bitcast.21), custom_call_target="tpu_custom_call" | custom-call | flops 13107200 | bytes 524288 | tf_op jit(solution)/shard_map/markers/pallas_call | solution.py:726
  27.6 12.7 %all-to-all-start = ((f32[64,1,768]{2,1,0:T(1,128)}), f32[64,1,768]{2,1,0:T(1,128)S(1)}, u32[]{:S(2)}, u32[]{:S(2)}) async-start(f32[64,1,768]{2,1,0:T(1,128)} %bitcast.5), calls=%async_computation | async-start | bytes 393216 | tf_op jit(solution)/shard_map/all_to_all | solution.py:738
  40.3 0.1 copy.22
  40.5 0.1 copy.23
  40.6 0.1 copy.21
  40.8 7.6 %ring.1 = (f32[8,12,8,128]{3,2,1,0:T(8,128)S(1)}, bf16[6,10,48,128]{3,2,1,0:T(8,128)(2,1)S(1)}, bf16[6,10,48,128]{3,2,1,0:T(8,128)(2,1)S(1)}, f32[6,16,128]{2,1,0:T(8,128)S(1)}, f32[6,16,128]{2,1,0:T(8,128)S(1)}) custom-call(s32[6,8,12]{2,1,0:T(8,128)S(1)} %fusion.codes, f32[4,8,8,128]{3,2,1,0:T(8,128)S(1)} %prep.1.own, ...), custom_call_target="tpu_custom_call" | custom-call | flops 47185920 | bytes 524288 | tf_op jit(solution)/shard_map/ring/pallas_call | solution.py:755
  48.4 2.8 %all-to-all-done = f32[64,1,768]{2,1,0:T(1,128)S(1)} async-done(((f32[64,1,768]{2,1,0:T(1,128)}), f32[64,1,768]{2,1,0:T(1,128)S(1)}, u32[]{:S(2)}, u32[]{:S(2)}) %all-to-all-start) | async-done | bytes 196640 | tf_op jit(solution)/shard_map/all_to_all | solution.py:738
  51.3 3.9 %collective-permute-start.6 = (f32[8,128]{1,0:T(8,128)S(1)}, f32[8,128]{1,0:T(8,128)S(1)}, u32[]{:S(2)}, u32[]{:S(2)}) collective-permute-start(f32[8,128]{1,0:T(8,128)S(1)} %share.1.first), channel_id=1, source_target_pairs={{0,3},{1,0},{2,1},{3,2},{4,7},{5,4},{6,5},{7,6},{8,11},{9,8},{10,9... | collective-permute-start | bytes 12296 | tf_op jit(solution)/shard_map/ppermute | solution.py:776
  55.2 0.7 collective-permute-start.4
  55.9 3.2 %collective-permute-done.5.third = f32[8,128]{1,0:T(8,128)S(1)} collective-permute-done((f32[8,128]{1,0:T(8,128)S(1)}, f32[8,128]{1,0:T(8,128)S(1)}, u32[]{:S(2)}, u32[]{:S(2)}) %collective-permute-start.5) | collective-permute-done | bytes 4128 | tf_op jit(solution)/shard_map/ppermute | solution.py:776
  59.1 0.7 advance.1
  59.8 9.0 %all-to-all-start.1 = ((f32[64,1,768]{2,1,0:T(1,128)}), f32[64,1,768]{2,1,0:T(1,128)S(1)}, u32[]{:S(2)}, u32[]{:S(2)}) async-start(f32[64,1,768]{2,1,0:T(1,128)} %bitcast.11), calls=%async_computation.1 | async-start | bytes 393216 | tf_op jit(solution)/shard_map/all_to_all | solution.py:791
  68.9 8.4 %accel.1 = f32[4,3,8,128]{3,2,1,0:T(8,128)} custom-call(s32[6,4,8]{2,1,0:T(4,128)S(1)} %bitcast.26, f32[8,12,8,128]{3,2,1,0:T(8,128)S(1)} %get-tuple-element.35.ext, bf16[6,10,48,128]{3,2,1,0:T(8,128)(2,1)S(1)} %get-tuple-element.36.btab, bf16[6,10,48,128]{3,2,1,0:T(8,128)(2,1)S(1)} %get-tuple-element.37.ftab, ...), custom_call_target="tpu_custom_call" | custom-call | flops 47185920 | bytes 524288 | tf_op jit(solution)/shard_map/accel/pallas_call | solution.py:792
  77.3 2.5 %all-to-all-done.1 = f32[64,1,768]{2,1,0:T(1,128)S(1)} async-done(((f32[64,1,768]{2,1,0:T(1,128)}), f32[64,1,768]{2,1,0:T(1,128)S(1)}, u32[]{:S(2)}, u32[]{:S(2)}) %all-to-all-start.1) | async-done | bytes 196640 | tf_op jit(solution)/shard_map/all_to_all | solution.py:791
  79.8 2.7 %pick.1 = f32[3,4096]{1,0:T(4,128)} custom-call(f32[384,128]{1,0:T(8,128)S(1)} %bitcast.16, f32[3,4096]{1,0:T(4,128)S(1)} %copy-done.1, s32[32,128]{1,0:T(8,128)S(1)} %bitcast.20, s32[32,128]{1,0:T(8,128)S(1)} %bitcast.22), custom_call_target="tpu_custom_call" | custom-call | tf_op jit(solution)/shard_map/pick/pallas_call | solution.py:804
  (31 shorter events, 0.3 us)
Async XLA Ops:
  1.7 6.7 %collective-permute-start.1 = (f32[2,8,8,128]{3,2,1,0:T(8,128)S(1)}, f32[2,8,8,128]{3,2,1,0:T(8,128)S(1)}, u32[]{:S(2)}, u32[]{:S(2)}) collective-permute-start(f32[2,8,8,128]{3,2,1,0:T(8,128)S(1)} %get-tuple-element.45), channel_id=1, source_target_pairs={{1,0},{2,1},{3,2},{5,4},{6,5},{7,6},{9,8},{10,9},{11,10},{13,12},{... | collective-permute-start | bytes 196616 | tf_op jit(solution)/shard_map/ppermute | solution.py:647
  3.0 6.0 %collective-permute-start = (f32[2,8,8,128]{3,2,1,0:T(8,128)S(1)}, f32[2,8,8,128]{3,2,1,0:T(8,128)S(1)}, u32[]{:S(2)}, u32[]{:S(2)}) collective-permute-start(f32[2,8,8,128]{3,2,1,0:T(8,128)S(1)} %get-tuple-element.46), channel_id=1, source_target_pairs={{0,1},{1,2},{2,3},{4,5},{5,6},{6,7},{8,9},{9,10},{10,11},{12,13},{... | collective-permute-start | bytes 196616 | tf_op jit(solution)/shard_map/ppermute | solution.py:647
  9.0 7.5 %copy-start.4 = (s32[4,8,6]{1,0,2:T(4,128)S(1)}, s32[4,8,6]{1,0,2:T(4,128)}, u32[]{:S(2)}) copy-start(s32[4,8,6]{1,0,2:T(4,128)} %param.12) | copy-start | bytes 2308
  9.0 9.5 %collective-permute-start.3 = (f32[8,2,8,128]{3,2,1,0:T(8,128)S(1)}, f32[8,2,8,128]{3,2,1,0:T(8,128)S(1)}, u32[]{:S(2)}, u32[]{:S(2)}) collective-permute-start(f32[8,2,8,128]{3,2,1,0:T(8,128)S(1)} %get-tuple-element.43), channel_id=1, source_target_pairs={{4,0},{8,4},{12,8},{16,12},{20,16},{24,20},{28,24},{32,28},{36,32}... | collective-permute-start | bytes 196616 | tf_op jit(solution)/shard_map/ppermute | solution.py:647
  14.6 3.9 %collective-permute-start.2 = (f32[8,2,8,128]{3,2,1,0:T(8,128)S(1)}, f32[8,2,8,128]{3,2,1,0:T(8,128)S(1)}, u32[]{:S(2)}, u32[]{:S(2)}) collective-permute-start(f32[8,2,8,128]{3,2,1,0:T(8,128)S(1)} %get-tuple-element.44), channel_id=1, source_target_pairs={{0,4},{4,8},{8,12},{12,16},{16,20},{20,24},{24,28},{28,32},{32,36}... | collective-permute-start | bytes 196616 | tf_op jit(solution)/shard_map/ppermute | solution.py:647
  18.4 2.7 %copy-start = (f32[4,8,6,128]{3,1,2,0:T(8,128)S(1)}, f32[4,8,6,128]{3,1,2,0:T(8,128)}, u32[]{:S(2)}) copy-start(f32[4,8,6,128]{3,1,2,0:T(8,128)} %param.10) | copy-start | bytes 294916
  18.4 2.7 %copy-start.1 = (f32[3,4096]{1,0:T(4,128)S(1)}, f32[3,4096]{1,0:T(4,128)}, u32[]{:S(2)}) copy-start(f32[3,4096]{1,0:T(4,128)} %place.3) | copy-start | bytes 147460
  18.4 2.7 %copy-start.2 = (s32[4096,1]{0,1:T(1,128)S(1)}, s32[4096,1]{0,1:T(1,128)}, u32[]{:S(2)}) copy-start(s32[4096,1]{0,1:T(1,128)} %param.16) | copy-start | bytes 49156
  18.4 2.7 %copy-start.3 = (s32[4096]{0:T(1024)S(1)}, s32[4096]{0:T(1024)}, u32[]{:S(2)}) copy-start(s32[4096]{0:T(1024)} %param.17) | copy-start | bytes 49156
  18.4 2.7 %copy-start.7 = (f32[3,4096]{1,0:T(4,128)S(1)}, f32[3,4096]{1,0:T(4,128)}, u32[]{:S(2)}) copy-start(f32[3,4096]{1,0:T(4,128)} %speed.1) | copy-start | bytes 147460
  18.5 2.7 %copy-start.8 = (s32[4096]{0:T(1024)S(1)}, s32[4096]{0:T(1024)}, u32[]{:S(2)}) copy-start(s32[4096]{0:T(1024)} %param.15) | copy-start | bytes 49156
  27.6 23.6 %all-to-all-start = ((f32[64,1,768]{2,1,0:T(1,128)}), f32[64,1,768]{2,1,0:T(1,128)S(1)}, u32[]{:S(2)}, u32[]{:S(2)}) async-start(f32[64,1,768]{2,1,0:T(1,128)} %bitcast.5), calls=%async_computation | async-start | bytes 393216 | tf_op jit(solution)/shard_map/all_to_all | solution.py:738
  51.2 7.9 %copy-start.5 = (f32[9,128]{1,0:T(8,128)S(1)}, f32[9,128]{1,0:T(8,128)}, u32[]{:S(2)}) copy-start(f32[9,128]{1,0:T(8,128)} %state.1) | copy-start | bytes 13828
  51.2 7.9 %copy-start.6 = (f32[4,128]{1,0:T(4,128)S(1)}, f32[4,128]{1,0:T(4,128)}, u32[]{:S(2)}) copy-start(f32[4,128]{1,0:T(4,128)} %inertia.1) | copy-start | bytes 6148
  51.3 4.6 %collective-permute-start.6 = (f32[8,128]{1,0:T(8,128)S(1)}, f32[8,128]{1,0:T(8,128)S(1)}, u32[]{:S(2)}, u32[]{:S(2)}) collective-permute-start(f32[8,128]{1,0:T(8,128)S(1)} %share.1.first), channel_id=1, source_target_pairs={{0,3},{1,0},{2,1},{3,2},{4,7},{5,4},{6,5},{7,6},{8,11},{9,8},{10,9... | collective-permute-start | bytes 12296 | tf_op jit(solution)/shard_map/ppermute | solution.py:776
  55.1 4.0 %collective-permute-start.5 = (f32[8,128]{1,0:T(8,128)S(1)}, f32[8,128]{1,0:T(8,128)S(1)}, u32[]{:S(2)}, u32[]{:S(2)}) collective-permute-start(f32[8,128]{1,0:T(8,128)S(1)} %share.1.first), channel_id=1, source_target_pairs={{0,2},{1,3},{2,0},{3,1},{4,6},{5,7},{6,4},{7,5},{8,10},{9,11},{10,... | collective-permute-start | bytes 12296 | tf_op jit(solution)/shard_map/ppermute | solution.py:776
  55.2 3.9 %collective-permute-start.4 = (f32[8,128]{1,0:T(8,128)S(1)}, f32[8,128]{1,0:T(8,128)S(1)}, u32[]{:S(2)}, u32[]{:S(2)}) collective-permute-start(f32[8,128]{1,0:T(8,128)S(1)} %share.1.first), channel_id=1, source_target_pairs={{0,1},{1,2},{2,3},{3,0},{4,5},{5,6},{6,7},{7,4},{8,9},{9,10},{10,1... | collective-permute-start | bytes 12296 | tf_op jit(solution)/shard_map/ppermute | solution.py:776
  59.8 20.0 %all-to-all-start.1 = ((f32[64,1,768]{2,1,0:T(1,128)}), f32[64,1,768]{2,1,0:T(1,128)S(1)}, u32[]{:S(2)}, u32[]{:S(2)}) async-start(f32[64,1,768]{2,1,0:T(1,128)} %bitcast.11), calls=%async_computation.1 | async-start | bytes 393216 | tf_op jit(solution)/shard_map/all_to_all | solution.py:791
